TPU v7x, 256 devices: a whole 4x4x8 slice. The times are simulated.
256 devices in a mesh: ctx: 32 (over z, x), head: 8 (over y, core).
Axes of the slice: x: 4, y: 4, z: 8, core: 2. Of those that a mesh axis runs over, the one named last changes fastest.
Arguments:
- queries: bfloat16 [65536, 2048], P('ctx', 'head'), may hold values from -6 to 6
- keys: bfloat16 [65536, 2048], P('ctx', 'head'), may hold values from -6 to 6
- values: bfloat16 [65536, 4096], P('ctx', 'head'), may hold values from -6 to 6
- gate_pre: float32 [2, 8, 65536], P(None, None, ('ctx', 'head')), may hold values from -8 to 320
Outputs:
- hidden: bfloat16 [65536, 4096], P('ctx', 'head')
- closing_memory: float32 [8, 256, 512], P('head', 'ctx')
- final_norm: float32 [8, 256], P('head')
- final_max: float32 [8], P('head')
All inputs are finite; a program needn't handle non-finite values.
Results may differ from a plain program's by a relative error of at most 0.004.
Values sent between devices are 32-bit elements; how exact they have to be, the bound alone decides.
No kernel may reach another device: no remote copies, remote signals or barrier semaphores. Data moves between devices by JAX's collectives and lax.ppermute only.
A program may use at most 64 MiB of HBM per device.

v0:
```python
import jax
import jax.numpy as jnp
from jax import lax
from jax.sharding import Mesh
from jax.sharding import PartitionSpec as P

DQK = 256
BLK = 512
CTX = ("ctx_0", "ctx_1")
CTX_HEAD = ("ctx_0", "ctx_1", "head")


NEG = -1e30


def neutral_like(x, identity):
    return jax.tree.map(
        lambda a, e: jnp.broadcast_to(jnp.asarray(e, a.dtype), a.shape), x, identity
    )


def all_in_one(x, axis):
    leaves = jax.tree.leaves(x)
    turns = sorted(range(len(leaves)), key=lambda k: -leaves[k].size)
    width = (1, *leaves[turns[0]].shape)[-1]
    lines = [
        jnp.pad(leaves[k].reshape(-1), (0, -leaves[k].size % width)).reshape(-1, width)
        for k in turns
    ]
    both, at, found = (lax.all_gather(jnp.concatenate(lines), axis), 0, {})
    for k, line in zip(turns, lines):
        section = both[:, at : at + len(line)].reshape(len(both), -1)
        found[k] = section[:, : leaves[k].size].reshape(-1, *leaves[k].shape)
        at += len(line)
    numbers = iter(range(len(leaves)))
    return jax.tree.map(lambda _: found[next(numbers)], x)


def prefix_by_axis(x, axes, combine, identity):
    before = start = neutral_like(x, identity)
    so_far = x
    for axis in reversed(axes):
        devices, index = (lax.axis_size(axis), lax.axis_index(axis))
        pieces = all_in_one(so_far, axis)
        inside, so_far = (start, start)
        for k in range(devices):
            passed = k < index
            so_far = combine(so_far, jax.tree.map(lambda part: part[k], pieces))
            inside = jax.tree.map(lambda new, old: jnp.where(passed, new, old), so_far, inside)
        before = combine(inside, before)
    return before


def sent_to_all(x, axis):
    copies = jnp.broadcast_to(x, (lax.axis_size(axis), *x.shape))
    return lax.all_to_all(copies, axis, split_axis=0, concat_axis=0, tiled=True)


def joined_by_halves(pieces, combine):
    while len(jax.tree.leaves(pieces)[0]) > 1:
        pieces = jax.vmap(combine)(*(pieces[side::2] for side in (0, 1)))
    return pieces[0]


def prefix(x, axis, combine, identity):
    devices, index = (lax.axis_size(axis), lax.axis_index(axis))
    passed = jnp.arange(devices) > index

    def kept(part, zero, own):
        part = jnp.where(
            passed.reshape(-1, *(1 for _ in own.shape)), part, jnp.asarray(zero, own.dtype)
        )
        return part[::-1]

    pieces = sent_to_all(x, axis)
    return joined_by_halves(kept(pieces, identity, x), combine)


def over_copies(x, axis):
    everything = sent_to_all(x, axis)
    return jnp.max(everything, axis=0)


def cut_along(x, dim, devices):
    before, after = (x.shape[:dim], x.shape[dim + 1 :])
    return jnp.moveaxis(x.reshape(*before, devices, -1, *after), dim, 0)


def sent_and_summed(x, axis, dim):
    pieces = cut_along(x, dim, lax.axis_size(axis))
    arrived = lax.all_to_all(pieces, axis, split_axis=0, concat_axis=0, tiled=True)
    return arrived.sum(axis=0)


def over_copies_2(x, axis):
    everything = sent_to_all(x, axis)
    return jnp.sum(everything, axis=0)


def block_step(carry, inputs):
    memory, normal, stab, offset = carry
    q_block, key_block, v_block, in_gate, forget = inputs
    length = q_block.shape[0]
    scale = q_block.shape[1] ** (-0.5)
    log_forget = jax.nn.log_sigmoid(forget)
    cum = jnp.cumsum(log_forget)
    whole = cum[-1]
    places = jnp.arange(length, dtype=jnp.int32)
    causal = places[:, None] >= places[None, :]
    log_weight = jnp.where(causal, cum[:, None] - cum[None, :] + in_gate[None, :], NEG)
    top = jnp.maximum(cum + stab, jnp.max(log_weight, axis=1))
    weights = jnp.where(causal, jnp.exp(log_weight - top[:, None]), 0.0)
    scores = jnp.dot(q_block, key_block.T, preferred_element_type=jnp.float32) * scale
    mixed = weights * scores
    denom = jnp.sum(mixed, axis=1)
    numer = jnp.dot(mixed.astype(jnp.bfloat16), v_block, preferred_element_type=jnp.float32)
    carried = jnp.exp(cum + stab - top)
    q_float = q_block.astype(jnp.float32)
    numer = numer + carried[:, None] * jnp.dot(q_float, memory, precision=lax.Precision.HIGHEST)
    denom = denom + carried * jnp.dot(q_float, normal, precision=lax.Precision.HIGHEST)
    new_stab = jnp.maximum(whole + stab, jnp.max(whole - cum + in_gate))
    keep = jnp.exp(whole + stab - new_stab)
    taken = jnp.exp(whole - cum + in_gate - new_stab)
    k_float = key_block.astype(jnp.float32) * scale * taken[:, None]
    memory = keep * memory + jnp.dot(
        k_float.T, v_block.astype(jnp.float32), precision=lax.Precision.HIGHEST
    )
    normal = keep * normal + jnp.sum(k_float, axis=0)
    return ((memory, normal, new_stab, offset + whole), (numer, denom, top, cum + offset))


def local_chain(q_head, k_head, v_head, in_gate, forget):
    count = q_head.shape[0] // BLK
    width = v_head.shape[1]
    blocks = (
        q_head.reshape(count, BLK, DQK),
        k_head.reshape(count, BLK, DQK),
        v_head.reshape(count, BLK, width),
        in_gate.reshape(count, BLK),
        forget.reshape(count, BLK),
    )
    start = (
        jnp.zeros((DQK, width), jnp.float32),
        jnp.zeros((DQK,), jnp.float32),
        jnp.full((), NEG, jnp.float32),
        jnp.zeros((), jnp.float32),
    )
    final, outs = lax.scan(block_step, start, blocks)
    numer, denom, top, cum = outs
    row_entries = q_head.shape[0]
    return (
        numer.reshape(row_entries, width),
        denom.reshape(row_entries),
        top.reshape(row_entries),
        cum.reshape(row_entries),
        final[0],
        final[1],
        final[2],
        final[3],
    )


def chain(early, late):
    early_mem, early_norm, early_stab, early_log = early
    late_mem, late_norm, late_stab, late_log = late
    shifted = early_stab + late_log
    peak = jnp.maximum(shifted, late_stab)
    early_factor = jnp.exp(shifted - peak)
    late_factor = jnp.exp(late_stab - peak)
    merged_mem = early_factor[:, None, None] * early_mem + late_factor[:, None, None] * late_mem
    merged_norm = early_factor[:, None] * early_norm + late_factor[:, None] * late_norm
    return (merged_mem, merged_norm, peak, early_log + late_log)


def plus(early, late):
    return early + late


def on_device(queries, keys, values, gate_pre):
    toks = queries.shape[0]
    heads_here = queries.shape[1] // DQK
    width = values.shape[1] // heads_here
    gates = lax.all_to_all(gate_pre, "head", split_axis=1, concat_axis=2, tiled=True)
    q_three = queries.reshape(toks, heads_here, DQK)
    k_three = keys.reshape(toks, heads_here, DQK)
    v_three = values.reshape(toks, heads_here, width)
    numer, denom, top, cum, memory, normal, stab, total = jax.vmap(
        local_chain, in_axes=(1, 1, 1, 0, 0)
    )(q_three, k_three, v_three, gates[0], gates[1])
    zero_heads = jnp.zeros((heads_here,), jnp.float32)
    identity = (
        jnp.zeros_like(memory),
        jnp.zeros_like(normal),
        jnp.full((heads_here,), NEG, jnp.float32),
        zero_heads,
    )
    in_mem, in_norm, in_stab, in_log = prefix_by_axis(
        (memory, normal, stab, total), CTX, chain, identity
    )
    reach = cum + in_stab[:, None]
    peak_all = jnp.maximum(reach, top)
    local_factor = jnp.exp(top - peak_all)
    carried = jnp.exp(reach - peak_all)
    q_float = q_three.astype(jnp.float32)
    from_memory = jnp.einsum("thd,hde->hte", q_float, in_mem, precision=lax.Precision.HIGHEST)
    from_norm = jnp.einsum("thd,hd->ht", q_float, in_norm, precision=lax.Precision.HIGHEST)
    numer = numer * local_factor[..., None] + carried[..., None] * from_memory
    denom = denom * local_factor + carried * from_norm
    result = (numer / jnp.maximum(jnp.abs(denom), 1.0)[..., None]).astype(jnp.bfloat16)
    hidden = result.transpose(1, 0, 2).reshape(toks, heads_here * width)
    after = prefix(total, CTX, plus, zero_heads)
    at_end = stab + after
    final_max = over_copies(at_end, CTX)
    factor = jnp.exp(at_end - final_max)
    closing_memory = sent_and_summed(memory * factor[:, None, None], CTX, 1)
    final_norm = over_copies_2(normal * factor[:, None], CTX)
    return (hidden, closing_memory, final_norm, final_max)


def solution(mesh):
    split = Mesh(mesh.devices.reshape(8, 4, mesh.shape["head"]), ("ctx_0", "ctx_1", "head"))
    in_specs = (P(CTX, "head"), P(CTX, "head"), P(CTX, "head"), P(None, None, CTX_HEAD))
    out_specs = (P(CTX, "head"), P("head", CTX, None), P("head", None), P("head"))
    return jax.shard_map(
        on_device, mesh=split, in_specs=in_specs, out_specs=out_specs, check_vma=False
    )
```

profile of v0, /device:TPU:32, one launch (start us, length us, event | category | flops | bytes accessed | tf_op | source)
XLA Modules:
  0.0 240.0 jit_solution(6378185667972037786)
XLA Ops:
  8.5 4.5 %all-to-all-start = ((f32[2,8,256]{2,0,1:T(2,128)}), f32[2,8,256]{2,0,1:T(2,128)S(1)}, u32[]{:S(2)}, u32[]{:S(2)}) async-start(f32[2,8,256]{2,0,1:T(2,128)} %copy.32), calls=%async_computation | async-start | bytes 32768 | tf_op jit(solution)/shard_map/all_to_all | solution.py:183
  13.1 5.3 %all-to-all-done = f32[2,8,256]{2,0,1:T(2,128)S(1)} async-done(((f32[2,8,256]{2,0,1:T(2,128)}), f32[2,8,256]{2,0,1:T(2,128)S(1)}, u32[]{:S(2)}, u32[]{:S(2)}) %all-to-all-start) | async-done | bytes 16416 | tf_op jit(solution)/shard_map/all_to_all | solution.py:183
  18.3 57.5 %while.28 = (s32[]{:T(128)}, f32[1,256,512]{2,1,0:T(8,128)S(1)}, f32[1,256]{1,0:T(1,128)S(1)}, f32[1]{0:T(128)}, f32[1]{0:T(128)}, /*index=5*/f32[4,1,512,512]{3...) while((s32[]{:T(128)}, f32[1,256,512]{2,1,0:T(8,128)S(1)}, ...), condition=%wide.region_7.8_spmd.clone, body=%wide.region_0.7_spmd.clone.sunk | while | flops 2020553984 | bytes 16879588 | solution.py:148
  28.4 2.7 %fusion.240 = f32[4,1,512,512]{3,2,1,0:T(8,128)} fusion(f32[4,1,512,512]{3,2,1,0:T(8,128)} %get-tuple-element.427, s32[]{:T(128)S(6)} %copy.72, f32[512,512]{1,0:T(8,128)S(1)} %fusion.238, f32[512]{0:T(512)S(1)} %get-tuple-element.400, f32[1,256,512]{2,1,0:T(8,128)S(1)} %get-tuple-element.423, pred[]{:T(512)S(6)} %compare.9, ...), kind=kOutput, calls=%fused_computation.3.clone.1 | convolution fusion | flops 805961728 | bytes 2887168 | tf_op jit(solution)/shard_map/vmap()/while/body/eval_jaxpr/dot_general | solution.py:119
  31.1 1.7 fusion.235
  40.8 1.5 fusion.237
  42.8 2.6 %fusion.240 = f32[4,1,512,512]{3,2,1,0:T(8,128)} fusion(f32[4,1,512,512]{3,2,1,0:T(8,128)} %get-tuple-element.427, s32[]{:T(128)S(6)} %copy.72, f32[512,512]{1,0:T(8,128)S(1)} %fusion.238, f32[512]{0:T(512)S(1)} %get-tuple-element.400, f32[1,256,512]{2,1,0:T(8,128)S(1)} %get-tuple-element.423, pred[]{:T(512)S(6)} %compare.9, ...), kind=kOutput, calls=%fused_computation.3.clone.1 | convolution fusion | flops 805961728 | bytes 2887168 | tf_op jit(solution)/shard_map/vmap()/while/body/eval_jaxpr/dot_general | solution.py:119
  45.4 1.7 fusion.235
  57.1 2.6 %fusion.240 = f32[4,1,512,512]{3,2,1,0:T(8,128)} fusion(f32[4,1,512,512]{3,2,1,0:T(8,128)} %get-tuple-element.427, s32[]{:T(128)S(6)} %copy.72, f32[512,512]{1,0:T(8,128)S(1)} %fusion.238, f32[512]{0:T(512)S(1)} %get-tuple-element.400, f32[1,256,512]{2,1,0:T(8,128)S(1)} %get-tuple-element.423, pred[]{:T(512)S(6)} %compare.9, ...), kind=kOutput, calls=%fused_computation.3.clone.1 | convolution fusion | flops 805961728 | bytes 2887168 | tf_op jit(solution)/shard_map/vmap()/while/body/eval_jaxpr/dot_general | solution.py:119
  59.8 1.7 fusion.235
  71.5 2.6 %fusion.240 = f32[4,1,512,512]{3,2,1,0:T(8,128)} fusion(f32[4,1,512,512]{3,2,1,0:T(8,128)} %get-tuple-element.427, s32[]{:T(128)S(6)} %copy.72, f32[512,512]{1,0:T(8,128)S(1)} %fusion.238, f32[512]{0:T(512)S(1)} %get-tuple-element.400, f32[1,256,512]{2,1,0:T(8,128)S(1)} %get-tuple-element.423, pred[]{:T(512)S(6)} %compare.9, ...), kind=kOutput, calls=%fused_computation.3.clone.1 | convolution fusion | flops 805961728 | bytes 2887168 | tf_op jit(solution)/shard_map/vmap()/while/body/eval_jaxpr/dot_general | solution.py:119
  74.1 1.7 fusion.235
  76.8 34.5 %all-gather.7.cloned.1.call-done = f32[4,259,512]{2,1,0:T(8,128)} async-done(((f32[1,259,512]{2,1,0:T(8,128)}), f32[4,259,512]{2,1,0:T(8,128)}) %all-gather.7.cloned.1.call-update) | async-done | bytes 2121744 | tf_op jit(solution)/shard_map/all_gather | solution.py:30
  124.5 1.8 fusion.205
  127.8 8.8 %all-to-all-start.1 = ((f32[32,1,1]{2,1,0:T(1,128)}), f32[32,1,1]{2,1,0:T(1,128)S(1)}, u32[]{:S(2)}, u32[]{:S(2)}) async-start(f32[32,1,1]{2,1,0:T(1,128)} %broadcast_in_dim.48), calls=%async_computation.1 | async-start | bytes 32768 | tf_op jit(solution)/shard_map/all_to_all | solution.py:56
  136.6 8.7 %all-to-all-done.1 = f32[32,1,1]{2,1,0:T(1,128)S(1)} async-done(((f32[32,1,1]{2,1,0:T(1,128)}), f32[32,1,1]{2,1,0:T(1,128)S(1)}, u32[]{:S(2)}, u32[]{:S(2)}) %all-to-all-start.1) | async-done | bytes 160 | tf_op jit(solution)/shard_map/all_to_all | solution.py:56
  148.6 12.8 %all_to_all.34 = f32[32,1,1]{2,1,0:T(1,128)S(1)} all-to-all(f32[32,1,1]{2,1,0:T(1,128)S(1)} %broadcast_in_dim.50), channel_id=1, replica_groups=mesh['ctx_0'=8,'ctx_1'=4,'head'=8] {'ctx_0','ctx_1'}, dimensions={0} | all-to-all | bytes 256 | tf_op jit(solution)/shard_map/all_to_all | solution.py:56
  163.3 4.9 %all-to-all-start.4 = ((f32[32,1,256]{2,1,0:T(1,128)}), f32[32,1,256]{2,1,0:T(1,128)S(1)}, u32[]{:S(2)}, u32[]{:S(2)}) async-start(f32[32,1,256]{2,1,0:T(1,128)} %broadcast_in_dim.51), calls=%async_computation.4 | async-start | bytes 65536 | tf_op jit(solution)/shard_map/all_to_all | solution.py:56
  169.1 8.4 %all-to-all-done.4 = f32[32,1,256]{2,1,0:T(1,128)S(1)} async-done(((f32[32,1,256]{2,1,0:T(1,128)}), f32[32,1,256]{2,1,0:T(1,128)S(1)}, u32[]{:S(2)}, u32[]{:S(2)}) %all-to-all-start.4) | async-done | bytes 32800 | tf_op jit(solution)/shard_map/all_to_all | solution.py:56
  177.5 4.7 %all-to-all-start.3 = ((f32[32,1,8,512]{3,2,1,0:T(8,128)}), f32[32,1,8,512]{3,2,1,0:T(8,128)S(1)}, u32[]{:S(2)}, u32[]{:S(2)}) async-start(f32[32,1,8,512]{3,2,1,0:T(8,128)} %multiply_bitcast_fusion), calls=%async_computation.3 | async-start | bytes 1048576 | tf_op jit(solution)/shard_map/all_to_all | solution.py:91
  182.2 5.6 %copy.40 = f32[2048,512]{0,1:T(8,128)} copy(f32[2048,512]{1,0:T(8,128)} %bitcast.288) | data formatting | bytes 8388608 | tf_op jit(solution)/shard_map/vmap()/reshape;vmap()/transpose | solution.py:152
  188.4 9.4 %all-to-all-done.3 = f32[32,1,8,512]{3,2,1,0:T(8,128)S(1)} async-done(((f32[32,1,8,512]{3,2,1,0:T(8,128)}), f32[32,1,8,512]{3,2,1,0:T(8,128)S(1)}, u32[]{:S(2)}, u32[]{:S(2)}) %all-to-all-start.3) | async-done | bytes 524320 | tf_op jit(solution)/shard_map/all_to_all | solution.py:91
  218.8 10.5 %fusion.43 = bf16[2048,512]{0,1:T(8,128)(2,1)} fusion(f32[2048,512]{0,1:T(8,128)} %copy.40, bf16[2048,256]{1,0:T(8,128)(2,1)S(1)} %bitcast.286, f32[2048]{0:T(1024)S(1)} %get-tuple-element.250, f32[2048]{0:T(1024)S(1)} %get-tuple-element.252, f32[2048]{0:T(1024)S(1)} %get-tuple-element.251, f32[8,259,512]{2,1,0:T(8,128)} %all-gather.9.cloned.1.call-done, ...), kind=kOutput, calls=%fused_computation.67 | convolution fusion | flops 3234201600 | bytes 15252480 | tf_op jit(solution)/shard_map/thd,hde->hte/dot_general | solution.py:205
  229.2 3.9 %copy.39 = bf16[2048,512]{1,0:T(8,128)(2,1)} copy(bf16[2048,512]{0,1:T(8,128)(2,1)} %fusion.43) | data formatting | bytes 4194304
  (150 shorter events, 45.0 us)
Async XLA Ops:
  8.5 9.8 %all-to-all-start = ((f32[2,8,256]{2,0,1:T(2,128)}), f32[2,8,256]{2,0,1:T(2,128)S(1)}, u32[]{:S(2)}, u32[]{:S(2)}) async-start(f32[2,8,256]{2,0,1:T(2,128)} %copy.32), calls=%async_computation | async-start | bytes 32768 | tf_op jit(solution)/shard_map/all_to_all | solution.py:183
  13.0 98.4 %all-gather.7.cloned.1.call-start = ((), (), s32[]{:S(2)}) async-start(), calls=%async_computation.5 | async-start | bytes 2703360 | tf_op jit(solution)/shard_map/all_gather | solution.py:30
  18.4 9.5 %copy-start = (bf16[4,1,512,512]{3,2,1,0:T(8,128)(2,1)S(1)}, bf16[4,1,512,512]{3,2,1,0:T(8,128)(2,1)}, u32[]{:S(2)}) copy-start(bf16[4,1,512,512]{3,2,1,0:T(8,128)(2,1)} %get-tuple-element.451) | copy-start | bytes 6291460 | tf_op jit(solution)/shard_map/vmap()/while
  32.8 9.5 %copy-start = (bf16[4,1,512,512]{3,2,1,0:T(8,128)(2,1)S(1)}, bf16[4,1,512,512]{3,2,1,0:T(8,128)(2,1)}, u32[]{:S(2)}) copy-start(bf16[4,1,512,512]{3,2,1,0:T(8,128)(2,1)} %get-tuple-element.451) | copy-start | bytes 6291460 | tf_op jit(solution)/shard_map/vmap()/while
  47.1 9.5 %copy-start = (bf16[4,1,512,512]{3,2,1,0:T(8,128)(2,1)S(1)}, bf16[4,1,512,512]{3,2,1,0:T(8,128)(2,1)}, u32[]{:S(2)}) copy-start(bf16[4,1,512,512]{3,2,1,0:T(8,128)(2,1)} %get-tuple-element.451) | copy-start | bytes 6291460 | tf_op jit(solution)/shard_map/vmap()/while
  61.5 9.5 %copy-start = (bf16[4,1,512,512]{3,2,1,0:T(8,128)(2,1)S(1)}, bf16[4,1,512,512]{3,2,1,0:T(8,128)(2,1)}, u32[]{:S(2)}) copy-start(bf16[4,1,512,512]{3,2,1,0:T(8,128)(2,1)} %get-tuple-element.451) | copy-start | bytes 6291460 | tf_op jit(solution)/shard_map/vmap()/while
  76.8 122.5 %all-gather.9.cloned.1.call-start = ((), (), s32[]{:S(2)}) async-start(), calls=%async_computation.6 | async-start | bytes 4866048 | tf_op jit(solution)/shard_map/all_gather | solution.py:30
  127.8 17.5 %all-to-all-start.1 = ((f32[32,1,1]{2,1,0:T(1,128)}), f32[32,1,1]{2,1,0:T(1,128)S(1)}, u32[]{:S(2)}, u32[]{:S(2)}) async-start(f32[32,1,1]{2,1,0:T(1,128)} %broadcast_in_dim.48), calls=%async_computation.1 | async-start | bytes 32768 | tf_op jit(solution)/shard_map/all_to_all | solution.py:56
  163.3 14.2 %all-to-all-start.4 = ((f32[32,1,256]{2,1,0:T(1,128)}), f32[32,1,256]{2,1,0:T(1,128)S(1)}, u32[]{:S(2)}, u32[]{:S(2)}) async-start(f32[32,1,256]{2,1,0:T(1,128)} %broadcast_in_dim.51), calls=%async_computation.4 | async-start | bytes 65536 | tf_op jit(solution)/shard_map/all_to_all | solution.py:56
  177.5 20.3 %all-to-all-start.3 = ((f32[32,1,8,512]{3,2,1,0:T(8,128)}), f32[32,1,8,512]{3,2,1,0:T(8,128)S(1)}, u32[]{:S(2)}, u32[]{:S(2)}) async-start(f32[32,1,8,512]{3,2,1,0:T(8,128)} %multiply_bitcast_fusion), calls=%async_computation.3 | async-start | bytes 1048576 | tf_op jit(solution)/shard_map/all_to_all | solution.py:91
  182.2 35.6 %copy-start.1 = (bf16[4,1,512,256]{3,2,1,0:T(8,128)(2,1)S(1)}, bf16[4,1,512,256]{3,2,1,0:T(8,128)(2,1)}, u32[]{:S(2)}) copy-start(bf16[4,1,512,256]{3,2,1,0:T(8,128)(2,1)} %get-tuple-element.458) | copy-start | bytes 3145732
Sparse Core Ops, SparseCore 0:
  76.9 34.4 all-gather.6
  127.3 57.3 all-gather.8
where the time goes:
time: 243 us; the launch traced here: 240 us
  waiting for transfers between devices  66.4 us (27%)
  between operations  44.1 us (18%)
  matrix products  41.5 us (17%)
  starting transfers between devices  23 us (9%)
  other arithmetic  22.3 us (9%)
  local copies, waits for them, and re-layouts  21.7 us (9%)
  blocking collectives  12.8 us (5%)
  loops' own time  8.29 us (3%)
    all_gather x2, waiting for transfers between devices, all_in_one(): both, at, found = (lax.all_gather(jnp.concatenate(lines), axis), 0, {})  34.6 us
    all_to_all x2, waiting for transfers between devices, sent_to_all(): return lax.all_to_all(copies, axis, split_axis=0, concat_axis=0, tiled=True)  17.1 us
    all_to_all x2, starting transfers between devices, sent_to_all(): return lax.all_to_all(copies, axis, split_axis=0, concat_axis=0, tiled=True)  13.7 us
    all_to_all x1, blocking collectives, sent_to_all(): return lax.all_to_all(copies, axis, split_axis=0, concat_axis=0, tiled=True)  12.8 us
    dot_general x4, matrix products, block_step(): jnp.dot(q_float, memory, precision=lax.Precision.HIGHEST)  10.5 us
    dot_general x1, matrix products, on_device(): jnp.einsum('thd,hde->hte', q_float, in_mem, precision=lax.Precision.HIGHEST)  10.5 us
    all_to_all x1, waiting for transfers between devices, sent_and_summed(): lax.all_to_all(pieces, axis, split_axis=0, concat_axis=0, tiled=True)  9.43 us
    another operation x1, loops' own time, local_chain(): final, outs = lax.scan(block_step, start, blocks)  8.29 us
  transfers between devices with their start and end apart: 6, of which 5 were waited for; matrix products, arithmetic and copies ran while one was open for 5% of the time, Pallas kernels for 0%

commit v1 on v0

v1 whole, which is shorter than its diff:
```python
import functools

import jax
import jax.numpy as jnp
from jax import lax
from jax.experimental import pallas as pl
from jax.experimental.pallas import tpu as pltpu
from jax.sharding import Mesh
from jax.sharding import PartitionSpec as P

DQK = 256
DV = 512
XS = 4
ZS = 8
ROWS = DQK // (XS * ZS)
SLICE = ZS * ROWS
SENT = SLICE + 8
PIECES = 8
PIECE = 256
LANES = 128
WIDE = DV + LANES
TOKS = PIECES * PIECE
QB = 512
BLOCKS = TOKS // QB
PARTS = ((3,), (2,), (0, 1))
CTX = ("ctx_0", "ctx_1")
CTX_HEAD = ("ctx_0", "ctx_1", "head")
NEG = -1e30
F32 = jnp.float32
BF16 = jnp.bfloat16
VMEM = pl.BlockSpec(memory_space=pltpu.VMEM)
SMEM = pl.BlockSpec(memory_space=pltpu.SMEM)
HBM = pl.BlockSpec(memory_space=pltpu.HBM)
ANY = pl.BlockSpec(memory_space=pl.ANY)
MIB = 1 << 20


def in_hbm(x):
    return pltpu.with_memory_space_constraint(x, pltpu.HBM)


def log_sigmoid(x):
    z = jnp.exp(-jnp.abs(x))
    s = z / (2.0 + z)
    s2 = s * s
    tail = jnp.full_like(s, 1.0 / 17.0)
    for n in (15, 13, 11, 9, 7, 5, 3, 1):
        tail = tail * s2 + 1.0 / n
    return jnp.minimum(x, 0.0) - 2.0 * s * tail


def three_parts(x):
    high = x.astype(BF16)
    rest = x - high.astype(F32)
    mid = rest.astype(BF16)
    low = (rest - mid.astype(F32)).astype(BF16)
    return high, mid, low


def piece_sums(forget):
    n = forget.shape[1]
    upto = lax.broadcasted_iota(jnp.int32, (n, n), 0) <= lax.broadcasted_iota(jnp.int32, (n, n), 1)
    ones = jnp.where(upto, 1.0, 0.0).astype(BF16)
    parts = jnp.concatenate([p.astype(F32) for p in three_parts(log_sigmoid(forget))], axis=0)
    sums = jnp.dot(parts.astype(BF16), ones, preferred_element_type=F32)
    k = forget.shape[0]
    return sums[:k] + sums[k : 2 * k] + sums[2 * k :]


def gate_kernel(g_ref, out_ref):
    cum = piece_sums(g_ref[1])
    own = g_ref[0] - cum
    for h in range(own.shape[0]):
        out_ref[h, 0:1, :] = own[h : h + 1]
        out_ref[h, 1:2, :] = cum[h : h + 1]


def gate_sums(gate_pre):
    kinds, heads, n = gate_pre.shape
    return pl.pallas_call(
        gate_kernel,
        in_specs=[VMEM],
        out_specs=VMEM,
        out_shape=pltpu.VMEM((heads, kinds, n), F32),
        compiler_params=pltpu.CompilerParams(vmem_limit_bytes=8 * MIB),
        name="gate_sums",
    )(gate_pre)


def turned_kernel(k_ref, kt_ref):
    kt_ref[...] = k_ref[...].T


def turned(keys):
    return pl.pallas_call(
        turned_kernel,
        grid=(4,),
        in_specs=[pl.BlockSpec((TOKS // 4, DQK), lambda i: (i, 0))],
        out_specs=pl.BlockSpec((DQK, TOKS // 4), lambda i: (0, i)),
        out_shape=jax.ShapeDtypeStruct((DQK, TOKS), BF16),
        compiler_params=pltpu.CompilerParams(vmem_limit_bytes=8 * MIB),
        cost_estimate=pl.CostEstimate(flops=0, bytes_accessed=4 * MIB, transcendentals=0),
        name="turn_keys",
    )(keys)


def state_kernel(x_ref, g_ref, kt_ref, v_hbm, own_ref, one_ref, two_ref, three_ref, tick_ref, v_ref, w_ref, acc_ref, sem):
    copies = []
    for j in range(BLOCKS):
        span = pl.ds(j * QB, QB)
        copies.append(pltpu.make_async_copy(v_hbm.at[span], v_ref.at[span], sem.at[j]))
        copies[-1].start()
    own = g_ref[:, 0, :]
    cum = g_ref[:, 1, :]
    later = jnp.broadcast_to(cum[:, PIECE - 1 :], cum.shape)
    row = lax.broadcasted_iota(jnp.int32, cum.shape, 0)
    for shift in (1, 2, 4):
        moved = pltpu.roll(later, PIECES - shift, 0)
        later = later + jnp.where(row + shift < PIECES, moved, 0.0)
    reach = own + later
    stab = jnp.max(jnp.max(reach, axis=1, keepdims=True), axis=0, keepdims=True)
    w_ref[...] = jnp.exp(reach - stab) * (DQK**-0.5)
    norm = jnp.zeros((24, DQK), F32)
    for j in range(BLOCKS):
        span = pl.ds(j * QB, QB)
        weight = jnp.concatenate([w_ref[2 * j : 2 * j + 1, :], w_ref[2 * j + 1 : 2 * j + 2, :]], axis=1)
        k = kt_ref[:, span]
        scaled = (k.astype(F32) * weight).astype(BF16)
        parts = [jnp.broadcast_to(p.astype(F32), (8, QB)) for p in three_parts(weight)]
        parts = jnp.concatenate(parts, axis=0).astype(BF16)
        norm += lax.dot_general(parts, k, (((1,), (1,)), ((), ())), preferred_element_type=F32)
        copies[j].wait()
        product = jnp.dot(scaled, v_ref[span, :], preferred_element_type=F32)
        if j:
            product += acc_ref[...].reshape(DQK, DV)
        acc_ref[...] = product.reshape(ZS, XS, ROWS, DV)
    norm = norm[0:8] + norm[8:16] + norm[16:24]
    row = lax.broadcasted_iota(jnp.int32, (8, DV), 0)
    extra = jnp.concatenate([norm, norm], axis=1)
    extra = jnp.where(row == 1, stab, extra)
    extra = jnp.where(row == 2, later[0:1, 0:1], extra)
    x = x_ref[0]
    for k, ref in enumerate((own_ref, one_ref, two_ref, three_ref)):
        to = lax.rem(x + k, XS)
        ref[0:SLICE, :] = acc_ref[:, pl.ds(to, 1)].reshape(SLICE, DV)
        ref[SLICE:, :] = extra
    tick_ref[...] = extra[:, :LANES]


def state(x, gates, keys_t, values):
    return pl.pallas_call(
        state_kernel,
        in_specs=[SMEM, VMEM, VMEM, HBM],
        out_specs=[VMEM] * 5,
        out_shape=[pltpu.VMEM((SENT, DV), F32)] * 4 + [pltpu.VMEM((8, LANES), F32)],
        scratch_shapes=[
            pltpu.VMEM((TOKS, DV), BF16),
            pltpu.VMEM((PIECES, PIECE), F32),
            pltpu.VMEM((ZS, XS, ROWS, DV), F32),
            pltpu.SemaphoreType.DMA((BLOCKS,)),
        ],
        compiler_params=pltpu.CompilerParams(vmem_limit_bytes=12 * MIB),
        cost_estimate=pl.CostEstimate(flops=600_000_000, bytes_accessed=5 * MIB, transcendentals=0),
        name="shard_state",
    )(x, gates, keys_t, values)


def wide(x, n):
    return jnp.concatenate([x] * (n // LANES), axis=1)


def group_kernel(x_ref, own_ref, one_ref, two_ref, three_ref, after_ref, out_ref, all_ref, small_ref):
    x = x_ref[0]
    row = lax.broadcasted_iota(jnp.int32, (8, LANES), 0)
    for k, ref in enumerate((own_ref, one_ref, two_ref, three_ref)):
        at = lax.rem(x + XS - k, XS)
        all_ref[pl.ds(at, 1)] = ref[0:SLICE, :].reshape(1, ZS, ROWS, DV)
        tail = ref[SLICE:, :]
        small = jnp.where(row == 0, tail[0:1, :LANES], tail[0:1, LANES : 2 * LANES])
        small = jnp.where(row == 2, tail[1:2, :LANES], small)
        small = jnp.where(row == 3, tail[2:3, :LANES], small)
        small_ref[pl.ds(at, 1)] = small.reshape(1, 8, LANES)
    stab = small_ref[0, 2:3, :]
    total = small_ref[0, 3:4, :]
    normal = small_ref[0]
    keeps, takes = [], []
    for j in range(1, XS):
        own_total = small_ref[j, 3:4, :]
        own_stab = small_ref[j, 2:3, :]
        shifted = stab + own_total
        stab = jnp.maximum(shifted, own_stab)
        total = total + own_total
        keep, take = jnp.exp(shifted - stab), jnp.exp(own_stab - stab)
        normal = keep * normal + take * small_ref[j]
        keeps.append(wide(keep, DV))
        takes.append(wide(take, DV))
    for z in range(ZS):
        memory = all_ref[0, z]
        for j in range(1, XS):
            memory = keeps[j - 1] * memory + takes[j - 1] * all_ref[j, z]
        out_ref[z, :, :DV] = memory
    extra = jnp.where(row == 2, stab, normal)
    extra = jnp.where(row == 3, total, extra)
    out_ref[:, :, DV:] = jnp.broadcast_to(extra[None], (ZS, 8, LANES))


def grouped(x, parts, after):
    return pl.pallas_call(
        group_kernel,
        in_specs=[SMEM] + [VMEM] * 4 + [HBM],
        out_specs=[VMEM] * 3,
        out_shape=[
            pltpu.VMEM((ZS, ROWS, WIDE), F32),
            pltpu.HBM((XS, ZS, ROWS, DV), F32),
            pltpu.VMEM((XS, 8, LANES), F32),
        ],
        compiler_params=pltpu.CompilerParams(vmem_limit_bytes=4 * MIB),
        cost_estimate=pl.CostEstimate(flops=1_000_000, bytes_accessed=2 * MIB, transcendentals=0),
        name="group_states",
    )(x, *parts, in_hbm(after))


def chain_kernel(x_ref, z_ref, got_ref, small_ref, after_ref, before_ref, close_ref, norm_ref, top_ref, group_ref, mine_ref):
    row = lax.broadcasted_iota(jnp.int32, (8, LANES), 0)
    stab = jnp.full((1, LANES), NEG, F32)
    memory = jnp.zeros((ROWS, DV), F32)
    normal = jnp.zeros((8, LANES), F32)
    group = normal
    for k in range(ZS):
        before_ref[k] = memory
        group = jnp.where(z_ref[0] == k, jnp.where(row == 2, stab, normal), group)
        shifted = stab + got_ref[k, 3:4, DV:]
        own_stab = got_ref[k, 2:3, DV:]
        stab = jnp.maximum(shifted, own_stab)
        keep, take = jnp.exp(shifted - stab), jnp.exp(own_stab - stab)
        memory = wide(keep, DV) * memory + wide(take, DV) * got_ref[k, :, :DV]
        normal = keep * normal + take * got_ref[k, :, DV:]
    close_ref[0] = memory
    norm_ref[0:1, :LANES] = normal[0:1]
    norm_ref[0:1, LANES:] = normal[1:2]
    top_ref[...] = stab
    group_ref[...] = group
    mine = group
    normal, stab = group, group[2:3]
    for j in range(XS - 1):
        shifted = stab + small_ref[j, 3:4, :]
        own_stab = small_ref[j, 2:3, :]
        stab = jnp.maximum(shifted, own_stab)
        keep, take = jnp.exp(shifted - stab), jnp.exp(own_stab - stab)
        normal = keep * normal + take * small_ref[j]
        mine = jnp.where(x_ref[0] == j + 1, jnp.where(row == 2, stab, normal), mine)
    mine_ref[...] = mine


def chained(x, z, got, small, after):
    return pl.pallas_call(
        chain_kernel,
        in_specs=[SMEM, SMEM, VMEM, VMEM, HBM],
        out_specs=[VMEM] * 6,
        out_shape=[
            pltpu.VMEM((ZS, ROWS, DV), F32),
            pltpu.HBM((1, ROWS, DV), F32),
            pltpu.HBM((1, DQK), F32),
            pltpu.HBM((1, LANES), F32),
            pltpu.VMEM((8, LANES), F32),
            pltpu.VMEM((8, LANES), F32),
        ],
        compiler_params=pltpu.CompilerParams(vmem_limit_bytes=4 * MIB),
        cost_estimate=pl.CostEstimate(flops=1_000_000, bytes_accessed=MIB, transcendentals=0),
        name="chain_groups",
    )(x, z, got, small, in_hbm(after))


def spread_kernel(x_ref, got_ref, all_ref, small_ref, group_ref, mine_in, own_ref, one_ref, two_ref, three_ref, mine_ref, out_ref):
    x = x_ref[0]
    stab = group_ref[2:3, :]
    keeps, takes = [], []
    for j in range(XS - 1):
        shifted = stab + small_ref[j, 3:4, :]
        own_stab = small_ref[j, 2:3, :]
        stab = jnp.maximum(shifted, own_stab)
        keeps.append(wide(jnp.exp(shifted - stab), DV))
        takes.append(wide(jnp.exp(own_stab - stab), DV))
    for z in range(ZS):
        memory = got_ref[z]
        out_ref[0, z] = memory
        for j in range(XS - 1):
            memory = keeps[j] * memory + takes[j] * all_ref[j, z]
            out_ref[j + 1, z] = memory
    for k, ref in enumerate((own_ref, one_ref, two_ref, three_ref)):
        to = lax.rem(x + k, XS)
        ref[...] = out_ref[pl.ds(to, 1)].reshape(ZS, ROWS, DV)
    mine_ref[...] = mine_in[...]


def spread(x, got, everything, small, group, mine):
    return pl.pallas_call(
        spread_kernel,
        in_specs=[SMEM] + [VMEM] * 5,
        out_specs=[VMEM] * 5,
        out_shape=[pltpu.VMEM((ZS, ROWS, DV), F32)] * 4 + [pltpu.VMEM((8, LANES), F32)],
        scratch_shapes=[pltpu.VMEM((XS, ZS, ROWS, DV), F32)],
        compiler_params=pltpu.CompilerParams(vmem_limit_bytes=4 * MIB),
        cost_estimate=pl.CostEstimate(flops=1_000_000, bytes_accessed=2 * MIB, transcendentals=0),
        name="spread_prefixes",
    )(x, got, everything, small, group, mine)


def column(row):
    n = row.shape[1]
    return jnp.concatenate(
        [
            jnp.broadcast_to(row[:, at : at + LANES], (LANES, LANES)).T
            for at in range(0, n, LANES)
        ],
        axis=0,
    )


def tables(g_ref, table_ref):
    own, cum = [], []
    for r in range(0, PIECES, 2):
        first = g_ref[r, 1:2, :][:, PIECE - 1 :]
        own.append(jnp.concatenate([g_ref[r, 0:1, :], g_ref[r + 1, 0:1, :] - first], axis=1))
        cum.append(jnp.concatenate([g_ref[r, 1:2, :], g_ref[r + 1, 1:2, :] + first], axis=1))
    own = jnp.concatenate(own, axis=0)
    cum = jnp.concatenate(cum, axis=0)
    table_ref[0:BLOCKS, :] = own
    table_ref[BLOCKS : 2 * BLOCKS, :] = cum
    lane = lax.broadcasted_iota(jnp.int32, (BLOCKS, QB), 1)
    top = own
    shift = 1
    while shift < QB:
        moved = pltpu.roll(top, shift, 1)
        top = jnp.maximum(top, jnp.where(lane >= shift, moved, NEG))
        shift *= 2
    stab = jnp.full((1, 1), NEG, F32)
    for r in range(BLOCKS):
        at = 2 * BLOCKS + r
        table_ref[at : at + 1, :] = jnp.maximum(top[r : r + 1], stab)
        stab = jnp.maximum(stab, top[r : r + 1, QB - 1 :]) + cum[r : r + 1, QB - 1 :]


def attend(blocks, hbm, num_hbm, den_hbm, num_ref, den_ref, table_ref, q_ref, k_ref, v_ref, in_sem, out_sem, ready):
    q_hbm, k_hbm, v_hbm = hbm
    last = blocks[-1]

    def fetch(n, ref, j):
        span = pl.ds(pl.multiple_of(j * QB, QB), QB)
        return pltpu.make_async_copy(hbm[n].at[span], ref.at[span], in_sem.at[n, j])

    for i in reversed(blocks):
        fetch(0, q_ref, i).start()
    for j in range(last, -1, -1):
        fetch(1, k_ref, j).start()
        fetch(2, v_ref, j).start()
    ready()
    copies = []
    for n in range(len(blocks) - 1, -1, -1):
        i = blocks[n]
        here = pl.ds(n * QB, QB)
        top = wide(column(table_ref[2 * BLOCKS + i : 2 * BLOCKS + i + 1, :]), QB)
        fetch(0, q_ref, i).wait()
        q = q_ref[pl.ds(i * QB, QB), :]
        fresh = n == len(blocks) - 1

        def block(j, shift, masked):
            if fresh:
                fetch(1, k_ref, j).wait()
            at = pl.ds(pl.multiple_of(j * QB, QB), QB)
            scores = lax.dot_general(q, k_ref[at, :], (((1,), (1,)), ((), ())), preferred_element_type=F32) * (DQK**-0.5)
            power = (table_ref[pl.ds(j, 1), :] + shift) - top
            if masked:
                past = lax.broadcasted_iota(jnp.int32, (QB, QB), 0) >= lax.broadcasted_iota(jnp.int32, (QB, QB), 1)
                power = jnp.where(past, power, NEG)
            mixed = jnp.exp(power) * scores
            if fresh:
                fetch(2, v_ref, j).wait()
            lanes = sum(mixed[:, c : c + LANES] for c in range(0, QB, LANES))
            return lanes, jnp.dot(mixed.astype(BF16), v_ref[at, :], preferred_element_type=F32)

        den_ref[here, :], num_ref[here, :] = block(i, jnp.zeros((1, 1), F32), True)

        def earlier(m, shift):
            j = i - 1 - m
            shift = shift + table_ref[pl.ds(BLOCKS + j, 1), :][:, QB - 1 :]
            lanes, product = block(j, shift, False)
            den_ref[here, :] += lanes
            num_ref[here, :] += product
            return shift

        if i:
            lax.fori_loop(0, i, earlier, jnp.zeros((1, 1), F32))
        for m, (ref, out) in enumerate(((num_ref, num_hbm), (den_ref, den_hbm))):
            copies.append(pltpu.make_async_copy(ref.at[here], out.at[here], out_sem.at[m, n]))
            copies[-1].start()
    for copy in copies:
        copy.wait()


def first_kernel(blocks, g_ref, tick_ref, q_hbm, k_hbm, v_hbm, num_hbm, den_hbm, table_hbm, num_ref, den_ref, table_ref, q_ref, k_ref, v_ref, in_sem, out_sem, sem):
    copy = pltpu.make_async_copy(table_ref, table_hbm, sem)

    def ready():
        tables(g_ref, table_ref)
        copy.start()

    attend(blocks, (q_hbm, k_hbm, v_hbm), num_hbm, den_hbm, num_ref, den_ref, table_ref, q_ref, k_ref, v_ref, in_sem, out_sem, ready)
    copy.wait()


def next_kernel(blocks, table_hbm, tick_ref, q_hbm, k_hbm, v_hbm, num_hbm, den_hbm, num_ref, den_ref, table_ref, q_ref, k_ref, v_ref, in_sem, out_sem, sem):
    copy = pltpu.make_async_copy(table_hbm, table_ref, sem)
    copy.start()
    attend(blocks, (q_hbm, k_hbm, v_hbm), num_hbm, den_hbm, num_ref, den_ref, table_ref, q_ref, k_ref, v_ref, in_sem, out_sem, copy.wait)


def last_kernel(blocks, table_hbm, tick_ref, q_hbm, k_hbm, v_hbm, all_hbm, num_hbm, den_hbm, all_ref, *rest):
    sem = rest[-1]
    copy = pltpu.make_async_copy(all_hbm, all_ref, sem)
    next_kernel(blocks, table_hbm, tick_ref, q_hbm, k_hbm, v_hbm, num_hbm, den_hbm, *rest[:-1])
    copy.start()
    copy.wait()


def local(blocks, gates, tick, queries, keys, values, table=None, everything=None):
    count = len(blocks)
    units = sum(blocks) + count
    args = [gates if table is None else in_hbm(table), tick, in_hbm(queries), in_hbm(keys), in_hbm(values)]
    in_specs = [VMEM if table is None else HBM, ANY, HBM, HBM, HBM]
    out_specs = [HBM] * 2
    out_shape = [pltpu.HBM((count * QB, DV), F32), pltpu.HBM((count * QB, LANES), F32)]
    scratch = [
        pltpu.VMEM((count * QB, DV), F32),
        pltpu.VMEM((count * QB, LANES), F32),
        pltpu.VMEM((3 * BLOCKS, QB), F32),
        pltpu.VMEM((TOKS, DQK), BF16),
        pltpu.VMEM((TOKS, DQK), BF16),
        pltpu.VMEM((TOKS, DV), BF16),
        pltpu.SemaphoreType.DMA((3, BLOCKS)),
        pltpu.SemaphoreType.DMA((2, count)),
        pltpu.SemaphoreType.DMA(()),
    ]
    kernel = next_kernel
    if table is None:
        kernel = first_kernel
        out_specs += [HBM]
        out_shape += [pltpu.HBM((3 * BLOCKS, QB), F32)]
    if everything is not None:
        kernel = last_kernel
        args += [in_hbm(everything)]
        in_specs += [HBM]
        out_specs += [VMEM]
        out_shape += [pltpu.VMEM(everything.shape, F32)]
        scratch += [pltpu.SemaphoreType.DMA(())]
    return pl.pallas_call(
        functools.partial(kernel, blocks),
        in_specs=in_specs,
        out_specs=out_specs,
        out_shape=out_shape,
        scratch_shapes=scratch,
        compiler_params=pltpu.CompilerParams(vmem_limit_bytes=20 * MIB),
        cost_estimate=pl.CostEstimate(flops=800_000_000 * units, bytes_accessed=MIB * units, transcendentals=0),
        name="within_shard",
    )(*args)


def scale_kernel(mine_ref, table_hbm, q_hbm, *refs):
    count = len(PARTS)
    hbms, (pre_ref, carried_ref, q_ref, table_ref, den_ref, num_ref, table_sem, q_sem, sem) = refs[: 2 * count], refs[2 * count :]
    place = {i: (n, m) for n, blocks in enumerate(PARTS) for m, i in enumerate(blocks)}
    table_copy = pltpu.make_async_copy(table_hbm, table_ref, table_sem)
    table_copy.start()
    copies = []
    for i in range(BLOCKS):
        n, m = place[i]
        here, there = pl.ds(i * QB, QB), pl.ds(m * QB, QB)
        copies.append(
            (
                pltpu.make_async_copy(q_hbm.at[here], q_ref.at[here], q_sem.at[i]),
                pltpu.make_async_copy(hbms[2 * n + 1].at[there], den_ref.at[here], sem.at[1, i]),
                pltpu.make_async_copy(hbms[2 * n].at[there], num_ref.at[here], sem.at[0, i]),
            )
        )
        for copy in copies[-1]:
            copy.start()
    table_copy.wait()
    log_in = mine_ref[2:3, :]
    norm = jnp.concatenate([mine_ref[0:1, :], mine_ref[1:2, :]], axis=1)
    for i in range(BLOCKS):
        here = pl.ds(i * QB, QB)
        top = column(table_ref[2 * BLOCKS + i : 2 * BLOCKS + i + 1, :])
        peak = jnp.maximum(top, log_in)
        kept, carried = jnp.exp(top - peak), jnp.exp(log_in - peak)
        copies[i][0].wait()
        from_norm = jnp.sum(q_ref[here, :].astype(F32) * norm, axis=1, keepdims=True)
        copies[i][1].wait()
        denom = jnp.sum(den_ref[here, :], axis=1, keepdims=True) * kept + carried * from_norm
        inverse = 1.0 / jnp.maximum(jnp.abs(denom), 1.0)
        carried_ref[here, :] = carried * inverse
        copies[i][2].wait()
        pre_ref[here, :] = wide(kept * inverse, DV) * num_ref[here, :]
        log_in = log_in + table_ref[BLOCKS + i : BLOCKS + i + 1, :][:, QB - 1 :]


def scaled(table, mine, queries, pieces):
    refs = [in_hbm(a) for piece in pieces for a in piece]
    return pl.pallas_call(
        scale_kernel,
        in_specs=[VMEM] + [HBM] * (2 + len(refs)),
        out_specs=[VMEM] * 3,
        out_shape=[
            pltpu.VMEM((TOKS, DV), F32),
            pltpu.VMEM((TOKS, LANES), F32),
            pltpu.VMEM((TOKS, DQK), BF16),
        ],
        scratch_shapes=[
            pltpu.VMEM((3 * BLOCKS, QB), F32),
            pltpu.VMEM((TOKS, LANES), F32),
            pltpu.VMEM((TOKS, DV), F32),
            pltpu.SemaphoreType.DMA(()),
            pltpu.SemaphoreType.DMA((BLOCKS,)),
            pltpu.SemaphoreType.DMA((2, BLOCKS)),
        ],
        compiler_params=pltpu.CompilerParams(vmem_limit_bytes=12 * MIB),
        cost_estimate=pl.CostEstimate(flops=1_600_000_000, bytes_accessed=8 * MIB, transcendentals=0),
        name="row_scales",
    )(mine, in_hbm(table), in_hbm(queries), *refs)


def joined_kernel(x_ref, q_ref, own_ref, one_ref, two_ref, three_ref, carried_ref, pre_ref, out_hbm, mem_ref, mem_b_ref, out_ref, sem):
    x = x_ref[0]
    for k, ref in enumerate((own_ref, one_ref, two_ref, three_ref)):
        at = lax.rem(x + XS - k, XS)
        mem_ref[:, pl.ds(at, 1)] = ref[...].reshape(ZS, 1, ROWS, DV)
    mem_b_ref[...] = mem_ref[...].reshape(DQK, DV).astype(BF16)
    copies = []
    for i in range(BLOCKS):
        span = pl.ds(i * QB, QB)
        product = jnp.dot(q_ref[span, :], mem_b_ref[...], preferred_element_type=F32)
        out_ref[span, :] = (pre_ref[span, :] + wide(carried_ref[span, :], DV) * product).astype(BF16)
        copies.append(pltpu.make_async_copy(out_ref.at[span], out_hbm.at[span], sem.at[i]))
        copies[-1].start()
    for copy in copies:
        copy.wait()


def joined(x, queries, parts, carried, pre):
    return pl.pallas_call(
        joined_kernel,
        in_specs=[SMEM] + [VMEM] * 7,
        out_specs=HBM,
        out_shape=jax.ShapeDtypeStruct((TOKS, DV), BF16),
        scratch_shapes=[
            pltpu.VMEM((ZS, XS, ROWS, DV), F32),
            pltpu.VMEM((DQK, DV), BF16),
            pltpu.VMEM((TOKS, DV), BF16),
            pltpu.SemaphoreType.DMA((BLOCKS,)),
        ],
        compiler_params=pltpu.CompilerParams(vmem_limit_bytes=8 * MIB),
        cost_estimate=pl.CostEstimate(flops=600_000_000, bytes_accessed=9 * MIB, transcendentals=0),
        name="join_memory",
    )(x, queries, *parts, carried, pre)


def exchanged(x, axis):
    return lax.all_to_all(x, axis, split_axis=0, concat_axis=0, tiled=True)


def around(parts):
    moved = [parts[0]]
    for k in range(1, XS):
        moved.append(lax.ppermute(parts[k], "ctx_1", [(i, (i + k) % XS) for i in range(XS)]))
    return moved


def on_device(queries, keys, values, gate_pre):
    x = lax.axis_index("ctx_1").astype(jnp.int32).reshape(1)
    z = lax.axis_index("ctx_0").astype(jnp.int32).reshape(1)
    gates = exchanged(gate_sums(gate_pre), "head")
    keys_t = turned(keys)
    *parts, tick = state(x, gates, keys_t, values)
    moved = around(parts)
    qkv = (queries, keys, values)
    num_a, den_a, table = local(PARTS[0], gates, tick, *qkv)
    total, everything, small = grouped(x, moved, den_a)
    got = exchanged(total, "ctx_0")
    num_b, den_b = local(PARTS[1], None, small, *qkv, table)
    before, closing, final_norm, top, group, mine = chained(x, z, got, small, den_b)
    back = exchanged(before, "ctx_0")
    num_c, den_c, everything = local(PARTS[2], None, mine, *qkv, table, everything)
    *parts, mine = spread(x, back, everything, small, group, mine)
    moved = around(parts)
    pre, carried, q = scaled(table, mine, queries, [(num_a, den_a), (num_b, den_b), (num_c, den_c)])
    hidden = joined(x, q, moved, carried, pre)
    return (hidden, closing, final_norm, top[0, :1])


def solution(mesh):
    split = Mesh(mesh.devices.reshape(8, 4, mesh.shape["head"]), ("ctx_0", "ctx_1", "head"))
    in_specs = (P(CTX, "head"), P(CTX, "head"), P(CTX, "head"), P(None, None, CTX_HEAD))
    out_specs = (P(CTX, "head"), P("head", CTX, None), P("head", None), P("head"))
    return jax.shard_map(
        on_device, mesh=split, in_specs=in_specs, out_specs=out_specs, check_vma=False
    )
```

time: 243 us -> 68.6 us (0.28)
  waiting for transfers between devices: 66.4 us -> 7.87 us
  between operations: 44.1 us -> 0.92 us
  matrix products: 41.5 us -> 0 us
  Pallas kernels: 0 us -> 28.4 us
  other arithmetic: 22.3 us -> 0 us
  local copies, waits for them, and re-layouts: 21.7 us -> 2.09 us
  blocking collectives: 12.8 us -> 0 us
  loops' own time: 8.29 us -> 0 us
  starting transfers between devices: 23 us -> 28.3 us
    dot_general x22 -> x0, matrix products: 41.5 us -> none  [the longest x4 10.5 us: block_step(): jnp.dot(q_float, memory, precision=lax.Precision.HIGHEST)]
    all_gather x2 -> x0, waiting for transfers between devices: 34.6 us -> none  [all_in_one(): both, at, found = (lax.all_gather(jnp.concatenate(lines), axis), 0, {})]
    pallas_call x0 -> x11, Pallas kernels: none -> 28.4 us  [the longest x3 17.1 us: local(): pl.pallas_call(functools.partial(kernel, blocks), in_specs=in_specs, out_...]
    all_to_all x4 -> x3, waiting for transfers between devices: 31.8 us -> 7.85 us  [exchanged(): return lax.all_to_all(x, axis, split_axis=0, concat_axis=0, tiled=True)]
    all_to_all x1 -> x0, blocking collectives: 12.8 us -> none  [sent_to_all(): return lax.all_to_all(copies, axis, split_axis=0, concat_axis=0, tiled=True)]
    ppermute x0 -> x6, starting transfers between devices: none -> 10.5 us  [around(): lax.ppermute(parts[k], 'ctx_1', [(i, (i + k) % XS) for i in range(XS)])]
    slice x26 -> x0, local copies, waits for them, and re-layouts: 9.22 us -> none  [the longest x4 2.44 us: prefix_by_axis(): so_far = combine(so_far, jax.tree.map(lambda part: part[k], pieces))]
    another operation x1 -> x0, loops' own time: 8.29 us -> none  [local_chain(): final, outs = lax.scan(block_step, start, blocks)]
  transfers between devices with their start and end apart: 6 -> 9, of which waited for: 5 -> 3; matrix products, arithmetic and copies ran while one was open for 5% -> 0% of each run, Pallas kernels for 0% -> 33%
where the time goes in v1:
time: 68.6 us; the launch traced here: 67.6 us
  Pallas kernels  28.4 us (41%)
  starting transfers between devices  28.3 us (41%)
  waiting for transfers between devices  7.87 us (11%)
  local copies, waits for them, and re-layouts  2.09 us (3%)
  between operations  0.92 us (1%)
    all_to_all x3, starting transfers between devices, exchanged(): return lax.all_to_all(x, axis, split_axis=0, concat_axis=0, tiled=True)  17.8 us
    pallas_call x3, Pallas kernels, local(): pl.pallas_call(functools.partial(kernel, blocks), in_specs=in_specs, out_...  17.1 us
    ppermute x6, starting transfers between devices, around(): lax.ppermute(parts[k], 'ctx_1', [(i, (i + k) % XS) for i in range(XS)])  10.5 us
    all_to_all x3, waiting for transfers between devices, exchanged(): return lax.all_to_all(x, axis, split_axis=0, concat_axis=0, tiled=True)  7.85 us
    pallas_call x1, Pallas kernels, scaled(): pl.pallas_call(scale_kernel, in_specs=[VMEM] + [HBM] * (2 + len(refs)), o...  4.51 us
    unnamed x6, local copies, waits for them, and re-layouts  2.09 us
    pallas_call x1, Pallas kernels, state(): pl.pallas_call(state_kernel, in_specs=[SMEM, VMEM, VMEM, HBM], out_specs=...  2.02 us
    pallas_call x1, Pallas kernels, joined(): pl.pallas_call(joined_kernel, in_specs=[SMEM] + [VMEM] * 7, out_specs=HBM...  1.74 us
  transfers between devices with their start and end apart: 9, of which 3 were waited for; matrix products, arithmetic and copies ran while one was open for 0% of the time, Pallas kernels for 33%

profile of v1, /device:TPU:32, one launch (start us, length us, event | category | flops | bytes accessed | tf_op | source)
XLA Modules:
  0.0 67.6 jit_solution(1380011293683431765)
XLA Ops:
  0.7 0.9 %copy-done.2 = f32[2,8,256]{2,1,0:T(8,128)S(1)} copy-done((f32[2,8,256]{2,1,0:T(8,128)S(1)}, f32[2,8,256]{2,1,0:T(8,128)}, u32[]{:S(2)}) %copy-start.2) | copy-done | bytes 16408
  1.5 0.8 %gate_sums.1 = f32[8,2,256]{2,1,0:T(2,128)} custom-call(f32[2,8,256]{2,1,0:T(8,128)S(1)} %copy-done.2), custom_call_target="tpu_custom_call" | custom-call | tf_op jit(solution)/shard_map/gate_sums/pallas_call | solution.py:80
  2.3 4.5 %all-to-all-start = ((f32[8,2,256]{2,1,0:T(2,128)}), f32[8,2,256]{2,1,0:T(2,128)S(1)}, u32[]{:S(2)}, u32[]{:S(2)}) async-start(f32[8,2,256]{2,1,0:T(2,128)} %gate_sums.1), calls=%async_computation | async-start | bytes 32768 | tf_op jit(solution)/shard_map/all_to_all | solution.py:567
  6.8 1.2 %copy-done.1 = bf16[2048,256]{1,0:T(8,128)(2,1)S(1)} copy-done((bf16[2048,256]{1,0:T(8,128)(2,1)S(1)}, bf16[2048,256]{1,0:T(8,128)(2,1)}, u32[]{:S(2)}) %copy-start.1) | copy-done | bytes 1048600
  8.0 0.6 turn_keys.1.kt_ref
  8.6 3.5 %all-to-all-done.g_ref = f32[8,2,256]{2,1,0:T(2,128)S(1)} async-done(((f32[8,2,256]{2,1,0:T(2,128)}), f32[8,2,256]{2,1,0:T(2,128)S(1)}, u32[]{:S(2)}, u32[]{:S(2)}) %all-to-all-start) | async-done | bytes 16416 | tf_op jit(solution)/shard_map/all_to_all | solution.py:567
  12.1 2.0 %shard_state.1 = (f32[72,512]{1,0:T(8,128)S(1)}, f32[72,512]{1,0:T(8,128)S(1)}, f32[72,512]{1,0:T(8,128)S(1)}, f32[72,512]{1,0:T(8,128)S(1)}, f32[8,128]{1,0:T(8,128)S(1)}) custom-call(s32[1]{0:T(128)} %bitcast.x_ref, f32[8,2,256]{2,1,0:T(2,128)S(1)} %all-to-all-done.g_ref, bf16[256,2048]{1,0:T(8,128)(2,1)S(1)} %turn_keys.1.kt_ref, bf16[2048,512]{1,0:T(8,128)(2,1)S(1)} %copy-done), custom_call_target="tpu_custom_call" | custom-call | flops 600000000 | bytes 5242880 | tf_op jit(solution)/shard_map/shard_state/pallas_call | solution.py:151
  14.1 1.6 %collective-permute-start = (f32[72,512]{1,0:T(8,128)S(1)}, f32[72,512]{1,0:T(8,128)S(1)}, u32[]{:S(2)}, u32[]{:S(2)}) collective-permute-start(f32[72,512]{1,0:T(8,128)S(1)} %get-tuple-element.35), channel_id=1, source_target_pairs={{0,8},{8,16},{16,24},{24,0},{1,9},{9,17},{17,25},{25,1},{2,10},{10... | collective-permute-start | bytes 442376 | tf_op jit(solution)/shard_map/ppermute | solution.py:573
  15.7 2.7 %collective-permute-start.1 = (f32[72,512]{1,0:T(8,128)S(1)}, f32[72,512]{1,0:T(8,128)S(1)}, u32[]{:S(2)}, u32[]{:S(2)}) collective-permute-start(f32[72,512]{1,0:T(8,128)S(1)} %get-tuple-element.36), channel_id=1, source_target_pairs={{0,16},{8,24},{16,0},{24,8},{1,17},{9,25},{17,1},{25,9},{2,18},{10... | collective-permute-start | bytes 442376 | tf_op jit(solution)/shard_map/ppermute | solution.py:573
  18.5 1.4 %collective-permute-start.2 = (f32[72,512]{1,0:T(8,128)S(1)}, f32[72,512]{1,0:T(8,128)S(1)}, u32[]{:S(2)}, u32[]{:S(2)}) collective-permute-start(f32[72,512]{1,0:T(8,128)S(1)} %get-tuple-element.37), channel_id=1, source_target_pairs={{0,24},{8,0},{16,8},{24,16},{1,25},{9,1},{17,9},{25,17},{2,26},{10... | collective-permute-start | bytes 442376 | tf_op jit(solution)/shard_map/ppermute | solution.py:573
  19.9 5.8 %within_shard.3 = (f32[512,512]{1,0:T(8,128)}, f32[512,128]{1,0:T(8,128)}, f32[12,512]{1,0:T(8,128)}) custom-call(f32[8,2,256]{2,1,0:T(2,128)S(1)} %all-to-all-done.g_ref, f32[8,128]{1,0:T(8,128)S(1)} %get-tuple-element.38.tick_ref, bf16[2048,256]{1,0:T(8,128)(2,1)} %q_hbm.7, bf16[2048,256]{1,0:T(8,128)(2,1)} %k_hbm.5, bf16[2048,512]{1,0:T(8,128)(2,1)} %v_hbm.7), custom_call_target="tpu_custom_call" | custom-call | flops 3200000000 | bytes 4194304 | tf_op jit(solution)/shard_map/within_shard/pallas_call | solution.py:456
  25.7 0.9 %group_states.1 = (f32[8,8,640]{2,1,0:T(8,128)}, f32[4,8,8,512]{3,2,1,0:T(8,128)}, f32[4,8,128]{2,1,0:T(8,128)S(1)}) custom-call(s32[1]{0:T(128)} %bitcast.x_ref, f32[72,512]{1,0:T(8,128)S(1)} %get-tuple-element.34.own_ref, f32[72,512]{1,0:T(8,128)S(1)} %collective-permute-done.one_ref, f32[72,512]{1,0:T(8,128)S(1)} %collective-permute-done.1.two_ref, ...), custom_call_target="tpu_custom_call" | custom-call | flops 1000000 | bytes 2097152 | tf_op jit(solution)/shard_map/group_states/pallas_call | solution.py:208
  26.6 8.6 %all-to-all-start.1 = ((f32[8,8,640]{2,1,0:T(8,128)}), f32[8,8,640]{2,1,0:T(8,128)S(1)}, u32[]{:S(2)}, u32[]{:S(2)}) async-start(f32[8,8,640]{2,1,0:T(8,128)} %get-tuple-element.40), calls=%async_computation.1 | async-start | bytes 327680 | tf_op jit(solution)/shard_map/all_to_all | solution.py:567
  35.2 5.4 %within_shard.4 = (f32[512,512]{1,0:T(8,128)}, f32[512,128]{1,0:T(8,128)}) custom-call(f32[12,512]{1,0:T(8,128)} %get-tuple-element.42.table_hbm, f32[4,8,128]{2,1,0:T(8,128)S(1)} %get-tuple-element.41.tick_ref.small_ref, bf16[2048,256]{1,0:T(8,128)(2,1)} %q_hbm.7, bf16[2048,256]{1,0:T(8,128)(2,1)} %k_hbm.5, bf16[2048,512]{1,0:T(8,128)(2,1)} %v_hbm.7), custom_call_target="tpu_custom_call" | custom-call | flops 2400000000 | bytes 3145728 | tf_op jit(solution)/shard_map/within_shard/pallas_call | solution.py:456
  40.6 2.6 %all-to-all-done.1.got_ref = f32[8,8,640]{2,1,0:T(8,128)S(1)} async-done(((f32[8,8,640]{2,1,0:T(8,128)}), f32[8,8,640]{2,1,0:T(8,128)S(1)}, u32[]{:S(2)}, u32[]{:S(2)}) %all-to-all-start.1) | async-done | bytes 163872 | tf_op jit(solution)/shard_map/all_to_all | solution.py:567
  43.2 0.7 %chain_groups.1 = (f32[8,8,512]{2,1,0:T(8,128)}, f32[1,8,512]{2,1,0:T(8,128)}, f32[1,256]{1,0:T(1,128)}, f32[1,128]{1,0:T(1,128)}, f32[8,128]{1,0:T(8,128)S(1)}, /*index=5*/f32[8,128]{1,0:T(8,128)S(1)}) custom-call(s32[1]{0:T(128)} %bitcast.x_ref, s32[1]{0:T(128)} %bitcast.1.z_ref, f32[8,8,640]{2,1,0:T(8,128)S(1)} %all-to-all-done.1.got_ref, ...), custom_call_target="tpu_custom_call" | custom-call | flops 1000000 | bytes 1048576 | tf_op jit(solution)/shard_map/chain_groups/pallas_call | solution.py:256
  43.9 4.7 %all-to-all-start.2 = ((f32[8,8,512]{2,1,0:T(8,128)}), f32[8,8,512]{2,1,0:T(8,128)S(1)}, u32[]{:S(2)}, u32[]{:S(2)}) async-start(f32[8,8,512]{2,1,0:T(8,128)} %get-tuple-element.44), calls=%async_computation.2 | async-start | bytes 262144 | tf_op jit(solution)/shard_map/all_to_all | solution.py:567
  48.6 5.9 %within_shard.5 = (f32[1024,512]{1,0:T(8,128)}, f32[1024,128]{1,0:T(8,128)}, f32[4,8,8,512]{3,2,1,0:T(8,128)S(1)}) custom-call(f32[12,512]{1,0:T(8,128)} %get-tuple-element.42.table_hbm, f32[8,128]{1,0:T(8,128)S(1)} %get-tuple-element.45.tick_ref.mine_in, bf16[2048,256]{1,0:T(8,128)(2,1)} %q_hbm.7, bf16[2048,256]{1,0:T(8,128)(2,1)} %k_hbm.5, ...), custom_call_target="tpu_custom_call" | custom-call | flops 2400000000 | bytes 3145728 | tf_op jit(solution)/shard_map/within_shard/pallas_call | solution.py:456
  54.5 1.8 %all-to-all-done.2.got_ref = f32[8,8,512]{2,1,0:T(8,128)S(1)} async-done(((f32[8,8,512]{2,1,0:T(8,128)}), f32[8,8,512]{2,1,0:T(8,128)S(1)}, u32[]{:S(2)}, u32[]{:S(2)}) %all-to-all-start.2) | async-done | bytes 131104 | tf_op jit(solution)/shard_map/all_to_all | solution.py:567
  56.4 0.8 %collective-permute-start.3 = (f32[8,8,512]{2,1,0:T(8,128)S(1)}, f32[8,8,512]{2,1,0:T(8,128)S(1)}, u32[]{:S(2)}, u32[]{:S(2)}) collective-permute-start(f32[8,8,512]{2,1,0:T(8,128)S(1)} %get-tuple-element.56), channel_id=1, source_target_pairs={{0,8},{8,16},{16,24},{24,0},{1,9},{9,17},{17,25},{25,1},{2,10},{10... | collective-permute-start | bytes 393224 | tf_op jit(solution)/shard_map/ppermute | solution.py:573
  57.2 2.4 %collective-permute-start.4 = (f32[8,8,512]{2,1,0:T(8,128)S(1)}, f32[8,8,512]{2,1,0:T(8,128)S(1)}, u32[]{:S(2)}, u32[]{:S(2)}) collective-permute-start(f32[8,8,512]{2,1,0:T(8,128)S(1)} %get-tuple-element.57), channel_id=1, source_target_pairs={{0,16},{8,24},{16,0},{24,8},{1,17},{9,25},{17,1},{25,9},{2,18},{10... | collective-permute-start | bytes 393224 | tf_op jit(solution)/shard_map/ppermute | solution.py:573
  59.6 1.6 %collective-permute-start.5 = (f32[8,8,512]{2,1,0:T(8,128)S(1)}, f32[8,8,512]{2,1,0:T(8,128)S(1)}, u32[]{:S(2)}, u32[]{:S(2)}) collective-permute-start(f32[8,8,512]{2,1,0:T(8,128)S(1)} %get-tuple-element.58), channel_id=1, source_target_pairs={{0,24},{8,0},{16,8},{24,16},{1,25},{9,1},{17,9},{25,17},{2,26},{10... | collective-permute-start | bytes 393224 | tf_op jit(solution)/shard_map/ppermute | solution.py:573
  61.1 4.5 %row_scales.1 = (f32[2048,512]{1,0:T(8,128)S(1)}, f32[2048,128]{1,0:T(8,128)S(1)}, bf16[2048,256]{1,0:T(8,128)(2,1)S(1)}) custom-call(f32[8,128]{1,0:T(8,128)S(1)} %get-tuple-element.49.mine_ref, f32[12,512]{1,0:T(8,128)} %get-tuple-element.42.table_hbm, bf16[2048,256]{1,0:T(8,128)(2,1)} %q_hbm.7, f32[512,512]{1,0:T(8,128)} %get-tuple-element.50.refs_0_, ...), custom_call_target="tpu_custom_call" | custom-call | flops 1600000000 | bytes 8388608 | tf_op jit(solution)/shard_map/row_scales/pallas_call | solution.py:508
  65.7 1.7 %join_memory.1 = bf16[2048,512]{1,0:T(8,128)(2,1)} custom-call(s32[1]{0:T(128)} %bitcast.x_ref, bf16[2048,256]{1,0:T(8,128)(2,1)S(1)} %get-tuple-element.54.q_ref, f32[8,8,512]{2,1,0:T(8,128)S(1)} %get-tuple-element.55.own_ref, f32[8,8,512]{2,1,0:T(8,128)S(1)} %collective-permute-done.3.one_ref, f32[8,8,512]{2,1,0:T(8,128)S(1)} %collective-permute-done.4.two_ref, ...), custom_call_target="tpu_custom_call" | custom-call | flops 600000000 | bytes 9437184 | tf_op jit(solution)/shard_map/join_memory/pallas_call | solution.py:549
  (11 shorter events, 0.1 us)
Async XLA Ops:
  0.6 11.5 %copy-start = (bf16[2048,512]{1,0:T(8,128)(2,1)S(1)}, bf16[2048,512]{1,0:T(8,128)(2,1)}, u32[]{:S(2)}) copy-start(bf16[2048,512]{1,0:T(8,128)(2,1)} %v_hbm.7) | copy-start | bytes 6291460
  0.6 0.9 %copy-start.2 = (f32[2,8,256]{2,1,0:T(8,128)S(1)}, f32[2,8,256]{2,1,0:T(8,128)}, u32[]{:S(2)}) copy-start(f32[2,8,256]{2,1,0:T(8,128)} %g_ref.1) | copy-start | bytes 49156
  2.3 9.8 %all-to-all-start = ((f32[8,2,256]{2,1,0:T(2,128)}), f32[8,2,256]{2,1,0:T(2,128)S(1)}, u32[]{:S(2)}, u32[]{:S(2)}) async-start(f32[8,2,256]{2,1,0:T(2,128)} %gate_sums.1), calls=%async_computation | async-start | bytes 32768 | tf_op jit(solution)/shard_map/all_to_all | solution.py:567
  6.8 1.2 %copy-start.1 = (bf16[2048,256]{1,0:T(8,128)(2,1)S(1)}, bf16[2048,256]{1,0:T(8,128)(2,1)}, u32[]{:S(2)}) copy-start(bf16[2048,256]{1,0:T(8,128)(2,1)} %k_hbm.5) | copy-start | bytes 3145732
  14.1 11.6 %collective-permute-start = (f32[72,512]{1,0:T(8,128)S(1)}, f32[72,512]{1,0:T(8,128)S(1)}, u32[]{:S(2)}, u32[]{:S(2)}) collective-permute-start(f32[72,512]{1,0:T(8,128)S(1)} %get-tuple-element.35), channel_id=1, source_target_pairs={{0,8},{8,16},{16,24},{24,0},{1,9},{9,17},{17,25},{25,1},{2,10},{10... | collective-permute-start | bytes 442376 | tf_op jit(solution)/shard_map/ppermute | solution.py:573
  15.7 10.0 %collective-permute-start.1 = (f32[72,512]{1,0:T(8,128)S(1)}, f32[72,512]{1,0:T(8,128)S(1)}, u32[]{:S(2)}, u32[]{:S(2)}) collective-permute-start(f32[72,512]{1,0:T(8,128)S(1)} %get-tuple-element.36), channel_id=1, source_target_pairs={{0,16},{8,24},{16,0},{24,8},{1,17},{9,25},{17,1},{25,9},{2,18},{10... | collective-permute-start | bytes 442376 | tf_op jit(solution)/shard_map/ppermute | solution.py:573
  18.5 7.3 %collective-permute-start.2 = (f32[72,512]{1,0:T(8,128)S(1)}, f32[72,512]{1,0:T(8,128)S(1)}, u32[]{:S(2)}, u32[]{:S(2)}) collective-permute-start(f32[72,512]{1,0:T(8,128)S(1)} %get-tuple-element.37), channel_id=1, source_target_pairs={{0,24},{8,0},{16,8},{24,16},{1,25},{9,1},{17,9},{25,17},{2,26},{10... | collective-permute-start | bytes 442376 | tf_op jit(solution)/shard_map/ppermute | solution.py:573
  26.6 16.5 %all-to-all-start.1 = ((f32[8,8,640]{2,1,0:T(8,128)}), f32[8,8,640]{2,1,0:T(8,128)S(1)}, u32[]{:S(2)}, u32[]{:S(2)}) async-start(f32[8,8,640]{2,1,0:T(8,128)} %get-tuple-element.40), calls=%async_computation.1 | async-start | bytes 327680 | tf_op jit(solution)/shard_map/all_to_all | solution.py:567
  43.9 12.4 %all-to-all-start.2 = ((f32[8,8,512]{2,1,0:T(8,128)}), f32[8,8,512]{2,1,0:T(8,128)S(1)}, u32[]{:S(2)}, u32[]{:S(2)}) async-start(f32[8,8,512]{2,1,0:T(8,128)} %get-tuple-element.44), calls=%async_computation.2 | async-start | bytes 262144 | tf_op jit(solution)/shard_map/all_to_all | solution.py:567
  56.4 9.3 %collective-permute-start.3 = (f32[8,8,512]{2,1,0:T(8,128)S(1)}, f32[8,8,512]{2,1,0:T(8,128)S(1)}, u32[]{:S(2)}, u32[]{:S(2)}) collective-permute-start(f32[8,8,512]{2,1,0:T(8,128)S(1)} %get-tuple-element.56), channel_id=1, source_target_pairs={{0,8},{8,16},{16,24},{24,0},{1,9},{9,17},{17,25},{25,1},{2,10},{10... | collective-permute-start | bytes 393224 | tf_op jit(solution)/shard_map/ppermute | solution.py:573
  57.2 8.5 %collective-permute-start.4 = (f32[8,8,512]{2,1,0:T(8,128)S(1)}, f32[8,8,512]{2,1,0:T(8,128)S(1)}, u32[]{:S(2)}, u32[]{:S(2)}) collective-permute-start(f32[8,8,512]{2,1,0:T(8,128)S(1)} %get-tuple-element.57), channel_id=1, source_target_pairs={{0,16},{8,24},{16,0},{24,8},{1,17},{9,25},{17,1},{25,9},{2,18},{10... | collective-permute-start | bytes 393224 | tf_op jit(solution)/shard_map/ppermute | solution.py:573
  59.6 6.1 %collective-permute-start.5 = (f32[8,8,512]{2,1,0:T(8,128)S(1)}, f32[8,8,512]{2,1,0:T(8,128)S(1)}, u32[]{:S(2)}, u32[]{:S(2)}) collective-permute-start(f32[8,8,512]{2,1,0:T(8,128)S(1)} %get-tuple-element.58), channel_id=1, source_target_pairs={{0,24},{8,0},{16,8},{24,16},{1,25},{9,1},{17,9},{25,17},{2,26},{10... | collective-permute-start | bytes 393224 | tf_op jit(solution)/shard_map/ppermute | solution.py:573

commit v2 on v1

v2 whole, which is shorter than its diff:
```python
import functools

import jax
import jax.numpy as jnp
from jax import lax
from jax.experimental import pallas as pl
from jax.experimental.pallas import tpu as pltpu
from jax.sharding import Mesh
from jax.sharding import PartitionSpec as P

DQK = 256
DV = 512
XS = 4
ZS = 8
ROWS = DQK // (XS * ZS)
SLICE = ZS * ROWS
SENT = SLICE + 8
PIECES = 8
PIECE = 256
LANES = 128
WIDE = DV + LANES
TOKS = PIECES * PIECE
QB = 512
BLOCKS = TOKS // QB
PARTS = ((3,), (0, 1), (2,))
CTX = ("ctx_0", "ctx_1")
CTX_HEAD = ("ctx_0", "ctx_1", "head")
NEG = -1e30
F32 = jnp.float32
BF16 = jnp.bfloat16
VMEM = pl.BlockSpec(memory_space=pltpu.VMEM)
HBM = pl.BlockSpec(memory_space=pltpu.HBM)
ANY = pl.BlockSpec(memory_space=pl.ANY)
MIB = 1 << 20


def place_of(axis):
    return lax.axis_index(axis).astype(jnp.int32)


def log_sigmoid(x):
    z = jnp.exp(-jnp.abs(x))
    s = z / (2.0 + z)
    s2 = s * s
    tail = jnp.full_like(s, 1.0 / 17.0)
    for n in (15, 13, 11, 9, 7, 5, 3, 1):
        tail = tail * s2 + 1.0 / n
    return jnp.minimum(x, 0.0) - 2.0 * s * tail


def three_parts(x):
    high = x.astype(BF16)
    rest = x - high.astype(F32)
    mid = rest.astype(BF16)
    low = (rest - mid.astype(F32)).astype(BF16)
    return high, mid, low


def piece_sums(forget):
    n = forget.shape[1]
    upto = lax.broadcasted_iota(jnp.int32, (n, n), 0) <= lax.broadcasted_iota(jnp.int32, (n, n), 1)
    ones = jnp.where(upto, 1.0, 0.0).astype(BF16)
    parts = jnp.concatenate([p.astype(F32) for p in three_parts(log_sigmoid(forget))], axis=0)
    sums = jnp.dot(parts.astype(BF16), ones, preferred_element_type=F32)
    k = forget.shape[0]
    return sums[:k] + sums[k : 2 * k] + sums[2 * k :]


def gate_kernel(g_ref, out_ref):
    cum = piece_sums(g_ref[1])
    own = g_ref[0] - cum
    for h in range(own.shape[0]):
        out_ref[h, 0:1, :] = own[h : h + 1]
        out_ref[h, 1:2, :] = cum[h : h + 1]


def gate_sums(gate_pre):
    kinds, heads, n = gate_pre.shape
    return pl.pallas_call(
        gate_kernel,
        in_specs=[VMEM],
        out_specs=VMEM,
        out_shape=pltpu.VMEM((heads, kinds, n), F32),
        compiler_params=pltpu.CompilerParams(vmem_limit_bytes=8 * MIB),
        name="gate_sums",
    )(gate_pre)


def turned_kernel(k_ref, kt_ref):
    kt_ref[...] = k_ref[...].T


def turned(keys):
    return pl.pallas_call(
        turned_kernel,
        grid=(4,),
        in_specs=[pl.BlockSpec((TOKS // 4, DQK), lambda i: (i, 0))],
        out_specs=pl.BlockSpec((DQK, TOKS // 4), lambda i: (0, i)),
        out_shape=jax.ShapeDtypeStruct((DQK, TOKS), BF16),
        compiler_params=pltpu.CompilerParams(vmem_limit_bytes=8 * MIB),
        cost_estimate=pl.CostEstimate(flops=0, bytes_accessed=4 * MIB, transcendentals=0),
        name="turn_keys",
    )(keys)


def state_kernel(g_ref, kt_ref, v_ref, own_ref, one_ref, two_ref, three_ref, tick_ref, w_ref, acc_ref):
    own = g_ref[:, 0, :]
    cum = g_ref[:, 1, :]
    later = jnp.broadcast_to(cum[:, PIECE - 1 :], cum.shape)
    row = lax.broadcasted_iota(jnp.int32, cum.shape, 0)
    for shift in (1, 2, 4):
        moved = pltpu.roll(later, PIECES - shift, 0)
        later = later + jnp.where(row + shift < PIECES, moved, 0.0)
    reach = own + later
    stab = jnp.max(jnp.max(reach, axis=1, keepdims=True), axis=0, keepdims=True)
    w_ref[...] = jnp.exp(reach - stab) * (DQK**-0.5)
    norm = jnp.zeros((24, DQK), F32)
    for j in range(BLOCKS):
        span = pl.ds(j * QB, QB)
        weight = jnp.concatenate([w_ref[2 * j : 2 * j + 1, :], w_ref[2 * j + 1 : 2 * j + 2, :]], axis=1)
        k = kt_ref[:, span]
        scaled = (k.astype(F32) * weight).astype(BF16)
        parts = [jnp.broadcast_to(p.astype(F32), (8, QB)) for p in three_parts(weight)]
        parts = jnp.concatenate(parts, axis=0).astype(BF16)
        norm += lax.dot_general(parts, k, (((1,), (1,)), ((), ())), preferred_element_type=F32)
        product = jnp.dot(scaled, v_ref[span, :], preferred_element_type=F32)
        if j:
            product += acc_ref[...].reshape(DQK, DV)
        acc_ref[...] = product.reshape(ZS, XS, ROWS, DV)
    norm = norm[0:8] + norm[8:16] + norm[16:24]
    norm = jnp.concatenate([norm, norm], axis=1)
    extra = tail_of(norm[0:1], stab, later[0:1, 0:1])
    x = place_of("ctx_1")
    for k, ref in enumerate((own_ref, one_ref, two_ref, three_ref)):
        to = lax.rem(x + k, XS)
        ref[0:SLICE, :] = acc_ref[:, pl.ds(to, 1)].reshape(SLICE, DV)
        ref[SLICE:, :] = extra
    tick_ref[...] = extra[:, :LANES]


def state(gates, keys_t, values):
    return pl.pallas_call(
        state_kernel,
        in_specs=[VMEM, VMEM, VMEM],
        out_specs=[VMEM] * 5,
        out_shape=[jax.ShapeDtypeStruct((SENT, DV), F32)] * 4 + [jax.ShapeDtypeStruct((8, LANES), F32)],
        scratch_shapes=[
            pltpu.VMEM((PIECES, PIECE), F32),
            pltpu.VMEM((ZS, XS, ROWS, DV), F32),
        ],
        compiler_params=pltpu.CompilerParams(vmem_limit_bytes=12 * MIB),
        cost_estimate=pl.CostEstimate(flops=600_000_000, bytes_accessed=5 * MIB, transcendentals=0),
        name="shard_state",
    )(gates, keys_t, values)


def tail_of(norm, stab, total):
    row = lax.broadcasted_iota(jnp.int32, (8, DV), 0)
    return jnp.where(row == 0, norm, jnp.where(row == 1, stab, total))


def pieces_of(tail):
    return tail[0:1, :], tail[1:2, :], tail[2:3, :]


def chain_of(early, late):
    norm_e, stab_e, total_e = early
    norm_l, stab_l, total_l = late
    shifted = stab_e + total_l
    stab = jnp.maximum(shifted, stab_l)
    keep, take = jnp.exp(shifted - stab), jnp.exp(stab_l - stab)
    return keep, take, (keep * norm_e + take * norm_l, stab, total_e + total_l)


def group_kernel(own_ref, one_ref, two_ref, three_ref, after_ref, out_ref, all_ref):
    x = place_of("ctx_1")
    for k, ref in enumerate((own_ref, one_ref, two_ref, three_ref)):
        at = lax.rem(x + XS - k, XS)
        all_ref[pl.ds(at, 1)] = ref[...].reshape(1, SENT, DV)
    small = pieces_of(all_ref[0, SLICE:, :])
    factors = []
    for j in range(1, XS):
        keep, take, small = chain_of(small, pieces_of(all_ref[j, SLICE:, :]))
        factors.append((keep, take))
    for at in range(0, SLICE, ROWS):
        memory = all_ref[0, at : at + ROWS, :]
        for j, (keep, take) in enumerate(factors):
            memory = keep * memory + take * all_ref[j + 1, at : at + ROWS, :]
        out_ref[at : at + ROWS, :] = memory
    out_ref[SLICE:, :] = tail_of(*small)


def grouped(parts, after):
    return pl.pallas_call(
        group_kernel,
        in_specs=[VMEM] * 4 + [ANY],
        out_specs=[VMEM] * 2,
        out_shape=[
            jax.ShapeDtypeStruct((SENT, DV), F32),
            jax.ShapeDtypeStruct((XS, SENT, DV), F32),
        ],
        compiler_params=pltpu.CompilerParams(vmem_limit_bytes=4 * MIB),
        cost_estimate=pl.CostEstimate(flops=1_000_000, bytes_accessed=2 * MIB, transcendentals=0),
        name="group_states",
    )(*parts, after)


def merge(later, total_ref, got_ref, prefix_ref, new_total, new_prefix):
    own, got = pieces_of(total_ref[SLICE:, :]), pieces_of(got_ref[SLICE:, :])
    first = [jnp.where(later, g, o) for g, o in zip(got, own)]
    second = [jnp.where(later, o, g) for g, o in zip(got, own)]
    keep, take, small = chain_of(first, second)
    f_own, f_got = jnp.where(later, take, keep), jnp.where(later, keep, take)
    for at in range(0, SLICE, ROWS):
        here = slice(at, at + ROWS)
        new_total[here, :] = f_own * total_ref[here, :] + f_got * got_ref[here, :]
    new_total[SLICE:, :] = tail_of(*small)
    if prefix_ref is None:
        before = (jnp.zeros((1, DV), F32), jnp.full((1, DV), NEG, F32), jnp.zeros((1, DV), F32))
    else:
        before = pieces_of(prefix_ref[SLICE:, :])
    bring, hold, small = chain_of(got, before)
    bring, hold = jnp.where(later, bring, 0.0), jnp.where(later, hold, 1.0)
    for at in range(0, SLICE, ROWS):
        here = slice(at, at + ROWS)
        memory = bring * got_ref[here, :]
        if prefix_ref is not None:
            memory = memory + hold * prefix_ref[here, :]
        new_prefix[here, :] = memory
    new_prefix[SLICE:, :] = tail_of(*[jnp.where(later, n, o) for n, o in zip(small, before)])


def later_of(z, bit):
    return lax.rem(lax.div(z, 1 << bit), 2) == 1


def first_round_kernel(total_ref, got_ref, after_ref, new_total, new_prefix):
    merge(later_of(place_of("ctx_0"), 0), total_ref, got_ref, None, new_total, new_prefix)


def next_round_kernel(total_ref, got_ref, prefix_ref, after_ref, new_total, new_prefix):
    merge(later_of(place_of("ctx_0"), 1), total_ref, got_ref, prefix_ref, new_total, new_prefix)


def round_of(kernel, *args):
    return pl.pallas_call(
        kernel,
        in_specs=[VMEM] * (len(args) - 1) + [ANY],
        out_specs=[VMEM] * 2,
        out_shape=[jax.ShapeDtypeStruct((SENT, DV), F32)] * 2,
        compiler_params=pltpu.CompilerParams(vmem_limit_bytes=4 * MIB),
        cost_estimate=pl.CostEstimate(flops=1_000_000, bytes_accessed=MIB, transcendentals=0),
        name="merge_round",
    )(*args)


def spread_kernel(total_ref, got_ref, prefix_ref, all_ref, after_ref, own_ref, one_ref, two_ref, three_ref, mine_ref, close_ref, norm_ref, top_ref, sum_ref, before_ref, out_ref):
    x, z = place_of("ctx_1"), place_of("ctx_0")
    merge(later_of(z, 2), total_ref, got_ref, prefix_ref, sum_ref, before_ref)
    close_ref[0] = sum_ref[pl.ds(pl.multiple_of(z * ROWS, ROWS), ROWS), :]
    norm, top, _ = pieces_of(sum_ref[SLICE:, :])
    norm_ref[...] = norm[:, :DQK]
    top_ref[...] = top[:, :LANES]
    small = pieces_of(before_ref[SLICE:, :])
    mine = small
    factors = []
    for j in range(XS - 1):
        keep, take, small = chain_of(small, pieces_of(all_ref[j, SLICE:, :]))
        mine = [jnp.where(x == j + 1, n, o) for n, o in zip(small, mine)]
        factors.append((keep, take))
    for at in range(0, SLICE, ROWS):
        memory = before_ref[at : at + ROWS, :]
        out_ref[0, at : at + ROWS, :] = memory
        for j, (keep, take) in enumerate(factors):
            memory = keep * memory + take * all_ref[j, at : at + ROWS, :]
            out_ref[j + 1, at : at + ROWS, :] = memory
    for k, ref in enumerate((own_ref, one_ref, two_ref, three_ref)):
        ref[...] = out_ref[pl.ds(lax.rem(x + k, XS), 1)].reshape(ZS, ROWS, DV)
    mine_ref[...] = tail_of(*mine)


def spread(total, got, prefix, everything, after):
    return pl.pallas_call(
        spread_kernel,
        in_specs=[VMEM] * 4 + [ANY],
        out_specs=[VMEM] * 8,
        out_shape=[jax.ShapeDtypeStruct((ZS, ROWS, DV), F32)] * 4
        + [
            jax.ShapeDtypeStruct((8, DV), F32),
            jax.ShapeDtypeStruct((1, ROWS, DV), F32),
            jax.ShapeDtypeStruct((1, DQK), F32),
            jax.ShapeDtypeStruct((1, LANES), F32),
        ],
        scratch_shapes=[
            pltpu.VMEM((SENT, DV), F32),
            pltpu.VMEM((SENT, DV), F32),
            pltpu.VMEM((XS, SLICE, DV), F32),
        ],
        compiler_params=pltpu.CompilerParams(vmem_limit_bytes=4 * MIB),
        cost_estimate=pl.CostEstimate(flops=1_000_000, bytes_accessed=2 * MIB, transcendentals=0),
        name="spread_prefixes",
    )(total, got, prefix, everything, after)


def wide(x, n):
    return jnp.concatenate([x] * (n // LANES), axis=1)


def column(row):
    n = row.shape[1]
    return jnp.concatenate(
        [
            jnp.broadcast_to(row[:, at : at + LANES], (LANES, LANES)).T
            for at in range(0, n, LANES)
        ],
        axis=0,
    )


def tables(g_ref, table_ref):
    own, cum = [], []
    for r in range(0, PIECES, 2):
        first = g_ref[r, 1:2, :][:, PIECE - 1 :]
        own.append(jnp.concatenate([g_ref[r, 0:1, :], g_ref[r + 1, 0:1, :] - first], axis=1))
        cum.append(jnp.concatenate([g_ref[r, 1:2, :], g_ref[r + 1, 1:2, :] + first], axis=1))
    own = jnp.concatenate(own, axis=0)
    cum = jnp.concatenate(cum, axis=0)
    table_ref[0:BLOCKS, :] = own
    table_ref[BLOCKS : 2 * BLOCKS, :] = cum
    lane = lax.broadcasted_iota(jnp.int32, (BLOCKS, QB), 1)
    top = own
    shift = 1
    while shift < QB:
        moved = pltpu.roll(top, shift, 1)
        top = jnp.maximum(top, jnp.where(lane >= shift, moved, NEG))
        shift *= 2
    stab = jnp.full((1, 1), NEG, F32)
    for r in range(BLOCKS):
        at = 2 * BLOCKS + r
        table_ref[at : at + 1, :] = jnp.maximum(top[r : r + 1], stab)
        stab = jnp.maximum(stab, top[r : r + 1, QB - 1 :]) + cum[r : r + 1, QB - 1 :]


def local_kernel(blocks, table_ref, tick_ref, q_ref, k_ref, v_ref, num_ref, den_ref):
    for n, i in enumerate(blocks):
        here = pl.ds(n * QB, QB)
        top = column(table_ref[2 * BLOCKS + i : 2 * BLOCKS + i + 1, :])
        q = q_ref[pl.ds(i * QB, QB), :]

        def scores(j):
            at = pl.ds(pl.multiple_of(j * QB, QB), QB)
            return lax.dot_general(q, k_ref[at, :], (((1,), (1,)), ((), ())), preferred_element_type=F32)

        def sums(j, mixed):
            at = pl.ds(pl.multiple_of(j * QB, QB), QB)
            lanes = sum(mixed[:, c : c + LANES] for c in range(0, QB, LANES))
            return lanes, jnp.dot(mixed.astype(BF16), v_ref[at, :], preferred_element_type=F32)

        past = lax.broadcasted_iota(jnp.int32, (QB, QB), 0) >= lax.broadcasted_iota(jnp.int32, (QB, QB), 1)
        power = jnp.where(past, table_ref[i : i + 1, :] - wide(top, QB), NEG)
        den_ref[here, :], num_ref[here, :] = sums(i, jnp.exp(power) * scores(i))

        def earlier(m, shift):
            j = i - 1 - m
            shift = shift + table_ref[pl.ds(BLOCKS + j, 1), :][:, QB - 1 :]
            reach = table_ref[pl.ds(j, 1), :]
            peak = jnp.max(reach, axis=1, keepdims=True)
            lanes, product = sums(j, scores(j) * jnp.exp(reach - peak))
            factor = jnp.exp((peak + shift) - top)
            den_ref[here, :] += factor * lanes
            num_ref[here, :] += wide(factor, DV) * product
            return shift

        if i:
            lax.fori_loop(0, i, earlier, jnp.zeros((1, 1), F32))


def first_kernel(blocks, g_ref, tick_ref, q_ref, k_ref, v_ref, num_ref, den_ref, table_ref):
    tables(g_ref, table_ref)
    local_kernel(blocks, table_ref, tick_ref, q_ref, k_ref, v_ref, num_ref, den_ref)


def local(blocks, gates, tick, queries, keys, values, table=None):
    count = len(blocks)
    units = sum(blocks) + count
    first = table is None
    out_shape = [
        jax.ShapeDtypeStruct((count * QB, DV), F32),
        jax.ShapeDtypeStruct((count * QB, LANES), F32),
        jax.ShapeDtypeStruct((3 * BLOCKS, QB), F32),
    ][: 3 if first else 2]
    return pl.pallas_call(
        functools.partial(first_kernel if first else local_kernel, blocks),
        in_specs=[VMEM, ANY] + [VMEM] * 3,
        out_specs=[VMEM] * len(out_shape),
        out_shape=out_shape,
        compiler_params=pltpu.CompilerParams(vmem_limit_bytes=8 * MIB),
        cost_estimate=pl.CostEstimate(flops=800_000_000 * units, bytes_accessed=MIB * units, transcendentals=0),
        name="within_shard",
    )(gates if first else table, tick, queries, keys, values)


def scale_kernel(table_ref, mine_ref, q_ref, *refs):
    dens, (kept_ref, carried_ref) = refs[:-2], refs[-2:]
    norm, log_in, _ = pieces_of(mine_ref)
    norm, log_in = norm[:, :DQK], log_in[:, :LANES]
    place = {i: (dens[n], m) for n, blocks in enumerate(PARTS) for m, i in enumerate(blocks)}
    for i in range(BLOCKS):
        den_ref, m = place[i]
        here, there = pl.ds(i * QB, QB), pl.ds(m * QB, QB)
        top = column(table_ref[2 * BLOCKS + i : 2 * BLOCKS + i + 1, :])
        peak = jnp.maximum(top, log_in)
        kept, carried = jnp.exp(top - peak) * (DQK**-0.5), jnp.exp(log_in - peak)
        from_norm = jnp.sum(q_ref[here, :].astype(F32) * norm, axis=1, keepdims=True)
        denom = jnp.sum(den_ref[there, :], axis=1, keepdims=True) * kept + carried * from_norm
        inverse = 1.0 / jnp.maximum(jnp.abs(denom), 1.0)
        kept_ref[here, :] = kept * inverse
        carried_ref[here, :] = carried * inverse
        log_in = log_in + table_ref[BLOCKS + i : BLOCKS + i + 1, :][:, QB - 1 :]


def scales(table, mine, queries, dens):
    return pl.pallas_call(
        scale_kernel,
        in_specs=[VMEM] * (3 + len(dens)),
        out_specs=[VMEM] * 2,
        out_shape=[jax.ShapeDtypeStruct((TOKS, LANES), F32)] * 2,
        compiler_params=pltpu.CompilerParams(vmem_limit_bytes=4 * MIB),
        cost_estimate=pl.CostEstimate(flops=600_000_000, bytes_accessed=4 * MIB, transcendentals=0),
        name="row_scales",
    )(table, mine, queries, *dens)


def joined_kernel(q_ref, own_ref, one_ref, two_ref, three_ref, kept_ref, carried_ref, *refs):
    nums, (out_hbm, mem_ref, mem_b_ref, out_ref, sem) = refs[:-5], refs[-5:]
    x = place_of("ctx_1")
    for k, ref in enumerate((own_ref, one_ref, two_ref, three_ref)):
        at = lax.rem(x + XS - k, XS)
        mem_ref[:, pl.ds(at, 1)] = ref[...].reshape(ZS, 1, ROWS, DV)
    mem_b_ref[...] = mem_ref[...].reshape(DQK, DV).astype(BF16)
    copies = []
    for n, blocks in enumerate(PARTS):
        for m, i in enumerate(blocks):
            for half in range(0, QB, PIECE):
                span, there = pl.ds(i * QB + half, PIECE), pl.ds(m * QB + half, PIECE)
                product = jnp.dot(q_ref[span, :], mem_b_ref[...], preferred_element_type=F32)
                local_part = wide(kept_ref[span, :], DV) * nums[n][there, :]
                out_ref[span, :] = (local_part + wide(carried_ref[span, :], DV) * product).astype(BF16)
                copies.append(pltpu.make_async_copy(out_ref.at[span], out_hbm.at[span], sem.at[len(copies)]))
                copies[-1].start()
    for copy in copies:
        copy.wait()


def joined(queries, parts, kept, carried, nums):
    return pl.pallas_call(
        joined_kernel,
        in_specs=[VMEM] * (7 + len(nums)),
        out_specs=HBM,
        out_shape=jax.ShapeDtypeStruct((TOKS, DV), BF16),
        scratch_shapes=[
            pltpu.VMEM((ZS, XS, ROWS, DV), F32),
            pltpu.VMEM((DQK, DV), BF16),
            pltpu.VMEM((TOKS, DV), BF16),
            pltpu.SemaphoreType.DMA((PIECES,)),
        ],
        compiler_params=pltpu.CompilerParams(vmem_limit_bytes=8 * MIB),
        cost_estimate=pl.CostEstimate(flops=600_000_000, bytes_accessed=9 * MIB, transcendentals=0),
        name="join_memory",
    )(queries, *parts, kept, carried, *nums)


def exchanged(x, axis):
    return lax.all_to_all(x, axis, split_axis=0, concat_axis=0, tiled=True)


def around(parts):
    moved = [parts[0]]
    for k in range(1, XS):
        moved.append(lax.ppermute(parts[k], "ctx_1", [(i, (i + k) % XS) for i in range(XS)]))
    return moved


def swapped(x, partner):
    return lax.ppermute(x, "ctx_0", [(i, partner(i)) for i in range(ZS)])


def on_device(queries, keys, values, gate_pre):
    gates = exchanged(gate_sums(gate_pre), "head")
    keys_t = turned(keys)
    *parts, tick = state(gates, keys_t, values)
    moved = around(parts)
    qkv = (queries, keys, values)
    num_a, den_a, table = local(PARTS[0], gates, tick, *qkv)
    total, everything = grouped(moved, den_a)
    got = swapped(total, lambda i: i ^ 1)
    total, prefix = round_of(first_round_kernel, total, got, den_a)
    got = swapped(total, lambda i: i ^ 2)
    num_b, den_b = local(PARTS[1], None, prefix, *qkv, table)
    total, prefix = round_of(next_round_kernel, total, got, prefix, den_b)
    got = swapped(total, lambda i: ZS - 1 - i)
    num_c, den_c = local(PARTS[2], None, prefix, *qkv, table)
    *parts, mine, closing, final_norm, top = spread(total, got, prefix, everything, den_c)
    moved = around(parts)
    kept, carried = scales(table, mine, queries, [den_a, den_b, den_c])
    hidden = joined(queries, moved, kept, carried, [num_a, num_b, num_c])
    return (hidden, closing, final_norm, top[0, :1])


def solution(mesh):
    split = Mesh(mesh.devices.reshape(8, 4, mesh.shape["head"]), ("ctx_0", "ctx_1", "head"))
    in_specs = (P(CTX, "head"), P(CTX, "head"), P(CTX, "head"), P(None, None, CTX_HEAD))
    out_specs = (P(CTX, "head"), P("head", CTX, None), P("head", None), P("head"))
    return jax.shard_map(
        on_device, mesh=split, in_specs=in_specs, out_specs=out_specs, check_vma=False
    )
```

time: 68.6 us -> 61.8 us (0.901)
  the two profiles are of different devices: /device:TPU:32 before, /device:TPU:1 now
where the time goes in v2:
time: 61.8 us; the launch traced here: 61.6 us
  starting transfers between devices  29.3 us (47%)
  waiting for transfers between devices  16.7 us (27%)
  Pallas kernels  12.7 us (21%)
  local copies, waits for them, and re-layouts  2.09 us (3%)
  between operations  0.73 us (1%)
    ppermute x6, starting transfers between devices, around(): lax.ppermute(parts[k], 'ctx_1', [(i, (i + k) % XS) for i in range(XS)])  13.8 us
    ppermute x3, starting transfers between devices, swapped(): return lax.ppermute(x, 'ctx_0', [(i, partner(i)) for i in range(ZS)])  9.06 us
    ppermute x3, waiting for transfers between devices, swapped(): return lax.ppermute(x, 'ctx_0', [(i, partner(i)) for i in range(ZS)])  7.47 us
    all_to_all x1, starting transfers between devices, exchanged(): return lax.all_to_all(x, axis, split_axis=0, concat_axis=0, tiled=True)  6.44 us
    ppermute x6, waiting for transfers between devices, around(): lax.ppermute(parts[k], 'ctx_1', [(i, (i + k) % XS) for i in range(XS)])  6.4 us
    pallas_call x3, Pallas kernels, local(): pl.pallas_call(functools.partial(first_kernel if first else local_kernel,...  6.38 us
    all_to_all x1, waiting for transfers between devices, exchanged(): return lax.all_to_all(x, axis, split_axis=0, concat_axis=0, tiled=True)  2.84 us
    unnamed x10, local copies, waits for them, and re-layouts  2.09 us
  transfers between devices with their start and end apart: 10, of which 7 were waited for; matrix products, arithmetic and copies ran while one was open for 0% of the time, Pallas kernels for 13%

profile of v2, /device:TPU:1, one launch (start us, length us, event | category | flops | bytes accessed | tf_op | source)
XLA Modules:
  0.0 61.6 jit_solution(3056943017342579496)
XLA Ops:
  0.7 0.9 %copy-done.4 = f32[2,8,256]{2,1,0:T(8,128)S(1)} copy-done((f32[2,8,256]{2,1,0:T(8,128)S(1)}, f32[2,8,256]{2,1,0:T(8,128)}, u32[]{:S(2)}) %copy-start.4) | copy-done | bytes 16408
  1.5 0.8 %gate_sums.1 = f32[8,2,256]{2,1,0:T(2,128)} custom-call(f32[2,8,256]{2,1,0:T(8,128)S(1)} %copy-done.4), custom_call_target="tpu_custom_call" | custom-call | tf_op jit(solution)/shard_map/gate_sums/pallas_call | solution.py:79
  2.3 6.4 %all-to-all-start = ((f32[8,2,256]{2,1,0:T(2,128)}), f32[8,2,256]{2,1,0:T(2,128)S(1)}, u32[]{:S(2)}, u32[]{:S(2)}) async-start(f32[8,2,256]{2,1,0:T(2,128)} %gate_sums.1), calls=%async_computation | async-start | bytes 32768 | tf_op jit(solution)/shard_map/all_to_all | solution.py:474
  8.7 1.2 %copy-done.2 = bf16[2048,256]{1,0:T(8,128)(2,1)S(1)} copy-done((bf16[2048,256]{1,0:T(8,128)(2,1)S(1)}, bf16[2048,256]{1,0:T(8,128)(2,1)}, u32[]{:S(2)}) %copy-start.2) | copy-done | bytes 1048600
  10.6 2.8 %all-to-all-done.g_ref = f32[8,2,256]{2,1,0:T(2,128)S(1)} async-done(((f32[8,2,256]{2,1,0:T(2,128)}), f32[8,2,256]{2,1,0:T(2,128)S(1)}, u32[]{:S(2)}, u32[]{:S(2)}) %all-to-all-start) | async-done | bytes 16416 | tf_op jit(solution)/shard_map/all_to_all | solution.py:474
  13.4 1.2 %shard_state.1 = (f32[72,512]{1,0:T(8,128)S(1)}, f32[72,512]{1,0:T(8,128)S(1)}, f32[72,512]{1,0:T(8,128)S(1)}, f32[72,512]{1,0:T(8,128)S(1)}, f32[8,128]{1,0:T(8,128)S(1)}) custom-call(f32[8,2,256]{2,1,0:T(2,128)S(1)} %all-to-all-done.g_ref, bf16[256,2048]{1,0:T(8,128)(2,1)S(1)} %turn_keys.1.kt_ref, bf16[2048,512]{1,0:T(8,128)(2,1)S(1)} %copy-done), custom_call_target="tpu_custom_call" | custom-call | flops 600000000 | bytes 5242880 | tf_op jit(solution)/shard_map/shard_state/pallas_call | solution.py:142
  14.6 0.8 %collective-permute-start = (f32[72,512]{1,0:T(8,128)S(1)}, f32[72,512]{1,0:T(8,128)S(1)}, u32[]{:S(2)}, u32[]{:S(2)}) collective-permute-start(f32[72,512]{1,0:T(8,128)S(1)} %get-tuple-element.33), channel_id=1, source_target_pairs={{0,8},{8,16},{16,24},{24,0},{1,9},{9,17},{17,25},{25,1},{2,10},{10... | collective-permute-start | bytes 442376 | tf_op jit(solution)/shard_map/ppermute | solution.py:480
  15.4 2.5 %collective-permute-start.1 = (f32[72,512]{1,0:T(8,128)S(1)}, f32[72,512]{1,0:T(8,128)S(1)}, u32[]{:S(2)}, u32[]{:S(2)}) collective-permute-start(f32[72,512]{1,0:T(8,128)S(1)} %get-tuple-element.34), channel_id=1, source_target_pairs={{0,16},{8,24},{16,0},{24,8},{1,17},{9,25},{17,1},{25,9},{2,18},{10... | collective-permute-start | bytes 442376 | tf_op jit(solution)/shard_map/ppermute | solution.py:480
  17.9 1.1 %collective-permute-start.2 = (f32[72,512]{1,0:T(8,128)S(1)}, f32[72,512]{1,0:T(8,128)S(1)}, u32[]{:S(2)}, u32[]{:S(2)}) collective-permute-start(f32[72,512]{1,0:T(8,128)S(1)} %get-tuple-element.35), channel_id=1, source_target_pairs={{0,24},{8,0},{16,8},{24,16},{1,25},{9,1},{17,9},{25,17},{2,26},{10... | collective-permute-start | bytes 442376 | tf_op jit(solution)/shard_map/ppermute | solution.py:480
  19.0 3.1 %within_shard.3 = (f32[512,512]{1,0:T(8,128)S(1)}, f32[512,128]{1,0:T(8,128)S(1)}, f32[12,512]{1,0:T(8,128)S(1)}) custom-call(f32[8,2,256]{2,1,0:T(2,128)S(1)} %all-to-all-done.g_ref, f32[8,128]{1,0:T(8,128)S(1)} %get-tuple-element.36.tick_ref, bf16[2048,256]{1,0:T(8,128)(2,1)S(1)} %copy-done.1, bf16[2048,256]{1,0:T(8,128)(2,1)S(1)} %copy-done.3, ...), custom_call_target="tpu_custom_call" | custom-call | flops 3200000000 | bytes 4194304 | tf_op jit(solution)/shard_map/within_shard/pallas_call | solution.py:392
  22.1 2.1 %collective-permute-done.1.two_ref = f32[72,512]{1,0:T(8,128)S(1)} collective-permute-done((f32[72,512]{1,0:T(8,128)S(1)}, f32[72,512]{1,0:T(8,128)S(1)}, u32[]{:S(2)}, u32[]{:S(2)}) %collective-permute-start.1) | collective-permute-done | bytes 147488 | tf_op jit(solution)/shard_map/ppermute | solution.py:480
  24.4 1.7 %collective-permute-start.3 = (f32[72,512]{1,0:T(8,128)S(1)}, f32[72,512]{1,0:T(8,128)S(1)}, u32[]{:S(2)}, u32[]{:S(2)}) collective-permute-start(f32[72,512]{1,0:T(8,128)S(1)} %get-tuple-element.38.total_ref), channel_id=1, source_target_pairs={{0,32},{32,0},{64,96},{96,64},{128,160},{160,128},{192,224},{224,1... | collective-permute-start | bytes 442376 | tf_op jit(solution)/shard_map/ppermute | solution.py:485
  26.1 2.5 %collective-permute-done.3.got_ref = f32[72,512]{1,0:T(8,128)S(1)} collective-permute-done((f32[72,512]{1,0:T(8,128)S(1)}, f32[72,512]{1,0:T(8,128)S(1)}, u32[]{:S(2)}, u32[]{:S(2)}) %collective-permute-start.3) | collective-permute-done | bytes 147488 | tf_op jit(solution)/shard_map/ppermute | solution.py:485
  28.7 3.1 %collective-permute-start.4 = (f32[72,512]{1,0:T(8,128)S(1)}, f32[72,512]{1,0:T(8,128)S(1)}, u32[]{:S(2)}, u32[]{:S(2)}) collective-permute-start(f32[72,512]{1,0:T(8,128)S(1)} %get-tuple-element.39.total_ref), channel_id=1, source_target_pairs={{0,64},{32,96},{64,0},{96,32},{128,192},{160,224},{192,128},{224,1... | collective-permute-start | bytes 442376 | tf_op jit(solution)/shard_map/ppermute | solution.py:485
  31.8 1.4 %within_shard.4 = (f32[1024,512]{1,0:T(8,128)S(1)}, f32[1024,128]{1,0:T(8,128)S(1)}) custom-call(f32[12,512]{1,0:T(8,128)S(1)} %get-tuple-element.41.table_ref, f32[72,512]{1,0:T(8,128)S(1)} %get-tuple-element.40.tick_ref.prefix_ref, bf16[2048,256]{1,0:T(8,128)(2,1)S(1)} %copy-done.1, bf16[2048,256]{1,0:T(8,128)(2,1)S(1)} %copy-done.3, ...), custom_call_target="tpu_custom_call" | custom-call | flops 2400000000 | bytes 3145728 | tf_op jit(solution)/shard_map/within_shard/pallas_call | solution.py:392
  33.2 3.3 %collective-permute-done.4.got_ref = f32[72,512]{1,0:T(8,128)S(1)} collective-permute-done((f32[72,512]{1,0:T(8,128)S(1)}, f32[72,512]{1,0:T(8,128)S(1)}, u32[]{:S(2)}, u32[]{:S(2)}) %collective-permute-start.4) | collective-permute-done | bytes 147488 | tf_op jit(solution)/shard_map/ppermute | solution.py:485
  36.6 4.3 %collective-permute-start.5 = (f32[72,512]{1,0:T(8,128)S(1)}, f32[72,512]{1,0:T(8,128)S(1)}, u32[]{:S(2)}, u32[]{:S(2)}) collective-permute-start(f32[72,512]{1,0:T(8,128)S(1)} %get-tuple-element.43.total_ref), channel_id=1, source_target_pairs={{0,224},{32,192},{64,160},{96,128},{128,96},{160,64},{192,32},{224... | collective-permute-start | bytes 442376 | tf_op jit(solution)/shard_map/ppermute | solution.py:485
  40.8 1.8 %within_shard.5 = (f32[512,512]{1,0:T(8,128)S(1)}, f32[512,128]{1,0:T(8,128)S(1)}) custom-call(f32[12,512]{1,0:T(8,128)S(1)} %get-tuple-element.41.table_ref, f32[72,512]{1,0:T(8,128)S(1)} %get-tuple-element.44.tick_ref.prefix_ref, bf16[2048,256]{1,0:T(8,128)(2,1)S(1)} %copy-done.1, bf16[2048,256]{1,0:T(8,128)(2,1)S(1)} %copy-done.3, ...), custom_call_target="tpu_custom_call" | custom-call | flops 2400000000 | bytes 3145728 | tf_op jit(solution)/shard_map/within_shard/pallas_call | solution.py:392
  42.7 1.7 %collective-permute-done.5.got_ref = f32[72,512]{1,0:T(8,128)S(1)} collective-permute-done((f32[72,512]{1,0:T(8,128)S(1)}, f32[72,512]{1,0:T(8,128)S(1)}, u32[]{:S(2)}, u32[]{:S(2)}) %collective-permute-start.5) | collective-permute-done | bytes 147488 | tf_op jit(solution)/shard_map/ppermute | solution.py:485
  45.0 7.0 %collective-permute-start.6 = (f32[8,8,512]{2,1,0:T(8,128)S(1)}, f32[8,8,512]{2,1,0:T(8,128)S(1)}, u32[]{:S(2)}, u32[]{:S(2)}) collective-permute-start(f32[8,8,512]{2,1,0:T(8,128)S(1)} %get-tuple-element.48), channel_id=1, source_target_pairs={{0,8},{8,16},{16,24},{24,0},{1,9},{9,17},{17,25},{25,1},{2,10},{10... | collective-permute-start | bytes 393224 | tf_op jit(solution)/shard_map/ppermute | solution.py:480
  52.0 2.0 %collective-permute-start.7 = (f32[8,8,512]{2,1,0:T(8,128)S(1)}, f32[8,8,512]{2,1,0:T(8,128)S(1)}, u32[]{:S(2)}, u32[]{:S(2)}) collective-permute-start(f32[8,8,512]{2,1,0:T(8,128)S(1)} %get-tuple-element.49), channel_id=1, source_target_pairs={{0,16},{8,24},{16,0},{24,8},{1,17},{9,25},{17,1},{25,9},{2,18},{10... | collective-permute-start | bytes 393224 | tf_op jit(solution)/shard_map/ppermute | solution.py:480
  54.4 1.2 %row_scales.1 = (f32[2048,128]{1,0:T(8,128)S(1)}, f32[2048,128]{1,0:T(8,128)S(1)}) custom-call(f32[12,512]{1,0:T(8,128)S(1)} %get-tuple-element.41.table_ref, f32[8,512]{1,0:T(8,128)S(1)} %get-tuple-element.51.mine_ref, bf16[2048,256]{1,0:T(8,128)(2,1)S(1)} %copy-done.1, f32[512,128]{1,0:T(8,128)S(1)} %get-tuple-element.37.after_ref.refs_0_, ...), custom_call_target="tpu_custom_call" | custom-call | flops 600000000 | bytes 4194304 | tf_op jit(solution)/shard_map/row_scales/pallas_call | solution.py:423
  56.2 3.7 %collective-permute-done.7.two_ref = f32[8,8,512]{2,1,0:T(8,128)S(1)} collective-permute-done((f32[8,8,512]{2,1,0:T(8,128)S(1)}, f32[8,8,512]{2,1,0:T(8,128)S(1)}, u32[]{:S(2)}, u32[]{:S(2)}) %collective-permute-start.7) | collective-permute-done | bytes 131104 | tf_op jit(solution)/shard_map/ppermute | solution.py:480
  59.9 1.7 %join_memory.1 = bf16[2048,512]{1,0:T(8,128)(2,1)} custom-call(bf16[2048,256]{1,0:T(8,128)(2,1)S(1)} %copy-done.1, f32[8,8,512]{2,1,0:T(8,128)S(1)} %get-tuple-element.47.own_ref, f32[8,8,512]{2,1,0:T(8,128)S(1)} %collective-permute-done.6.one_ref, f32[8,8,512]{2,1,0:T(8,128)S(1)} %collective-permute-done.7.two_ref, ...), custom_call_target="tpu_custom_call" | custom-call | flops 600000000 | bytes 9437184 | tf_op jit(solution)/shard_map/join_memory/pallas_call | solution.py:456
  (18 shorter events, 2.4 us)
Async XLA Ops:
  0.6 12.8 %copy-start = (bf16[2048,512]{1,0:T(8,128)(2,1)S(1)}, bf16[2048,512]{1,0:T(8,128)(2,1)}, u32[]{:S(2)}) copy-start(bf16[2048,512]{1,0:T(8,128)(2,1)} %v_ref.7) | copy-start | bytes 6291460
  0.6 0.9 %copy-start.4 = (f32[2,8,256]{2,1,0:T(8,128)S(1)}, f32[2,8,256]{2,1,0:T(8,128)}, u32[]{:S(2)}) copy-start(f32[2,8,256]{2,1,0:T(8,128)} %g_ref.1) | copy-start | bytes 49156
  2.3 11.1 %all-to-all-start = ((f32[8,2,256]{2,1,0:T(2,128)}), f32[8,2,256]{2,1,0:T(2,128)S(1)}, u32[]{:S(2)}, u32[]{:S(2)}) async-start(f32[8,2,256]{2,1,0:T(2,128)} %gate_sums.1), calls=%async_computation | async-start | bytes 32768 | tf_op jit(solution)/shard_map/all_to_all | solution.py:474
  8.7 1.2 %copy-start.2 = (bf16[2048,256]{1,0:T(8,128)(2,1)S(1)}, bf16[2048,256]{1,0:T(8,128)(2,1)}, u32[]{:S(2)}) copy-start(bf16[2048,256]{1,0:T(8,128)(2,1)} %k_ref.7) | copy-start | bytes 3145732
  13.4 5.6 %copy-start.1 = (bf16[2048,256]{1,0:T(8,128)(2,1)S(1)}, bf16[2048,256]{1,0:T(8,128)(2,1)}, u32[]{:S(2)}) copy-start(bf16[2048,256]{1,0:T(8,128)(2,1)} %q_ref.9) | copy-start | bytes 3145732
  13.4 5.6 %copy-start.3 = (bf16[2048,256]{1,0:T(8,128)(2,1)S(1)}, bf16[2048,256]{1,0:T(8,128)(2,1)}, u32[]{:S(2)}) copy-start(bf16[2048,256]{1,0:T(8,128)(2,1)} %k_ref.7) | copy-start | bytes 3145732
  14.6 7.5 %collective-permute-start = (f32[72,512]{1,0:T(8,128)S(1)}, f32[72,512]{1,0:T(8,128)S(1)}, u32[]{:S(2)}, u32[]{:S(2)}) collective-permute-start(f32[72,512]{1,0:T(8,128)S(1)} %get-tuple-element.33), channel_id=1, source_target_pairs={{0,8},{8,16},{16,24},{24,0},{1,9},{9,17},{17,25},{25,1},{2,10},{10... | collective-permute-start | bytes 442376 | tf_op jit(solution)/shard_map/ppermute | solution.py:480
  15.4 8.8 %collective-permute-start.1 = (f32[72,512]{1,0:T(8,128)S(1)}, f32[72,512]{1,0:T(8,128)S(1)}, u32[]{:S(2)}, u32[]{:S(2)}) collective-permute-start(f32[72,512]{1,0:T(8,128)S(1)} %get-tuple-element.34), channel_id=1, source_target_pairs={{0,16},{8,24},{16,0},{24,8},{1,17},{9,25},{17,1},{25,9},{2,18},{10... | collective-permute-start | bytes 442376 | tf_op jit(solution)/shard_map/ppermute | solution.py:480
  17.9 6.4 %collective-permute-start.2 = (f32[72,512]{1,0:T(8,128)S(1)}, f32[72,512]{1,0:T(8,128)S(1)}, u32[]{:S(2)}, u32[]{:S(2)}) collective-permute-start(f32[72,512]{1,0:T(8,128)S(1)} %get-tuple-element.35), channel_id=1, source_target_pairs={{0,24},{8,0},{16,8},{24,16},{1,25},{9,1},{17,9},{25,17},{2,26},{10... | collective-permute-start | bytes 442376 | tf_op jit(solution)/shard_map/ppermute | solution.py:480
  24.4 4.3 %collective-permute-start.3 = (f32[72,512]{1,0:T(8,128)S(1)}, f32[72,512]{1,0:T(8,128)S(1)}, u32[]{:S(2)}, u32[]{:S(2)}) collective-permute-start(f32[72,512]{1,0:T(8,128)S(1)} %get-tuple-element.38.total_ref), channel_id=1, source_target_pairs={{0,32},{32,0},{64,96},{96,64},{128,160},{160,128},{192,224},{224,1... | collective-permute-start | bytes 442376 | tf_op jit(solution)/shard_map/ppermute | solution.py:485
  28.7 7.8 %collective-permute-start.4 = (f32[72,512]{1,0:T(8,128)S(1)}, f32[72,512]{1,0:T(8,128)S(1)}, u32[]{:S(2)}, u32[]{:S(2)}) collective-permute-start(f32[72,512]{1,0:T(8,128)S(1)} %get-tuple-element.39.total_ref), channel_id=1, source_target_pairs={{0,64},{32,96},{64,0},{96,32},{128,192},{160,224},{192,128},{224,1... | collective-permute-start | bytes 442376 | tf_op jit(solution)/shard_map/ppermute | solution.py:485
  36.6 7.8 %collective-permute-start.5 = (f32[72,512]{1,0:T(8,128)S(1)}, f32[72,512]{1,0:T(8,128)S(1)}, u32[]{:S(2)}, u32[]{:S(2)}) collective-permute-start(f32[72,512]{1,0:T(8,128)S(1)} %get-tuple-element.43.total_ref), channel_id=1, source_target_pairs={{0,224},{32,192},{64,160},{96,128},{128,96},{160,64},{192,32},{224... | collective-permute-start | bytes 442376 | tf_op jit(solution)/shard_map/ppermute | solution.py:485
  45.0 11.2 %collective-permute-start.6 = (f32[8,8,512]{2,1,0:T(8,128)S(1)}, f32[8,8,512]{2,1,0:T(8,128)S(1)}, u32[]{:S(2)}, u32[]{:S(2)}) collective-permute-start(f32[8,8,512]{2,1,0:T(8,128)S(1)} %get-tuple-element.48), channel_id=1, source_target_pairs={{0,8},{8,16},{16,24},{24,0},{1,9},{9,17},{17,25},{25,1},{2,10},{10... | collective-permute-start | bytes 393224 | tf_op jit(solution)/shard_map/ppermute | solution.py:480
  52.0 7.8 %collective-permute-start.7 = (f32[8,8,512]{2,1,0:T(8,128)S(1)}, f32[8,8,512]{2,1,0:T(8,128)S(1)}, u32[]{:S(2)}, u32[]{:S(2)}) collective-permute-start(f32[8,8,512]{2,1,0:T(8,128)S(1)} %get-tuple-element.49), channel_id=1, source_target_pairs={{0,16},{8,24},{16,0},{24,8},{1,17},{9,25},{17,1},{25,9},{2,18},{10... | collective-permute-start | bytes 393224 | tf_op jit(solution)/shard_map/ppermute | solution.py:480
  54.1 5.8 %collective-permute-start.8 = (f32[8,8,512]{2,1,0:T(8,128)S(1)}, f32[8,8,512]{2,1,0:T(8,128)S(1)}, u32[]{:S(2)}, u32[]{:S(2)}) collective-permute-start(f32[8,8,512]{2,1,0:T(8,128)S(1)} %get-tuple-element.50), channel_id=1, source_target_pairs={{0,24},{8,0},{16,8},{24,16},{1,25},{9,1},{17,9},{25,17},{2,26},{10... | collective-permute-start | bytes 393224 | tf_op jit(solution)/shard_map/ppermute | solution.py:480

commit v3 on v2

--- a/solution.py
+++ b/solution.py
@@ -34,6 +34,10 @@
 MIB = 1 << 20
 
 
+def in_hbm(x):
+    return pltpu.with_memory_space_constraint(x, pltpu.HBM)
+
+
 def place_of(axis):
     return lax.axis_index(axis).astype(jnp.int32)
 
@@ -66,7 +70,10 @@
     return sums[:k] + sums[k : 2 * k] + sums[2 * k :]
 
 
-def gate_kernel(g_ref, out_ref):
+def gate_kernel(g_hbm, out_ref, g_ref, sem):
+    copy = pltpu.make_async_copy(g_hbm, g_ref, sem)
+    copy.start()
+    copy.wait()
     cum = piece_sums(g_ref[1])
     own = g_ref[0] - cum
     for h in range(own.shape[0]):
@@ -78,29 +85,45 @@
     kinds, heads, n = gate_pre.shape
     return pl.pallas_call(
         gate_kernel,
-        in_specs=[VMEM],
+        in_specs=[HBM],
         out_specs=VMEM,
-        out_shape=pltpu.VMEM((heads, kinds, n), F32),
-        compiler_params=pltpu.CompilerParams(vmem_limit_bytes=8 * MIB),
+        out_shape=jax.ShapeDtypeStruct((heads, kinds, n), F32),
+        scratch_shapes=[pltpu.VMEM(gate_pre.shape, F32), pltpu.SemaphoreType.DMA(())],
+        compiler_params=pltpu.CompilerParams(vmem_limit_bytes=4 * MIB),
         name="gate_sums",
-    )(gate_pre)
-
-
-def turned_kernel(k_ref, kt_ref):
-    kt_ref[...] = k_ref[...].T
-
-
-def turned(keys):
+    )(in_hbm(gate_pre))
+
+
+def turned_kernel(k_hbm, v_hbm, kt_ref, v_ref, k_ref, k_sem, v_sem):
+    copies = []
+    for j in range(BLOCKS):
+        span = pl.ds(j * QB, QB)
+        copies.append(pltpu.make_async_copy(k_hbm.at[span], k_ref.at[span], k_sem.at[j]))
+        copies[-1].start()
+    values = pltpu.make_async_copy(v_hbm, v_ref, v_sem)
+    values.start()
+    for j in range(BLOCKS):
+        span = pl.ds(j * QB, QB)
+        copies[j].wait()
+        kt_ref[:, span] = k_ref[span, :].T
+    values.wait()
+
+
+def turned(keys, values):
     return pl.pallas_call(
         turned_kernel,
-        grid=(4,),
-        in_specs=[pl.BlockSpec((TOKS // 4, DQK), lambda i: (i, 0))],
-        out_specs=pl.BlockSpec((DQK, TOKS // 4), lambda i: (0, i)),
-        out_shape=jax.ShapeDtypeStruct((DQK, TOKS), BF16),
-        compiler_params=pltpu.CompilerParams(vmem_limit_bytes=8 * MIB),
+        in_specs=[HBM] * 2,
+        out_specs=[VMEM] * 2,
+        out_shape=[jax.ShapeDtypeStruct((DQK, TOKS), BF16), jax.ShapeDtypeStruct((TOKS, DV), BF16)],
+        scratch_shapes=[
+            pltpu.VMEM((TOKS, DQK), BF16),
+            pltpu.SemaphoreType.DMA((BLOCKS,)),
+            pltpu.SemaphoreType.DMA(()),
+        ],
+        compiler_params=pltpu.CompilerParams(vmem_limit_bytes=4 * MIB),
         cost_estimate=pl.CostEstimate(flops=0, bytes_accessed=4 * MIB, transcendentals=0),
         name="turn_keys",
-    )(keys)
+    )(in_hbm(keys), in_hbm(values))
 
 
 def state_kernel(g_ref, kt_ref, v_ref, own_ref, one_ref, two_ref, three_ref, tick_ref, w_ref, acc_ref):
@@ -254,14 +277,13 @@
     )(*args)
 
 
-def spread_kernel(total_ref, got_ref, prefix_ref, all_ref, after_ref, own_ref, one_ref, two_ref, three_ref, mine_ref, close_ref, norm_ref, top_ref, sum_ref, before_ref, out_ref):
-    x, z = place_of("ctx_1"), place_of("ctx_0")
-    merge(later_of(z, 2), total_ref, got_ref, prefix_ref, sum_ref, before_ref)
-    close_ref[0] = sum_ref[pl.ds(pl.multiple_of(z * ROWS, ROWS), ROWS), :]
-    norm, top, _ = pieces_of(sum_ref[SLICE:, :])
-    norm_ref[...] = norm[:, :DQK]
-    top_ref[...] = top[:, :LANES]
-    small = pieces_of(before_ref[SLICE:, :])
+def spread_kernel(got_ref, prefix_ref, all_ref, after_ref, own_ref, one_ref, two_ref, three_ref, mine_ref, out_ref):
+    x = place_of("ctx_1")
+    later = later_of(place_of("ctx_0"), 2)
+    before = pieces_of(prefix_ref[SLICE:, :])
+    bring, hold, small = chain_of(pieces_of(got_ref[SLICE:, :]), before)
+    bring, hold = jnp.where(later, bring, 0.0), jnp.where(later, hold, 1.0)
+    small = [jnp.where(later, n, o) for n, o in zip(small, before)]
     mine = small
     factors = []
     for j in range(XS - 1):
@@ -269,37 +291,28 @@
         mine = [jnp.where(x == j + 1, n, o) for n, o in zip(small, mine)]
         factors.append((keep, take))
     for at in range(0, SLICE, ROWS):
-        memory = before_ref[at : at + ROWS, :]
-        out_ref[0, at : at + ROWS, :] = memory
+        here = slice(at, at + ROWS)
+        memory = bring * got_ref[here, :] + hold * prefix_ref[here, :]
+        out_ref[0, here, :] = memory
         for j, (keep, take) in enumerate(factors):
-            memory = keep * memory + take * all_ref[j, at : at + ROWS, :]
-            out_ref[j + 1, at : at + ROWS, :] = memory
+            memory = keep * memory + take * all_ref[j, here, :]
+            out_ref[j + 1, here, :] = memory
     for k, ref in enumerate((own_ref, one_ref, two_ref, three_ref)):
         ref[...] = out_ref[pl.ds(lax.rem(x + k, XS), 1)].reshape(ZS, ROWS, DV)
     mine_ref[...] = tail_of(*mine)
 
 
-def spread(total, got, prefix, everything, after):
+def spread(got, prefix, everything, after):
     return pl.pallas_call(
         spread_kernel,
-        in_specs=[VMEM] * 4 + [ANY],
-        out_specs=[VMEM] * 8,
-        out_shape=[jax.ShapeDtypeStruct((ZS, ROWS, DV), F32)] * 4
-        + [
-            jax.ShapeDtypeStruct((8, DV), F32),
-            jax.ShapeDtypeStruct((1, ROWS, DV), F32),
-            jax.ShapeDtypeStruct((1, DQK), F32),
-            jax.ShapeDtypeStruct((1, LANES), F32),
-        ],
-        scratch_shapes=[
-            pltpu.VMEM((SENT, DV), F32),
-            pltpu.VMEM((SENT, DV), F32),
-            pltpu.VMEM((XS, SLICE, DV), F32),
-        ],
+        in_specs=[VMEM] * 3 + [ANY],
+        out_specs=[VMEM] * 5,
+        out_shape=[jax.ShapeDtypeStruct((ZS, ROWS, DV), F32)] * 4 + [jax.ShapeDtypeStruct((8, DV), F32)],
+        scratch_shapes=[pltpu.VMEM((XS, SLICE, DV), F32)],
         compiler_params=pltpu.CompilerParams(vmem_limit_bytes=4 * MIB),
         cost_estimate=pl.CostEstimate(flops=1_000_000, bytes_accessed=2 * MIB, transcendentals=0),
         name="spread_prefixes",
-    )(total, got, prefix, everything, after)
+    )(got, prefix, everything, after)
 
 
 def wide(x, n):
@@ -375,8 +388,13 @@
             lax.fori_loop(0, i, earlier, jnp.zeros((1, 1), F32))
 
 
-def first_kernel(blocks, g_ref, tick_ref, q_ref, k_ref, v_ref, num_ref, den_ref, table_ref):
+def first_kernel(blocks, g_ref, tick_ref, q_hbm, k_hbm, v_ref, num_ref, den_ref, table_ref, q_ref, k_ref, q_sem, k_sem):
+    copies = [pltpu.make_async_copy(q_hbm, q_ref, q_sem), pltpu.make_async_copy(k_hbm, k_ref, k_sem)]
+    for copy in copies:
+        copy.start()
     tables(g_ref, table_ref)
+    for copy in copies:
+        copy.wait()
     local_kernel(blocks, table_ref, tick_ref, q_ref, k_ref, v_ref, num_ref, den_ref)
 
 
@@ -388,20 +406,34 @@
         jax.ShapeDtypeStruct((count * QB, DV), F32),
         jax.ShapeDtypeStruct((count * QB, LANES), F32),
         jax.ShapeDtypeStruct((3 * BLOCKS, QB), F32),
-    ][: 3 if first else 2]
+        jax.ShapeDtypeStruct((TOKS, DQK), BF16),
+        jax.ShapeDtypeStruct((TOKS, DQK), BF16),
+    ][: 5 if first else 2]
     return pl.pallas_call(
         functools.partial(first_kernel if first else local_kernel, blocks),
-        in_specs=[VMEM, ANY] + [VMEM] * 3,
+        in_specs=[VMEM, ANY, HBM, HBM, VMEM] if first else [VMEM, ANY] + [VMEM] * 3,
         out_specs=[VMEM] * len(out_shape),
         out_shape=out_shape,
+        scratch_shapes=[pltpu.SemaphoreType.DMA(())] * (2 * first),
         compiler_params=pltpu.CompilerParams(vmem_limit_bytes=8 * MIB),
         cost_estimate=pl.CostEstimate(flops=800_000_000 * units, bytes_accessed=MIB * units, transcendentals=0),
         name="within_shard",
-    )(gates if first else table, tick, queries, keys, values)
-
-
-def scale_kernel(table_ref, mine_ref, q_ref, *refs):
-    dens, (kept_ref, carried_ref) = refs[:-2], refs[-2:]
+    )(*((gates, tick, in_hbm(queries), in_hbm(keys), values) if first else (table, tick, queries, keys, values)))
+
+
+def scale_kernel(table_ref, mine_ref, q_ref, total_ref, got_ref, *refs):
+    dens, (kept_ref, carried_ref, close_ref, norm_ref, top_ref) = refs[:-5], refs[-5:]
+    z = place_of("ctx_0")
+    later = later_of(z, 2)
+    here = pl.ds(pl.multiple_of(z * ROWS, ROWS), ROWS)
+    own, got = pieces_of(total_ref[SLICE:, :]), pieces_of(got_ref[SLICE:, :])
+    first = [jnp.where(later, g, o) for g, o in zip(got, own)]
+    second = [jnp.where(later, o, g) for g, o in zip(got, own)]
+    keep, take, (end_norm, end_top, _) = chain_of(first, second)
+    f_own, f_got = jnp.where(later, take, keep), jnp.where(later, keep, take)
+    close_ref[0] = f_own * total_ref[here, :] + f_got * got_ref[here, :]
+    norm_ref[...] = end_norm[:, :DQK]
+    top_ref[...] = end_top[:, :LANES]
     norm, log_in, _ = pieces_of(mine_ref)
     norm, log_in = norm[:, :DQK], log_in[:, :LANES]
     place = {i: (dens[n], m) for n, blocks in enumerate(PARTS) for m, i in enumerate(blocks)}
@@ -419,16 +451,21 @@
         log_in = log_in + table_ref[BLOCKS + i : BLOCKS + i + 1, :][:, QB - 1 :]
 
 
-def scales(table, mine, queries, dens):
+def scales(table, mine, queries, total, got, dens):
     return pl.pallas_call(
         scale_kernel,
-        in_specs=[VMEM] * (3 + len(dens)),
-        out_specs=[VMEM] * 2,
-        out_shape=[jax.ShapeDtypeStruct((TOKS, LANES), F32)] * 2,
+        in_specs=[VMEM] * (5 + len(dens)),
+        out_specs=[VMEM] * 5,
+        out_shape=[jax.ShapeDtypeStruct((TOKS, LANES), F32)] * 2
+        + [
+            jax.ShapeDtypeStruct((1, ROWS, DV), F32),
+            jax.ShapeDtypeStruct((1, DQK), F32),
+            jax.ShapeDtypeStruct((1, LANES), F32),
+        ],
         compiler_params=pltpu.CompilerParams(vmem_limit_bytes=4 * MIB),
         cost_estimate=pl.CostEstimate(flops=600_000_000, bytes_accessed=4 * MIB, transcendentals=0),
         name="row_scales",
-    )(table, mine, queries, *dens)
+    )(table, mine, queries, total, got, *dens)
 
 
 def joined_kernel(q_ref, own_ref, one_ref, two_ref, three_ref, kept_ref, carried_ref, *refs):
@@ -487,22 +524,22 @@
 
 def on_device(queries, keys, values, gate_pre):
     gates = exchanged(gate_sums(gate_pre), "head")
-    keys_t = turned(keys)
+    keys_t, values = turned(keys, values)
     *parts, tick = state(gates, keys_t, values)
     moved = around(parts)
+    num_a, den_a, table, queries, keys = local(PARTS[0], gates, tick, queries, keys, values)
     qkv = (queries, keys, values)
-    num_a, den_a, table = local(PARTS[0], gates, tick, *qkv)
     total, everything = grouped(moved, den_a)
     got = swapped(total, lambda i: i ^ 1)
     total, prefix = round_of(first_round_kernel, total, got, den_a)
     got = swapped(total, lambda i: i ^ 2)
     num_b, den_b = local(PARTS[1], None, prefix, *qkv, table)
     total, prefix = round_of(next_round_kernel, total, got, prefix, den_b)
-    got = swapped(total, lambda i: ZS - 1 - i)
+    got = swapped(total, lambda i: (6, 7, 5, 4, 3, 2, 0, 1)[i])
     num_c, den_c = local(PARTS[2], None, prefix, *qkv, table)
-    *parts, mine, closing, final_norm, top = spread(total, got, prefix, everything, den_c)
+    *parts, mine = spread(got, prefix, everything, den_c)
     moved = around(parts)
-    kept, carried = scales(table, mine, queries, [den_a, den_b, den_c])
+    kept, carried, closing, final_norm, top = scales(table, mine, queries, total, got, [den_a, den_b, den_c])
     hidden = joined(queries, moved, kept, carried, [num_a, num_b, num_c])
     return (hidden, closing, final_norm, top[0, :1])
 

time: 61.8 us -> 60.8 us (0.984)
  the two profiles are of different devices: /device:TPU:1 before, /device:TPU:32 now
where the time goes in v3:
time: 60.8 us; the launch traced here: 60.6 us
  starting transfers between devices  26.7 us (44%)
  waiting for transfers between devices  17.3 us (28%)
  Pallas kernels  15.9 us (26%)
  between operations  0.71 us (1%)
    ppermute x6, starting transfers between devices, around(): lax.ppermute(parts[k], 'ctx_1', [(i, (i + k) % XS) for i in range(XS)])  12.6 us
    ppermute x3, starting transfers between devices, swapped(): return lax.ppermute(x, 'ctx_0', [(i, partner(i)) for i in range(ZS)])  9.62 us
    ppermute x3, waiting for transfers between devices, swapped(): return lax.ppermute(x, 'ctx_0', [(i, partner(i)) for i in range(ZS)])  9.28 us
    pallas_call x3, Pallas kernels, local(): pl.pallas_call(functools.partial(first_kernel if first else local_kernel,...  7.31 us
    ppermute x6, waiting for transfers between devices, around(): lax.ppermute(parts[k], 'ctx_1', [(i, (i + k) % XS) for i in range(XS)])  4.67 us
    all_to_all x1, starting transfers between devices, exchanged(): return lax.all_to_all(x, axis, split_axis=0, concat_axis=0, tiled=True)  4.48 us
    all_to_all x1, waiting for transfers between devices, exchanged(): return lax.all_to_all(x, axis, split_axis=0, concat_axis=0, tiled=True)  3.38 us
    pallas_call x1, Pallas kernels, turned(): pl.pallas_call(turned_kernel, in_specs=[HBM] * 2, out_specs=[VMEM] * 2, o...  1.97 us
  transfers between devices with their start and end apart: 10, of which 6 were waited for; matrix products, arithmetic and copies ran while one was open for 0% of the time, Pallas kernels for 18%

profile of v3, /device:TPU:32, one launch (start us, length us, event | category | flops | bytes accessed | tf_op | source)
XLA Modules:
  0.0 60.6 jit_solution(10301419883842624271)
XLA Ops:
  0.6 1.5 %gate_sums.1 = f32[8,2,256]{2,1,0:T(2,128)} custom-call(f32[2,8,256]{2,1,0:T(8,128)} %g_hbm.1), custom_call_target="tpu_custom_call" | custom-call | tf_op jit(solution)/shard_map/gate_sums/pallas_call | solution.py:86
  2.1 4.5 %all-to-all-start = ((f32[8,2,256]{2,1,0:T(2,128)}), f32[8,2,256]{2,1,0:T(2,128)S(1)}, u32[]{:S(2)}, u32[]{:S(2)}) async-start(f32[8,2,256]{2,1,0:T(2,128)} %gate_sums.1), calls=%async_computation | async-start | bytes 32768 | tf_op jit(solution)/shard_map/all_to_all | solution.py:511
  6.6 2.0 %turn_keys.1 = (bf16[256,2048]{1,0:T(8,128)(2,1)S(1)}, bf16[2048,512]{1,0:T(8,128)(2,1)S(1)}) custom-call(bf16[2048,256]{1,0:T(8,128)(2,1)} %k_hbm.3, bf16[2048,512]{1,0:T(8,128)(2,1)} %v_hbm.1), custom_call_target="tpu_custom_call" | custom-call | bytes 4194304 | tf_op jit(solution)/shard_map/turn_keys/pallas_call | solution.py:113
  8.6 3.4 %all-to-all-done.g_ref = f32[8,2,256]{2,1,0:T(2,128)S(1)} async-done(((f32[8,2,256]{2,1,0:T(2,128)}), f32[8,2,256]{2,1,0:T(2,128)S(1)}, u32[]{:S(2)}, u32[]{:S(2)}) %all-to-all-start) | async-done | bytes 16416 | tf_op jit(solution)/shard_map/all_to_all | solution.py:511
  12.0 1.2 %shard_state.1 = (f32[72,512]{1,0:T(8,128)S(1)}, f32[72,512]{1,0:T(8,128)S(1)}, f32[72,512]{1,0:T(8,128)S(1)}, f32[72,512]{1,0:T(8,128)S(1)}, f32[8,128]{1,0:T(8,128)S(1)}) custom-call(f32[8,2,256]{2,1,0:T(2,128)S(1)} %all-to-all-done.g_ref, bf16[256,2048]{1,0:T(8,128)(2,1)S(1)} %get-tuple-element.36.kt_ref, bf16[2048,512]{1,0:T(8,128)(2,1)S(1)} %get-tuple-element.37.v_ref), custom_call_target="tpu_custom_call" | custom-call | flops 600000000 | bytes 5242880 | tf_op jit(solution)/shard_map/shard_state/pallas_call | solution.py:165
  13.2 1.6 %collective-permute-start = (f32[72,512]{1,0:T(8,128)S(1)}, f32[72,512]{1,0:T(8,128)S(1)}, u32[]{:S(2)}, u32[]{:S(2)}) collective-permute-start(f32[72,512]{1,0:T(8,128)S(1)} %get-tuple-element.41), channel_id=1, source_target_pairs={{0,8},{8,16},{16,24},{24,0},{1,9},{9,17},{17,25},{25,1},{2,10},{10... | collective-permute-start | bytes 442376 | tf_op jit(solution)/shard_map/ppermute | solution.py:517
  14.8 2.7 %collective-permute-start.1 = (f32[72,512]{1,0:T(8,128)S(1)}, f32[72,512]{1,0:T(8,128)S(1)}, u32[]{:S(2)}, u32[]{:S(2)}) collective-permute-start(f32[72,512]{1,0:T(8,128)S(1)} %get-tuple-element.42), channel_id=1, source_target_pairs={{0,16},{8,24},{16,0},{24,8},{1,17},{9,25},{17,1},{25,9},{2,18},{10... | collective-permute-start | bytes 442376 | tf_op jit(solution)/shard_map/ppermute | solution.py:517
  17.5 1.4 %collective-permute-start.2 = (f32[72,512]{1,0:T(8,128)S(1)}, f32[72,512]{1,0:T(8,128)S(1)}, u32[]{:S(2)}, u32[]{:S(2)}) collective-permute-start(f32[72,512]{1,0:T(8,128)S(1)} %get-tuple-element.43), channel_id=1, source_target_pairs={{0,24},{8,0},{16,8},{24,16},{1,25},{9,1},{17,9},{25,17},{2,26},{10... | collective-permute-start | bytes 442376 | tf_op jit(solution)/shard_map/ppermute | solution.py:517
  18.9 4.0 %within_shard.3 = (f32[512,512]{1,0:T(8,128)S(1)}, f32[512,128]{1,0:T(8,128)S(1)}, f32[12,512]{1,0:T(8,128)S(1)}, bf16[2048,256]{1,0:T(8,128)(2,1)S(1)}, bf16[2048,256]{1,0:T(8,128)(2,1)S(1)}) custom-call(f32[8,2,256]{2,1,0:T(2,128)S(1)} %all-to-all-done.g_ref, f32[8,128]{1,0:T(8,128)S(1)} %get-tuple-element.38.tick_ref, bf16[2048,256]{1,0:T(8,128)(2,1)} %q_hbm.1, ...), custom_call_target="tpu_custom_call" | custom-call | flops 3200000000 | bytes 4194304 | tf_op jit(solution)/shard_map/within_shard/pallas_call | solution.py:412
  23.0 1.2 %collective-permute-done.1.two_ref = f32[72,512]{1,0:T(8,128)S(1)} collective-permute-done((f32[72,512]{1,0:T(8,128)S(1)}, f32[72,512]{1,0:T(8,128)S(1)}, u32[]{:S(2)}, u32[]{:S(2)}) %collective-permute-start.1) | collective-permute-done | bytes 147488 | tf_op jit(solution)/shard_map/ppermute | solution.py:517
  24.3 0.3 collective-permute-start.3
  24.6 5.0 %collective-permute-done.3.got_ref = f32[72,512]{1,0:T(8,128)S(1)} collective-permute-done((f32[72,512]{1,0:T(8,128)S(1)}, f32[72,512]{1,0:T(8,128)S(1)}, u32[]{:S(2)}, u32[]{:S(2)}) %collective-permute-start.3) | collective-permute-done | bytes 147488 | tf_op jit(solution)/shard_map/ppermute | solution.py:522
  29.6 3.4 %collective-permute-start.4 = (f32[72,512]{1,0:T(8,128)S(1)}, f32[72,512]{1,0:T(8,128)S(1)}, u32[]{:S(2)}, u32[]{:S(2)}) collective-permute-start(f32[72,512]{1,0:T(8,128)S(1)} %get-tuple-element.46.total_ref), channel_id=1, source_target_pairs={{0,64},{32,96},{64,0},{96,32},{128,192},{160,224},{192,128},{224,1... | collective-permute-start | bytes 442376 | tf_op jit(solution)/shard_map/ppermute | solution.py:522
  33.0 1.4 %within_shard.4 = (f32[1024,512]{1,0:T(8,128)S(1)}, f32[1024,128]{1,0:T(8,128)S(1)}) custom-call(f32[12,512]{1,0:T(8,128)S(1)} %get-tuple-element.48.table_ref, f32[72,512]{1,0:T(8,128)S(1)} %get-tuple-element.47.tick_ref.prefix_ref, bf16[2048,256]{1,0:T(8,128)(2,1)S(1)} %get-tuple-element.39.q_ref, bf16[2048,256]{1,0:T(8,128)(2,1)S(1)} %get-tuple-element.49.k_ref, ...), custom_call_target="tpu_custom_call" | custom-call | flops 2400000000 | bytes 3145728 | tf_op jit(solution)/shard_map/within_shard/pallas_call | solution.py:412
  34.4 2.5 %collective-permute-done.4.got_ref = f32[72,512]{1,0:T(8,128)S(1)} collective-permute-done((f32[72,512]{1,0:T(8,128)S(1)}, f32[72,512]{1,0:T(8,128)S(1)}, u32[]{:S(2)}, u32[]{:S(2)}) %collective-permute-start.4) | collective-permute-done | bytes 147488 | tf_op jit(solution)/shard_map/ppermute | solution.py:522
  37.0 6.0 %collective-permute-start.5 = (f32[72,512]{1,0:T(8,128)S(1)}, f32[72,512]{1,0:T(8,128)S(1)}, u32[]{:S(2)}, u32[]{:S(2)}) collective-permute-start(f32[72,512]{1,0:T(8,128)S(1)} %get-tuple-element.51.total_ref), channel_id=1, source_target_pairs={{0,192},{32,224},{64,160},{96,128},{128,96},{160,64},{192,0},{224,... | collective-permute-start | bytes 442376 | tf_op jit(solution)/shard_map/ppermute | solution.py:522
  43.0 1.8 %within_shard.5 = (f32[512,512]{1,0:T(8,128)S(1)}, f32[512,128]{1,0:T(8,128)S(1)}) custom-call(f32[12,512]{1,0:T(8,128)S(1)} %get-tuple-element.48.table_ref, f32[72,512]{1,0:T(8,128)S(1)} %get-tuple-element.52.tick_ref.prefix_ref, bf16[2048,256]{1,0:T(8,128)(2,1)S(1)} %get-tuple-element.39.q_ref, bf16[2048,256]{1,0:T(8,128)(2,1)S(1)} %get-tuple-element.49.k_ref, ...), custom_call_target="tpu_custom_call" | custom-call | flops 2400000000 | bytes 3145728 | tf_op jit(solution)/shard_map/within_shard/pallas_call | solution.py:412
  44.8 1.8 %collective-permute-done.5.got_ref = f32[72,512]{1,0:T(8,128)S(1)} collective-permute-done((f32[72,512]{1,0:T(8,128)S(1)}, f32[72,512]{1,0:T(8,128)S(1)}, u32[]{:S(2)}, u32[]{:S(2)}) %collective-permute-start.5) | collective-permute-done | bytes 147488 | tf_op jit(solution)/shard_map/ppermute | solution.py:522
  46.8 4.1 %collective-permute-start.6 = (f32[8,8,512]{2,1,0:T(8,128)S(1)}, f32[8,8,512]{2,1,0:T(8,128)S(1)}, u32[]{:S(2)}, u32[]{:S(2)}) collective-permute-start(f32[8,8,512]{2,1,0:T(8,128)S(1)} %get-tuple-element.56), channel_id=1, source_target_pairs={{0,8},{8,16},{16,24},{24,0},{1,9},{9,17},{17,25},{25,1},{2,10},{10... | collective-permute-start | bytes 393224 | tf_op jit(solution)/shard_map/ppermute | solution.py:517
  50.9 1.9 %collective-permute-start.7 = (f32[8,8,512]{2,1,0:T(8,128)S(1)}, f32[8,8,512]{2,1,0:T(8,128)S(1)}, u32[]{:S(2)}, u32[]{:S(2)}) collective-permute-start(f32[8,8,512]{2,1,0:T(8,128)S(1)} %get-tuple-element.57), channel_id=1, source_target_pairs={{0,16},{8,24},{16,0},{24,8},{1,17},{9,25},{17,1},{25,9},{2,18},{10... | collective-permute-start | bytes 393224 | tf_op jit(solution)/shard_map/ppermute | solution.py:517
  52.7 0.9 %collective-permute-start.8 = (f32[8,8,512]{2,1,0:T(8,128)S(1)}, f32[8,8,512]{2,1,0:T(8,128)S(1)}, u32[]{:S(2)}, u32[]{:S(2)}) collective-permute-start(f32[8,8,512]{2,1,0:T(8,128)S(1)} %get-tuple-element.58), channel_id=1, source_target_pairs={{0,24},{8,0},{16,8},{24,16},{1,25},{9,1},{17,9},{25,17},{2,26},{10... | collective-permute-start | bytes 393224 | tf_op jit(solution)/shard_map/ppermute | solution.py:517
  53.7 1.8 %row_scales.1 = (f32[2048,128]{1,0:T(8,128)S(1)}, f32[2048,128]{1,0:T(8,128)S(1)}, f32[1,8,512]{2,1,0:T(8,128)}, f32[1,256]{1,0:T(1,128)}, f32[1,128]{1,0:T(1,128)}) custom-call(f32[12,512]{1,0:T(8,128)S(1)} %get-tuple-element.48.table_ref, f32[8,512]{1,0:T(8,128)S(1)} %get-tuple-element.59.mine_ref, bf16[2048,256]{1,0:T(8,128)(2,1)S(1)} %get-tuple-element.39.q_ref, ...), custom_call_target="tpu_custom_call" | custom-call | flops 600000000 | bytes 4194304 | tf_op jit(solution)/shard_map/row_scales/pallas_call | solution.py:455
  55.5 3.4 %collective-permute-done.7.two_ref = f32[8,8,512]{2,1,0:T(8,128)S(1)} collective-permute-done((f32[8,8,512]{2,1,0:T(8,128)S(1)}, f32[8,8,512]{2,1,0:T(8,128)S(1)}, u32[]{:S(2)}, u32[]{:S(2)}) %collective-permute-start.7) | collective-permute-done | bytes 131104 | tf_op jit(solution)/shard_map/ppermute | solution.py:517
  58.9 1.7 %join_memory.1 = bf16[2048,512]{1,0:T(8,128)(2,1)} custom-call(bf16[2048,256]{1,0:T(8,128)(2,1)S(1)} %get-tuple-element.39.q_ref, f32[8,8,512]{2,1,0:T(8,128)S(1)} %get-tuple-element.55.own_ref, f32[8,8,512]{2,1,0:T(8,128)S(1)} %collective-permute-done.6.one_ref, f32[8,8,512]{2,1,0:T(8,128)S(1)} %collective-permute-done.7.two_ref, ...), custom_call_target="tpu_custom_call" | custom-call | flops 600000000 | bytes 9437184 | tf_op jit(solution)/shard_map/join_memory/pallas_call | solution.py:493
  (8 shorter events, 0.4 us)
Async XLA Ops:
  2.1 9.8 %all-to-all-start = ((f32[8,2,256]{2,1,0:T(2,128)}), f32[8,2,256]{2,1,0:T(2,128)S(1)}, u32[]{:S(2)}, u32[]{:S(2)}) async-start(f32[8,2,256]{2,1,0:T(2,128)} %gate_sums.1), calls=%async_computation | async-start | bytes 32768 | tf_op jit(solution)/shard_map/all_to_all | solution.py:511
  13.2 9.8 %collective-permute-start = (f32[72,512]{1,0:T(8,128)S(1)}, f32[72,512]{1,0:T(8,128)S(1)}, u32[]{:S(2)}, u32[]{:S(2)}) collective-permute-start(f32[72,512]{1,0:T(8,128)S(1)} %get-tuple-element.41), channel_id=1, source_target_pairs={{0,8},{8,16},{16,24},{24,0},{1,9},{9,17},{17,25},{25,1},{2,10},{10... | collective-permute-start | bytes 442376 | tf_op jit(solution)/shard_map/ppermute | solution.py:517
  14.8 9.4 %collective-permute-start.1 = (f32[72,512]{1,0:T(8,128)S(1)}, f32[72,512]{1,0:T(8,128)S(1)}, u32[]{:S(2)}, u32[]{:S(2)}) collective-permute-start(f32[72,512]{1,0:T(8,128)S(1)} %get-tuple-element.42), channel_id=1, source_target_pairs={{0,16},{8,24},{16,0},{24,8},{1,17},{9,25},{17,1},{25,9},{2,18},{10... | collective-permute-start | bytes 442376 | tf_op jit(solution)/shard_map/ppermute | solution.py:517
  17.5 6.7 %collective-permute-start.2 = (f32[72,512]{1,0:T(8,128)S(1)}, f32[72,512]{1,0:T(8,128)S(1)}, u32[]{:S(2)}, u32[]{:S(2)}) collective-permute-start(f32[72,512]{1,0:T(8,128)S(1)} %get-tuple-element.43), channel_id=1, source_target_pairs={{0,24},{8,0},{16,8},{24,16},{1,25},{9,1},{17,9},{25,17},{2,26},{10... | collective-permute-start | bytes 442376 | tf_op jit(solution)/shard_map/ppermute | solution.py:517
  24.3 5.2 %collective-permute-start.3 = (f32[72,512]{1,0:T(8,128)S(1)}, f32[72,512]{1,0:T(8,128)S(1)}, u32[]{:S(2)}, u32[]{:S(2)}) collective-permute-start(f32[72,512]{1,0:T(8,128)S(1)} %get-tuple-element.45.total_ref), channel_id=1, source_target_pairs={{0,32},{32,0},{64,96},{96,64},{128,160},{160,128},{192,224},{224,1... | collective-permute-start | bytes 442376 | tf_op jit(solution)/shard_map/ppermute | solution.py:522
  29.6 7.3 %collective-permute-start.4 = (f32[72,512]{1,0:T(8,128)S(1)}, f32[72,512]{1,0:T(8,128)S(1)}, u32[]{:S(2)}, u32[]{:S(2)}) collective-permute-start(f32[72,512]{1,0:T(8,128)S(1)} %get-tuple-element.46.total_ref), channel_id=1, source_target_pairs={{0,64},{32,96},{64,0},{96,32},{128,192},{160,224},{192,128},{224,1... | collective-permute-start | bytes 442376 | tf_op jit(solution)/shard_map/ppermute | solution.py:522
  37.0 9.7 %collective-permute-start.5 = (f32[72,512]{1,0:T(8,128)S(1)}, f32[72,512]{1,0:T(8,128)S(1)}, u32[]{:S(2)}, u32[]{:S(2)}) collective-permute-start(f32[72,512]{1,0:T(8,128)S(1)} %get-tuple-element.51.total_ref), channel_id=1, source_target_pairs={{0,192},{32,224},{64,160},{96,128},{128,96},{160,64},{192,0},{224,... | collective-permute-start | bytes 442376 | tf_op jit(solution)/shard_map/ppermute | solution.py:522
  46.8 8.6 %collective-permute-start.6 = (f32[8,8,512]{2,1,0:T(8,128)S(1)}, f32[8,8,512]{2,1,0:T(8,128)S(1)}, u32[]{:S(2)}, u32[]{:S(2)}) collective-permute-start(f32[8,8,512]{2,1,0:T(8,128)S(1)} %get-tuple-element.56), channel_id=1, source_target_pairs={{0,8},{8,16},{16,24},{24,0},{1,9},{9,17},{17,25},{25,1},{2,10},{10... | collective-permute-start | bytes 393224 | tf_op jit(solution)/shard_map/ppermute | solution.py:517
  50.9 8.0 %collective-permute-start.7 = (f32[8,8,512]{2,1,0:T(8,128)S(1)}, f32[8,8,512]{2,1,0:T(8,128)S(1)}, u32[]{:S(2)}, u32[]{:S(2)}) collective-permute-start(f32[8,8,512]{2,1,0:T(8,128)S(1)} %get-tuple-element.57), channel_id=1, source_target_pairs={{0,16},{8,24},{16,0},{24,8},{1,17},{9,25},{17,1},{25,9},{2,18},{10... | collective-permute-start | bytes 393224 | tf_op jit(solution)/shard_map/ppermute | solution.py:517
  52.7 6.2 %collective-permute-start.8 = (f32[8,8,512]{2,1,0:T(8,128)S(1)}, f32[8,8,512]{2,1,0:T(8,128)S(1)}, u32[]{:S(2)}, u32[]{:S(2)}) collective-permute-start(f32[8,8,512]{2,1,0:T(8,128)S(1)} %get-tuple-element.58), channel_id=1, source_target_pairs={{0,24},{8,0},{16,8},{24,16},{1,25},{9,1},{17,9},{25,17},{2,26},{10... | collective-permute-start | bytes 393224 | tf_op jit(solution)/shard_map/ppermute | solution.py:517

commit v4 on v3

--- a/solution.py
+++ b/solution.py
@@ -13,12 +13,11 @@
 XS = 4
 ZS = 8
 ROWS = DQK // (XS * ZS)
-SLICE = ZS * ROWS
-SENT = SLICE + 8
 PIECES = 8
 PIECE = 256
 LANES = 128
-WIDE = DV + LANES
+SLICE = ZS * DV
+SENT = SLICE + LANES
 TOKS = PIECES * PIECE
 QB = 512
 BLOCKS = TOKS // QB
@@ -151,14 +150,15 @@
             product += acc_ref[...].reshape(DQK, DV)
         acc_ref[...] = product.reshape(ZS, XS, ROWS, DV)
     norm = norm[0:8] + norm[8:16] + norm[16:24]
-    norm = jnp.concatenate([norm, norm], axis=1)
-    extra = tail_of(norm[0:1], stab, later[0:1, 0:1])
+    norm = jnp.concatenate([norm[0:1, :LANES], norm[0:1, LANES:]], axis=0)
+    extra = tail_of(norm, stab, later[0:1, :LANES])
     x = place_of("ctx_1")
     for k, ref in enumerate((own_ref, one_ref, two_ref, three_ref)):
         to = lax.rem(x + k, XS)
-        ref[0:SLICE, :] = acc_ref[:, pl.ds(to, 1)].reshape(SLICE, DV)
-        ref[SLICE:, :] = extra
-    tick_ref[...] = extra[:, :LANES]
+        for z in range(ZS):
+            ref[:, z * DV : (z + 1) * DV] = acc_ref[z, pl.ds(to, 1)].reshape(ROWS, DV)
+        ref[:, SLICE:] = extra
+    tick_ref[...] = extra
 
 
 def state(gates, keys_t, values):
@@ -166,7 +166,7 @@
         state_kernel,
         in_specs=[VMEM, VMEM, VMEM],
         out_specs=[VMEM] * 5,
-        out_shape=[jax.ShapeDtypeStruct((SENT, DV), F32)] * 4 + [jax.ShapeDtypeStruct((8, LANES), F32)],
+        out_shape=[jax.ShapeDtypeStruct((ROWS, SENT), F32)] * 4 + [jax.ShapeDtypeStruct((8, LANES), F32)],
         scratch_shapes=[
             pltpu.VMEM((PIECES, PIECE), F32),
             pltpu.VMEM((ZS, XS, ROWS, DV), F32),
@@ -178,12 +178,13 @@
 
 
 def tail_of(norm, stab, total):
-    row = lax.broadcasted_iota(jnp.int32, (8, DV), 0)
-    return jnp.where(row == 0, norm, jnp.where(row == 1, stab, total))
+    row = lax.broadcasted_iota(jnp.int32, (8, LANES), 0)
+    tail = jnp.where(row == 0, norm[0:1], norm[1:2])
+    return jnp.where(row == 2, stab, jnp.where(row == 3, total, tail))
 
 
 def pieces_of(tail):
-    return tail[0:1, :], tail[1:2, :], tail[2:3, :]
+    return tail[0:2, :], tail[2:3, :], tail[3:4, :]
 
 
 def chain_of(early, late):
@@ -195,22 +196,26 @@
     return keep, take, (keep * norm_e + take * norm_l, stab, total_e + total_l)
 
 
+def spans():
+    return [slice(z * DV, (z + 1) * DV) for z in range(ZS)]
+
+
 def group_kernel(own_ref, one_ref, two_ref, three_ref, after_ref, out_ref, all_ref):
     x = place_of("ctx_1")
     for k, ref in enumerate((own_ref, one_ref, two_ref, three_ref)):
         at = lax.rem(x + XS - k, XS)
-        all_ref[pl.ds(at, 1)] = ref[...].reshape(1, SENT, DV)
-    small = pieces_of(all_ref[0, SLICE:, :])
+        all_ref[pl.ds(at, 1)] = ref[...].reshape(1, ROWS, SENT)
+    small = pieces_of(all_ref[0, :, SLICE:])
     factors = []
     for j in range(1, XS):
-        keep, take, small = chain_of(small, pieces_of(all_ref[j, SLICE:, :]))
-        factors.append((keep, take))
-    for at in range(0, SLICE, ROWS):
-        memory = all_ref[0, at : at + ROWS, :]
+        keep, take, small = chain_of(small, pieces_of(all_ref[j, :, SLICE:]))
+        factors.append((wide(keep, DV), wide(take, DV)))
+    for here in spans():
+        memory = all_ref[0, :, here]
         for j, (keep, take) in enumerate(factors):
-            memory = keep * memory + take * all_ref[j + 1, at : at + ROWS, :]
-        out_ref[at : at + ROWS, :] = memory
-    out_ref[SLICE:, :] = tail_of(*small)
+            memory = keep * memory + take * all_ref[j + 1, :, here]
+        out_ref[:, here] = memory
+    out_ref[:, SLICE:] = tail_of(*small)
 
 
 def grouped(parts, after):
@@ -219,8 +224,8 @@
         in_specs=[VMEM] * 4 + [ANY],
         out_specs=[VMEM] * 2,
         out_shape=[
-            jax.ShapeDtypeStruct((SENT, DV), F32),
-            jax.ShapeDtypeStruct((XS, SENT, DV), F32),
+            jax.ShapeDtypeStruct((ROWS, SENT), F32),
+            jax.ShapeDtypeStruct((XS, ROWS, SENT), F32),
         ],
         compiler_params=pltpu.CompilerParams(vmem_limit_bytes=4 * MIB),
         cost_estimate=pl.CostEstimate(flops=1_000_000, bytes_accessed=2 * MIB, transcendentals=0),
@@ -228,29 +233,18 @@
     )(*parts, after)
 
 
-def merge(later, total_ref, got_ref, prefix_ref, new_total, new_prefix):
-    own, got = pieces_of(total_ref[SLICE:, :]), pieces_of(got_ref[SLICE:, :])
+def merged(later, total_ref, got_ref):
+    own, got = pieces_of(total_ref[:, SLICE:]), pieces_of(got_ref[:, SLICE:])
     first = [jnp.where(later, g, o) for g, o in zip(got, own)]
     second = [jnp.where(later, o, g) for g, o in zip(got, own)]
     keep, take, small = chain_of(first, second)
-    f_own, f_got = jnp.where(later, take, keep), jnp.where(later, keep, take)
-    for at in range(0, SLICE, ROWS):
-        here = slice(at, at + ROWS)
-        new_total[here, :] = f_own * total_ref[here, :] + f_got * got_ref[here, :]
-    new_total[SLICE:, :] = tail_of(*small)
-    if prefix_ref is None:
-        before = (jnp.zeros((1, DV), F32), jnp.full((1, DV), NEG, F32), jnp.zeros((1, DV), F32))
-    else:
-        before = pieces_of(prefix_ref[SLICE:, :])
-    bring, hold, small = chain_of(got, before)
+    return wide(jnp.where(later, take, keep), DV), wide(jnp.where(later, keep, take), DV), small
+
+
+def brought(later, got_ref, before):
+    bring, hold, small = chain_of(pieces_of(got_ref[:, SLICE:]), before)
     bring, hold = jnp.where(later, bring, 0.0), jnp.where(later, hold, 1.0)
-    for at in range(0, SLICE, ROWS):
-        here = slice(at, at + ROWS)
-        memory = bring * got_ref[here, :]
-        if prefix_ref is not None:
-            memory = memory + hold * prefix_ref[here, :]
-        new_prefix[here, :] = memory
-    new_prefix[SLICE:, :] = tail_of(*[jnp.where(later, n, o) for n, o in zip(small, before)])
+    return wide(bring, DV), wide(hold, DV), [jnp.where(later, n, o) for n, o in zip(small, before)]
 
 
 def later_of(z, bit):
@@ -258,11 +252,26 @@
 
 
 def first_round_kernel(total_ref, got_ref, after_ref, new_total, new_prefix):
-    merge(later_of(place_of("ctx_0"), 0), total_ref, got_ref, None, new_total, new_prefix)
+    later = later_of(place_of("ctx_0"), 0)
+    f_own, f_got, total = merged(later, total_ref, got_ref)
+    nothing = (jnp.zeros((2, LANES), F32), jnp.full((1, LANES), NEG, F32), jnp.zeros((1, LANES), F32))
+    bring, _, prefix = brought(later, got_ref, nothing)
+    for here in spans():
+        new_total[:, here] = f_own * total_ref[:, here] + f_got * got_ref[:, here]
+        new_prefix[:, here] = bring * got_ref[:, here]
+    new_total[:, SLICE:] = tail_of(*total)
+    new_prefix[:, SLICE:] = tail_of(*prefix)
 
 
 def next_round_kernel(total_ref, got_ref, prefix_ref, after_ref, new_total, new_prefix):
-    merge(later_of(place_of("ctx_0"), 1), total_ref, got_ref, prefix_ref, new_total, new_prefix)
+    later = later_of(place_of("ctx_0"), 1)
+    f_own, f_got, total = merged(later, total_ref, got_ref)
+    bring, hold, prefix = brought(later, got_ref, pieces_of(prefix_ref[:, SLICE:]))
+    for here in spans():
+        new_total[:, here] = f_own * total_ref[:, here] + f_got * got_ref[:, here]
+        new_prefix[:, here] = bring * got_ref[:, here] + hold * prefix_ref[:, here]
+    new_total[:, SLICE:] = tail_of(*total)
+    new_prefix[:, SLICE:] = tail_of(*prefix)
 
 
 def round_of(kernel, *args):
@@ -270,7 +279,7 @@
         kernel,
         in_specs=[VMEM] * (len(args) - 1) + [ANY],
         out_specs=[VMEM] * 2,
-        out_shape=[jax.ShapeDtypeStruct((SENT, DV), F32)] * 2,
+        out_shape=[jax.ShapeDtypeStruct((ROWS, SENT), F32)] * 2,
         compiler_params=pltpu.CompilerParams(vmem_limit_bytes=4 * MIB),
         cost_estimate=pl.CostEstimate(flops=1_000_000, bytes_accessed=MIB, transcendentals=0),
         name="merge_round",
@@ -280,23 +289,19 @@
 def spread_kernel(got_ref, prefix_ref, all_ref, after_ref, own_ref, one_ref, two_ref, three_ref, mine_ref, out_ref):
     x = place_of("ctx_1")
     later = later_of(place_of("ctx_0"), 2)
-    before = pieces_of(prefix_ref[SLICE:, :])
-    bring, hold, small = chain_of(pieces_of(got_ref[SLICE:, :]), before)
-    bring, hold = jnp.where(later, bring, 0.0), jnp.where(later, hold, 1.0)
-    small = [jnp.where(later, n, o) for n, o in zip(small, before)]
+    bring, hold, small = brought(later, got_ref, pieces_of(prefix_ref[:, SLICE:]))
     mine = small
     factors = []
     for j in range(XS - 1):
-        keep, take, small = chain_of(small, pieces_of(all_ref[j, SLICE:, :]))
+        keep, take, small = chain_of(small, pieces_of(all_ref[j, :, SLICE:]))
         mine = [jnp.where(x == j + 1, n, o) for n, o in zip(small, mine)]
-        factors.append((keep, take))
-    for at in range(0, SLICE, ROWS):
-        here = slice(at, at + ROWS)
-        memory = bring * got_ref[here, :] + hold * prefix_ref[here, :]
-        out_ref[0, here, :] = memory
+        factors.append((wide(keep, DV), wide(take, DV)))
+    for z, here in enumerate(spans()):
+        memory = bring * got_ref[:, here] + hold * prefix_ref[:, here]
+        out_ref[0, z] = memory
         for j, (keep, take) in enumerate(factors):
-            memory = keep * memory + take * all_ref[j, here, :]
-            out_ref[j + 1, here, :] = memory
+            memory = keep * memory + take * all_ref[j, :, here]
+            out_ref[j + 1, z] = memory
     for k, ref in enumerate((own_ref, one_ref, two_ref, three_ref)):
         ref[...] = out_ref[pl.ds(lax.rem(x + k, XS), 1)].reshape(ZS, ROWS, DV)
     mine_ref[...] = tail_of(*mine)
@@ -307,8 +312,8 @@
         spread_kernel,
         in_specs=[VMEM] * 3 + [ANY],
         out_specs=[VMEM] * 5,
-        out_shape=[jax.ShapeDtypeStruct((ZS, ROWS, DV), F32)] * 4 + [jax.ShapeDtypeStruct((8, DV), F32)],
-        scratch_shapes=[pltpu.VMEM((XS, SLICE, DV), F32)],
+        out_shape=[jax.ShapeDtypeStruct((ZS, ROWS, DV), F32)] * 4 + [jax.ShapeDtypeStruct((8, LANES), F32)],
+        scratch_shapes=[pltpu.VMEM((XS, ZS, ROWS, DV), F32)],
         compiler_params=pltpu.CompilerParams(vmem_limit_bytes=4 * MIB),
         cost_estimate=pl.CostEstimate(flops=1_000_000, bytes_accessed=2 * MIB, transcendentals=0),
         name="spread_prefixes",
@@ -424,18 +429,14 @@
 def scale_kernel(table_ref, mine_ref, q_ref, total_ref, got_ref, *refs):
     dens, (kept_ref, carried_ref, close_ref, norm_ref, top_ref) = refs[:-5], refs[-5:]
     z = place_of("ctx_0")
-    later = later_of(z, 2)
-    here = pl.ds(pl.multiple_of(z * ROWS, ROWS), ROWS)
-    own, got = pieces_of(total_ref[SLICE:, :]), pieces_of(got_ref[SLICE:, :])
-    first = [jnp.where(later, g, o) for g, o in zip(got, own)]
-    second = [jnp.where(later, o, g) for g, o in zip(got, own)]
-    keep, take, (end_norm, end_top, _) = chain_of(first, second)
-    f_own, f_got = jnp.where(later, take, keep), jnp.where(later, keep, take)
-    close_ref[0] = f_own * total_ref[here, :] + f_got * got_ref[here, :]
-    norm_ref[...] = end_norm[:, :DQK]
-    top_ref[...] = end_top[:, :LANES]
+    here = pl.ds(pl.multiple_of(z * DV, DV), DV)
+    f_own, f_got, (end_norm, end_top, _) = merged(later_of(z, 2), total_ref, got_ref)
+    close_ref[0] = f_own * total_ref[:, here] + f_got * got_ref[:, here]
+    norm_ref[:, :LANES] = end_norm[0:1]
+    norm_ref[:, LANES:] = end_norm[1:2]
+    top_ref[...] = end_top
     norm, log_in, _ = pieces_of(mine_ref)
-    norm, log_in = norm[:, :DQK], log_in[:, :LANES]
+    norm = jnp.concatenate([norm[0:1], norm[1:2]], axis=1)
     place = {i: (dens[n], m) for n, blocks in enumerate(PARTS) for m, i in enumerate(blocks)}
     for i in range(BLOCKS):
         den_ref, m = place[i]

time: 60.8 us -> 56.6 us (0.931)
  waiting for transfers between devices: 17.3 us -> 14.3 us
  starting transfers between devices: 26.7 us -> 25.3 us
    ppermute x6, waiting for transfers between devices: 4.67 us -> 2.29 us  [around(): lax.ppermute(parts[k], 'ctx_1', [(i, (i + k) % XS) for i in range(XS)])]
    ppermute x6, starting transfers between devices: 12.6 us -> 11.1 us  [around(): lax.ppermute(parts[k], 'ctx_1', [(i, (i + k) % XS) for i in range(XS)])]
    ppermute x3, waiting for transfers between devices: 9.28 us -> 8.58 us  [swapped(): return lax.ppermute(x, 'ctx_0', [(i, partner(i)) for i in range(ZS)])]
  transfers between devices with their start and end apart: 10 -> 10, of which waited for: 6 -> 6; matrix products, arithmetic and copies ran while one was open for 0% -> 0% of each run, Pallas kernels for 18% -> 20%
where the time goes in v4:
time: 56.6 us; the launch traced here: 56.1 us
  starting transfers between devices  25.3 us (45%)
  Pallas kernels  15.9 us (28%)
  waiting for transfers between devices  14.3 us (25%)
  between operations  0.72 us (1%)
    ppermute x6, starting transfers between devices, around(): lax.ppermute(parts[k], 'ctx_1', [(i, (i + k) % XS) for i in range(XS)])  11.1 us
    ppermute x3, starting transfers between devices, swapped(): return lax.ppermute(x, 'ctx_0', [(i, partner(i)) for i in range(ZS)])  9.67 us
    ppermute x3, waiting for transfers between devices, swapped(): return lax.ppermute(x, 'ctx_0', [(i, partner(i)) for i in range(ZS)])  8.58 us
    pallas_call x3, Pallas kernels, local(): pl.pallas_call(functools.partial(first_kernel if first else local_kernel,...  7.34 us
    all_to_all x1, starting transfers between devices, exchanged(): return lax.all_to_all(x, axis, split_axis=0, concat_axis=0, tiled=True)  4.48 us
    all_to_all x1, waiting for transfers between devices, exchanged(): return lax.all_to_all(x, axis, split_axis=0, concat_axis=0, tiled=True)  3.38 us
    ppermute x6, waiting for transfers between devices, around(): lax.ppermute(parts[k], 'ctx_1', [(i, (i + k) % XS) for i in range(XS)])  2.29 us
    pallas_call x1, Pallas kernels, turned(): pl.pallas_call(turned_kernel, in_specs=[HBM] * 2, out_specs=[VMEM] * 2, o...  1.97 us
  transfers between devices with their start and end apart: 10, of which 6 were waited for; matrix products, arithmetic and copies ran while one was open for 0% of the time, Pallas kernels for 20%

profile of v4, /device:TPU:32, one launch (start us, length us, event | category | flops | bytes accessed | tf_op | source)
XLA Modules:
  0.0 56.1 jit_solution(8036944150346181144)
XLA Ops:
  0.6 1.5 %gate_sums.1 = f32[8,2,256]{2,1,0:T(2,128)} custom-call(f32[2,8,256]{2,1,0:T(8,128)} %g_hbm.1), custom_call_target="tpu_custom_call" | custom-call | tf_op jit(solution)/shard_map/gate_sums/pallas_call | solution.py:85
  2.1 4.5 %all-to-all-start = ((f32[8,2,256]{2,1,0:T(2,128)}), f32[8,2,256]{2,1,0:T(2,128)S(1)}, u32[]{:S(2)}, u32[]{:S(2)}) async-start(f32[8,2,256]{2,1,0:T(2,128)} %gate_sums.1), calls=%async_computation | async-start | bytes 32768 | tf_op jit(solution)/shard_map/all_to_all | solution.py:512
  6.6 2.0 %turn_keys.1 = (bf16[256,2048]{1,0:T(8,128)(2,1)S(1)}, bf16[2048,512]{1,0:T(8,128)(2,1)S(1)}) custom-call(bf16[2048,256]{1,0:T(8,128)(2,1)} %k_hbm.3, bf16[2048,512]{1,0:T(8,128)(2,1)} %v_hbm.1), custom_call_target="tpu_custom_call" | custom-call | bytes 4194304 | tf_op jit(solution)/shard_map/turn_keys/pallas_call | solution.py:112
  8.6 3.4 %all-to-all-done.g_ref = f32[8,2,256]{2,1,0:T(2,128)S(1)} async-done(((f32[8,2,256]{2,1,0:T(2,128)}), f32[8,2,256]{2,1,0:T(2,128)S(1)}, u32[]{:S(2)}, u32[]{:S(2)}) %all-to-all-start) | async-done | bytes 16416 | tf_op jit(solution)/shard_map/all_to_all | solution.py:512
  12.0 1.2 %shard_state.1 = (f32[8,4224]{1,0:T(8,128)S(1)}, f32[8,4224]{1,0:T(8,128)S(1)}, f32[8,4224]{1,0:T(8,128)S(1)}, f32[8,4224]{1,0:T(8,128)S(1)}, f32[8,128]{1,0:T(8,128)S(1)}) custom-call(f32[8,2,256]{2,1,0:T(2,128)S(1)} %all-to-all-done.g_ref, bf16[256,2048]{1,0:T(8,128)(2,1)S(1)} %get-tuple-element.36.kt_ref, bf16[2048,512]{1,0:T(8,128)(2,1)S(1)} %get-tuple-element.37.v_ref), custom_call_target="tpu_custom_call" | custom-call | flops 600000000 | bytes 5242880 | tf_op jit(solution)/shard_map/shard_state/pallas_call | solution.py:165
  13.2 1.6 %collective-permute-start = (f32[8,4224]{1,0:T(8,128)S(1)}, f32[8,4224]{1,0:T(8,128)S(1)}, u32[]{:S(2)}, u32[]{:S(2)}) collective-permute-start(f32[8,4224]{1,0:T(8,128)S(1)} %get-tuple-element.41), channel_id=1, source_target_pairs={{0,8},{8,16},{16,24},{24,0},{1,9},{9,17},{17,25},{25,1},{2,10},{10... | collective-permute-start | bytes 405512 | tf_op jit(solution)/shard_map/ppermute | solution.py:518
  14.8 2.7 %collective-permute-start.1 = (f32[8,4224]{1,0:T(8,128)S(1)}, f32[8,4224]{1,0:T(8,128)S(1)}, u32[]{:S(2)}, u32[]{:S(2)}) collective-permute-start(f32[8,4224]{1,0:T(8,128)S(1)} %get-tuple-element.42), channel_id=1, source_target_pairs={{0,16},{8,24},{16,0},{24,8},{1,17},{9,25},{17,1},{25,9},{2,18},{10... | collective-permute-start | bytes 405512 | tf_op jit(solution)/shard_map/ppermute | solution.py:518
  17.5 1.4 %collective-permute-start.2 = (f32[8,4224]{1,0:T(8,128)S(1)}, f32[8,4224]{1,0:T(8,128)S(1)}, u32[]{:S(2)}, u32[]{:S(2)}) collective-permute-start(f32[8,4224]{1,0:T(8,128)S(1)} %get-tuple-element.43), channel_id=1, source_target_pairs={{0,24},{8,0},{16,8},{24,16},{1,25},{9,1},{17,9},{25,17},{2,26},{10... | collective-permute-start | bytes 405512 | tf_op jit(solution)/shard_map/ppermute | solution.py:518
  18.9 4.0 %within_shard.3 = (f32[512,512]{1,0:T(8,128)S(1)}, f32[512,128]{1,0:T(8,128)S(1)}, f32[12,512]{1,0:T(8,128)S(1)}, bf16[2048,256]{1,0:T(8,128)(2,1)S(1)}, bf16[2048,256]{1,0:T(8,128)(2,1)S(1)}) custom-call(f32[8,2,256]{2,1,0:T(2,128)S(1)} %all-to-all-done.g_ref, f32[8,128]{1,0:T(8,128)S(1)} %get-tuple-element.38.tick_ref, bf16[2048,256]{1,0:T(8,128)(2,1)} %q_hbm.1, ...), custom_call_target="tpu_custom_call" | custom-call | flops 3200000000 | bytes 4194304 | tf_op jit(solution)/shard_map/within_shard/pallas_call | solution.py:417
  23.0 0.7 %collective-permute-done.1.two_ref = f32[8,4224]{1,0:T(8,128)S(1)} collective-permute-done((f32[8,4224]{1,0:T(8,128)S(1)}, f32[8,4224]{1,0:T(8,128)S(1)}, u32[]{:S(2)}, u32[]{:S(2)}) %collective-permute-start.1) | collective-permute-done | bytes 135200 | tf_op jit(solution)/shard_map/ppermute | solution.py:518
  23.8 0.3 collective-permute-start.3
  24.0 4.8 %collective-permute-done.3.got_ref = f32[8,4224]{1,0:T(8,128)S(1)} collective-permute-done((f32[8,4224]{1,0:T(8,128)S(1)}, f32[8,4224]{1,0:T(8,128)S(1)}, u32[]{:S(2)}, u32[]{:S(2)}) %collective-permute-start.3) | collective-permute-done | bytes 135200 | tf_op jit(solution)/shard_map/ppermute | solution.py:523
  28.9 3.4 %collective-permute-start.4 = (f32[8,4224]{1,0:T(8,128)S(1)}, f32[8,4224]{1,0:T(8,128)S(1)}, u32[]{:S(2)}, u32[]{:S(2)}) collective-permute-start(f32[8,4224]{1,0:T(8,128)S(1)} %get-tuple-element.46.total_ref), channel_id=1, source_target_pairs={{0,64},{32,96},{64,0},{96,32},{128,192},{160,224},{192,128},{224,1... | collective-permute-start | bytes 405512 | tf_op jit(solution)/shard_map/ppermute | solution.py:523
  32.3 1.4 %within_shard.4 = (f32[1024,512]{1,0:T(8,128)S(1)}, f32[1024,128]{1,0:T(8,128)S(1)}) custom-call(f32[12,512]{1,0:T(8,128)S(1)} %get-tuple-element.48.table_ref, f32[8,4224]{1,0:T(8,128)S(1)} %get-tuple-element.47.tick_ref.prefix_ref, bf16[2048,256]{1,0:T(8,128)(2,1)S(1)} %get-tuple-element.39.q_ref, bf16[2048,256]{1,0:T(8,128)(2,1)S(1)} %get-tuple-element.49.k_ref, ...), custom_call_target="tpu_custom_call" | custom-call | flops 2400000000 | bytes 3145728 | tf_op jit(solution)/shard_map/within_shard/pallas_call | solution.py:417
  33.7 2.1 %collective-permute-done.4.got_ref = f32[8,4224]{1,0:T(8,128)S(1)} collective-permute-done((f32[8,4224]{1,0:T(8,128)S(1)}, f32[8,4224]{1,0:T(8,128)S(1)}, u32[]{:S(2)}, u32[]{:S(2)}) %collective-permute-start.4) | collective-permute-done | bytes 135200 | tf_op jit(solution)/shard_map/ppermute | solution.py:523
  35.9 6.1 %collective-permute-start.5 = (f32[8,4224]{1,0:T(8,128)S(1)}, f32[8,4224]{1,0:T(8,128)S(1)}, u32[]{:S(2)}, u32[]{:S(2)}) collective-permute-start(f32[8,4224]{1,0:T(8,128)S(1)} %get-tuple-element.51.total_ref), channel_id=1, source_target_pairs={{0,192},{32,224},{64,160},{96,128},{128,96},{160,64},{192,0},{224,... | collective-permute-start | bytes 405512 | tf_op jit(solution)/shard_map/ppermute | solution.py:523
  41.9 1.9 %within_shard.5 = (f32[512,512]{1,0:T(8,128)S(1)}, f32[512,128]{1,0:T(8,128)S(1)}) custom-call(f32[12,512]{1,0:T(8,128)S(1)} %get-tuple-element.48.table_ref, f32[8,4224]{1,0:T(8,128)S(1)} %get-tuple-element.52.tick_ref.prefix_ref, bf16[2048,256]{1,0:T(8,128)(2,1)S(1)} %get-tuple-element.39.q_ref, bf16[2048,256]{1,0:T(8,128)(2,1)S(1)} %get-tuple-element.49.k_ref, ...), custom_call_target="tpu_custom_call" | custom-call | flops 2400000000 | bytes 3145728 | tf_op jit(solution)/shard_map/within_shard/pallas_call | solution.py:417
  43.8 1.7 %collective-permute-done.5.got_ref = f32[8,4224]{1,0:T(8,128)S(1)} collective-permute-done((f32[8,4224]{1,0:T(8,128)S(1)}, f32[8,4224]{1,0:T(8,128)S(1)}, u32[]{:S(2)}, u32[]{:S(2)}) %collective-permute-start.5) | collective-permute-done | bytes 135200 | tf_op jit(solution)/shard_map/ppermute | solution.py:523
  45.6 2.3 %collective-permute-start.6 = (f32[8,8,512]{2,1,0:T(8,128)S(1)}, f32[8,8,512]{2,1,0:T(8,128)S(1)}, u32[]{:S(2)}, u32[]{:S(2)}) collective-permute-start(f32[8,8,512]{2,1,0:T(8,128)S(1)} %get-tuple-element.56), channel_id=1, source_target_pairs={{0,8},{8,16},{16,24},{24,0},{1,9},{9,17},{17,25},{25,1},{2,10},{10... | collective-permute-start | bytes 393224 | tf_op jit(solution)/shard_map/ppermute | solution.py:518
  48.0 1.5 %collective-permute-start.7 = (f32[8,8,512]{2,1,0:T(8,128)S(1)}, f32[8,8,512]{2,1,0:T(8,128)S(1)}, u32[]{:S(2)}, u32[]{:S(2)}) collective-permute-start(f32[8,8,512]{2,1,0:T(8,128)S(1)} %get-tuple-element.57), channel_id=1, source_target_pairs={{0,16},{8,24},{16,0},{24,8},{1,17},{9,25},{17,1},{25,9},{2,18},{10... | collective-permute-start | bytes 393224 | tf_op jit(solution)/shard_map/ppermute | solution.py:518
  49.4 1.6 %collective-permute-start.8 = (f32[8,8,512]{2,1,0:T(8,128)S(1)}, f32[8,8,512]{2,1,0:T(8,128)S(1)}, u32[]{:S(2)}, u32[]{:S(2)}) collective-permute-start(f32[8,8,512]{2,1,0:T(8,128)S(1)} %get-tuple-element.58), channel_id=1, source_target_pairs={{0,24},{8,0},{16,8},{24,16},{1,25},{9,1},{17,9},{25,17},{2,26},{10... | collective-permute-start | bytes 393224 | tf_op jit(solution)/shard_map/ppermute | solution.py:518
  51.0 1.8 %row_scales.1 = (f32[2048,128]{1,0:T(8,128)S(1)}, f32[2048,128]{1,0:T(8,128)S(1)}, f32[1,8,512]{2,1,0:T(8,128)}, f32[1,256]{1,0:T(1,128)}, f32[1,128]{1,0:T(1,128)}) custom-call(f32[12,512]{1,0:T(8,128)S(1)} %get-tuple-element.48.table_ref, f32[8,128]{1,0:T(8,128)S(1)} %get-tuple-element.59.mine_ref, bf16[2048,256]{1,0:T(8,128)(2,1)S(1)} %get-tuple-element.39.q_ref, ...), custom_call_target="tpu_custom_call" | custom-call | flops 600000000 | bytes 4194304 | tf_op jit(solution)/shard_map/row_scales/pallas_call | solution.py:456
  52.8 1.6 %collective-permute-done.7.two_ref = f32[8,8,512]{2,1,0:T(8,128)S(1)} collective-permute-done((f32[8,8,512]{2,1,0:T(8,128)S(1)}, f32[8,8,512]{2,1,0:T(8,128)S(1)}, u32[]{:S(2)}, u32[]{:S(2)}) %collective-permute-start.7) | collective-permute-done | bytes 131104 | tf_op jit(solution)/shard_map/ppermute | solution.py:518
  54.4 1.7 %join_memory.1 = bf16[2048,512]{1,0:T(8,128)(2,1)} custom-call(bf16[2048,256]{1,0:T(8,128)(2,1)S(1)} %get-tuple-element.39.q_ref, f32[8,8,512]{2,1,0:T(8,128)S(1)} %get-tuple-element.55.own_ref, f32[8,8,512]{2,1,0:T(8,128)S(1)} %collective-permute-done.6.one_ref, f32[8,8,512]{2,1,0:T(8,128)S(1)} %collective-permute-done.7.two_ref, ...), custom_call_target="tpu_custom_call" | custom-call | flops 600000000 | bytes 9437184 | tf_op jit(solution)/shard_map/join_memory/pallas_call | solution.py:494
  (8 shorter events, 0.4 us)
Async XLA Ops:
  2.1 9.8 %all-to-all-start = ((f32[8,2,256]{2,1,0:T(2,128)}), f32[8,2,256]{2,1,0:T(2,128)S(1)}, u32[]{:S(2)}, u32[]{:S(2)}) async-start(f32[8,2,256]{2,1,0:T(2,128)} %gate_sums.1), calls=%async_computation | async-start | bytes 32768 | tf_op jit(solution)/shard_map/all_to_all | solution.py:512
  13.2 9.8 %collective-permute-start = (f32[8,4224]{1,0:T(8,128)S(1)}, f32[8,4224]{1,0:T(8,128)S(1)}, u32[]{:S(2)}, u32[]{:S(2)}) collective-permute-start(f32[8,4224]{1,0:T(8,128)S(1)} %get-tuple-element.41), channel_id=1, source_target_pairs={{0,8},{8,16},{16,24},{24,0},{1,9},{9,17},{17,25},{25,1},{2,10},{10... | collective-permute-start | bytes 405512 | tf_op jit(solution)/shard_map/ppermute | solution.py:518
  14.8 8.9 %collective-permute-start.1 = (f32[8,4224]{1,0:T(8,128)S(1)}, f32[8,4224]{1,0:T(8,128)S(1)}, u32[]{:S(2)}, u32[]{:S(2)}) collective-permute-start(f32[8,4224]{1,0:T(8,128)S(1)} %get-tuple-element.42), channel_id=1, source_target_pairs={{0,16},{8,24},{16,0},{24,8},{1,17},{9,25},{17,1},{25,9},{2,18},{10... | collective-permute-start | bytes 405512 | tf_op jit(solution)/shard_map/ppermute | solution.py:518
  17.5 6.2 %collective-permute-start.2 = (f32[8,4224]{1,0:T(8,128)S(1)}, f32[8,4224]{1,0:T(8,128)S(1)}, u32[]{:S(2)}, u32[]{:S(2)}) collective-permute-start(f32[8,4224]{1,0:T(8,128)S(1)} %get-tuple-element.43), channel_id=1, source_target_pairs={{0,24},{8,0},{16,8},{24,16},{1,25},{9,1},{17,9},{25,17},{2,26},{10... | collective-permute-start | bytes 405512 | tf_op jit(solution)/shard_map/ppermute | solution.py:518
  23.8 5.1 %collective-permute-start.3 = (f32[8,4224]{1,0:T(8,128)S(1)}, f32[8,4224]{1,0:T(8,128)S(1)}, u32[]{:S(2)}, u32[]{:S(2)}) collective-permute-start(f32[8,4224]{1,0:T(8,128)S(1)} %get-tuple-element.45.total_ref), channel_id=1, source_target_pairs={{0,32},{32,0},{64,96},{96,64},{128,160},{160,128},{192,224},{224,1... | collective-permute-start | bytes 405512 | tf_op jit(solution)/shard_map/ppermute | solution.py:523
  28.9 6.9 %collective-permute-start.4 = (f32[8,4224]{1,0:T(8,128)S(1)}, f32[8,4224]{1,0:T(8,128)S(1)}, u32[]{:S(2)}, u32[]{:S(2)}) collective-permute-start(f32[8,4224]{1,0:T(8,128)S(1)} %get-tuple-element.46.total_ref), channel_id=1, source_target_pairs={{0,64},{32,96},{64,0},{96,32},{128,192},{160,224},{192,128},{224,1... | collective-permute-start | bytes 405512 | tf_op jit(solution)/shard_map/ppermute | solution.py:523
  35.9 9.6 %collective-permute-start.5 = (f32[8,4224]{1,0:T(8,128)S(1)}, f32[8,4224]{1,0:T(8,128)S(1)}, u32[]{:S(2)}, u32[]{:S(2)}) collective-permute-start(f32[8,4224]{1,0:T(8,128)S(1)} %get-tuple-element.51.total_ref), channel_id=1, source_target_pairs={{0,192},{32,224},{64,160},{96,128},{128,96},{160,64},{192,0},{224,... | collective-permute-start | bytes 405512 | tf_op jit(solution)/shard_map/ppermute | solution.py:523
  45.6 7.2 %collective-permute-start.6 = (f32[8,8,512]{2,1,0:T(8,128)S(1)}, f32[8,8,512]{2,1,0:T(8,128)S(1)}, u32[]{:S(2)}, u32[]{:S(2)}) collective-permute-start(f32[8,8,512]{2,1,0:T(8,128)S(1)} %get-tuple-element.56), channel_id=1, source_target_pairs={{0,8},{8,16},{16,24},{24,0},{1,9},{9,17},{17,25},{25,1},{2,10},{10... | collective-permute-start | bytes 393224 | tf_op jit(solution)/shard_map/ppermute | solution.py:518
  48.0 6.5 %collective-permute-start.7 = (f32[8,8,512]{2,1,0:T(8,128)S(1)}, f32[8,8,512]{2,1,0:T(8,128)S(1)}, u32[]{:S(2)}, u32[]{:S(2)}) collective-permute-start(f32[8,8,512]{2,1,0:T(8,128)S(1)} %get-tuple-element.57), channel_id=1, source_target_pairs={{0,16},{8,24},{16,0},{24,8},{1,17},{9,25},{17,1},{25,9},{2,18},{10... | collective-permute-start | bytes 393224 | tf_op jit(solution)/shard_map/ppermute | solution.py:518
  49.4 5.0 %collective-permute-start.8 = (f32[8,8,512]{2,1,0:T(8,128)S(1)}, f32[8,8,512]{2,1,0:T(8,128)S(1)}, u32[]{:S(2)}, u32[]{:S(2)}) collective-permute-start(f32[8,8,512]{2,1,0:T(8,128)S(1)} %get-tuple-element.58), channel_id=1, source_target_pairs={{0,24},{8,0},{16,8},{24,16},{1,25},{9,1},{17,9},{25,17},{2,26},{10... | collective-permute-start | bytes 393224 | tf_op jit(solution)/shard_map/ppermute | solution.py:518

commit v5 on v4

--- a/solution.py
+++ b/solution.py
@@ -296,14 +296,14 @@
         keep, take, small = chain_of(small, pieces_of(all_ref[j, :, SLICE:]))
         mine = [jnp.where(x == j + 1, n, o) for n, o in zip(small, mine)]
         factors.append((wide(keep, DV), wide(take, DV)))
-    for z, here in enumerate(spans()):
+    for here in spans():
         memory = bring * got_ref[:, here] + hold * prefix_ref[:, here]
-        out_ref[0, z] = memory
+        out_ref[0, :, here] = memory
         for j, (keep, take) in enumerate(factors):
             memory = keep * memory + take * all_ref[j, :, here]
-            out_ref[j + 1, z] = memory
+            out_ref[j + 1, :, here] = memory
     for k, ref in enumerate((own_ref, one_ref, two_ref, three_ref)):
-        ref[...] = out_ref[pl.ds(lax.rem(x + k, XS), 1)].reshape(ZS, ROWS, DV)
+        ref[...] = out_ref[pl.ds(lax.rem(x + k, XS), 1)].reshape(ROWS, SLICE)
     mine_ref[...] = tail_of(*mine)
 
 
@@ -312,8 +312,8 @@
         spread_kernel,
         in_specs=[VMEM] * 3 + [ANY],
         out_specs=[VMEM] * 5,
-        out_shape=[jax.ShapeDtypeStruct((ZS, ROWS, DV), F32)] * 4 + [jax.ShapeDtypeStruct((8, LANES), F32)],
-        scratch_shapes=[pltpu.VMEM((XS, ZS, ROWS, DV), F32)],
+        out_shape=[jax.ShapeDtypeStruct((ROWS, SLICE), F32)] * 4 + [jax.ShapeDtypeStruct((8, LANES), F32)],
+        scratch_shapes=[pltpu.VMEM((XS, ROWS, SLICE), F32)],
         compiler_params=pltpu.CompilerParams(vmem_limit_bytes=4 * MIB),
         cost_estimate=pl.CostEstimate(flops=1_000_000, bytes_accessed=2 * MIB, transcendentals=0),
         name="spread_prefixes",
@@ -474,7 +474,8 @@
     x = place_of("ctx_1")
     for k, ref in enumerate((own_ref, one_ref, two_ref, three_ref)):
         at = lax.rem(x + XS - k, XS)
-        mem_ref[:, pl.ds(at, 1)] = ref[...].reshape(ZS, 1, ROWS, DV)
+        for z, here in enumerate(spans()):
+            mem_ref[z, pl.ds(at, 1)] = ref[:, here].reshape(1, ROWS, DV)
     mem_b_ref[...] = mem_ref[...].reshape(DQK, DV).astype(BF16)
     copies = []
     for n, blocks in enumerate(PARTS):

time: 56.6 us -> 56.6 us (level)
  no operation moved by 1% of the time
where the time goes in v5:
time: 56.6 us; the launch traced here: 56.1 us
  starting transfers between devices  25.3 us (45%)
  Pallas kernels  15.9 us (28%)
  waiting for transfers between devices  14.3 us (25%)
  between operations  0.72 us (1%)
    ppermute x6, starting transfers between devices, around(): lax.ppermute(parts[k], 'ctx_1', [(i, (i + k) % XS) for i in range(XS)])  11.1 us
    ppermute x3, starting transfers between devices, swapped(): return lax.ppermute(x, 'ctx_0', [(i, partner(i)) for i in range(ZS)])  9.67 us
    ppermute x3, waiting for transfers between devices, swapped(): return lax.ppermute(x, 'ctx_0', [(i, partner(i)) for i in range(ZS)])  8.58 us
    pallas_call x3, Pallas kernels, local(): pl.pallas_call(functools.partial(first_kernel if first else local_kernel,...  7.34 us
    all_to_all x1, starting transfers between devices, exchanged(): return lax.all_to_all(x, axis, split_axis=0, concat_axis=0, tiled=True)  4.48 us
    all_to_all x1, waiting for transfers between devices, exchanged(): return lax.all_to_all(x, axis, split_axis=0, concat_axis=0, tiled=True)  3.38 us
    ppermute x6, waiting for transfers between devices, around(): lax.ppermute(parts[k], 'ctx_1', [(i, (i + k) % XS) for i in range(XS)])  2.29 us
    pallas_call x1, Pallas kernels, turned(): pl.pallas_call(turned_kernel, in_specs=[HBM] * 2, out_specs=[VMEM] * 2, o...  1.97 us
  transfers between devices with their start and end apart: 10, of which 6 were waited for; matrix products, arithmetic and copies ran while one was open for 0% of the time, Pallas kernels for 20%

profile of v5, /device:TPU:32, one launch (start us, length us, event | category | flops | bytes accessed | tf_op | source)
XLA Modules:
  0.0 56.1 jit_solution(10558372413901080190)
XLA Ops:
  0.6 1.5 %gate_sums.1 = f32[8,2,256]{2,1,0:T(2,128)} custom-call(f32[2,8,256]{2,1,0:T(8,128)} %g_hbm.1), custom_call_target="tpu_custom_call" | custom-call | tf_op jit(solution)/shard_map/gate_sums/pallas_call | solution.py:85
  2.1 4.5 %all-to-all-start = ((f32[8,2,256]{2,1,0:T(2,128)}), f32[8,2,256]{2,1,0:T(2,128)S(1)}, u32[]{:S(2)}, u32[]{:S(2)}) async-start(f32[8,2,256]{2,1,0:T(2,128)} %gate_sums.1), calls=%async_computation | async-start | bytes 32768 | tf_op jit(solution)/shard_map/all_to_all | solution.py:513
  6.6 2.0 %turn_keys.1 = (bf16[256,2048]{1,0:T(8,128)(2,1)S(1)}, bf16[2048,512]{1,0:T(8,128)(2,1)S(1)}) custom-call(bf16[2048,256]{1,0:T(8,128)(2,1)} %k_hbm.3, bf16[2048,512]{1,0:T(8,128)(2,1)} %v_hbm.1), custom_call_target="tpu_custom_call" | custom-call | bytes 4194304 | tf_op jit(solution)/shard_map/turn_keys/pallas_call | solution.py:112
  8.6 3.4 %all-to-all-done.g_ref = f32[8,2,256]{2,1,0:T(2,128)S(1)} async-done(((f32[8,2,256]{2,1,0:T(2,128)}), f32[8,2,256]{2,1,0:T(2,128)S(1)}, u32[]{:S(2)}, u32[]{:S(2)}) %all-to-all-start) | async-done | bytes 16416 | tf_op jit(solution)/shard_map/all_to_all | solution.py:513
  12.0 1.2 %shard_state.1 = (f32[8,4224]{1,0:T(8,128)S(1)}, f32[8,4224]{1,0:T(8,128)S(1)}, f32[8,4224]{1,0:T(8,128)S(1)}, f32[8,4224]{1,0:T(8,128)S(1)}, f32[8,128]{1,0:T(8,128)S(1)}) custom-call(f32[8,2,256]{2,1,0:T(2,128)S(1)} %all-to-all-done.g_ref, bf16[256,2048]{1,0:T(8,128)(2,1)S(1)} %get-tuple-element.36.kt_ref, bf16[2048,512]{1,0:T(8,128)(2,1)S(1)} %get-tuple-element.37.v_ref), custom_call_target="tpu_custom_call" | custom-call | flops 600000000 | bytes 5242880 | tf_op jit(solution)/shard_map/shard_state/pallas_call | solution.py:165
  13.2 1.6 %collective-permute-start = (f32[8,4224]{1,0:T(8,128)S(1)}, f32[8,4224]{1,0:T(8,128)S(1)}, u32[]{:S(2)}, u32[]{:S(2)}) collective-permute-start(f32[8,4224]{1,0:T(8,128)S(1)} %get-tuple-element.41), channel_id=1, source_target_pairs={{0,8},{8,16},{16,24},{24,0},{1,9},{9,17},{17,25},{25,1},{2,10},{10... | collective-permute-start | bytes 405512 | tf_op jit(solution)/shard_map/ppermute | solution.py:519
  14.8 2.7 %collective-permute-start.1 = (f32[8,4224]{1,0:T(8,128)S(1)}, f32[8,4224]{1,0:T(8,128)S(1)}, u32[]{:S(2)}, u32[]{:S(2)}) collective-permute-start(f32[8,4224]{1,0:T(8,128)S(1)} %get-tuple-element.42), channel_id=1, source_target_pairs={{0,16},{8,24},{16,0},{24,8},{1,17},{9,25},{17,1},{25,9},{2,18},{10... | collective-permute-start | bytes 405512 | tf_op jit(solution)/shard_map/ppermute | solution.py:519
  17.5 1.4 %collective-permute-start.2 = (f32[8,4224]{1,0:T(8,128)S(1)}, f32[8,4224]{1,0:T(8,128)S(1)}, u32[]{:S(2)}, u32[]{:S(2)}) collective-permute-start(f32[8,4224]{1,0:T(8,128)S(1)} %get-tuple-element.43), channel_id=1, source_target_pairs={{0,24},{8,0},{16,8},{24,16},{1,25},{9,1},{17,9},{25,17},{2,26},{10... | collective-permute-start | bytes 405512 | tf_op jit(solution)/shard_map/ppermute | solution.py:519
  18.9 4.0 %within_shard.3 = (f32[512,512]{1,0:T(8,128)S(1)}, f32[512,128]{1,0:T(8,128)S(1)}, f32[12,512]{1,0:T(8,128)S(1)}, bf16[2048,256]{1,0:T(8,128)(2,1)S(1)}, bf16[2048,256]{1,0:T(8,128)(2,1)S(1)}) custom-call(f32[8,2,256]{2,1,0:T(2,128)S(1)} %all-to-all-done.g_ref, f32[8,128]{1,0:T(8,128)S(1)} %get-tuple-element.38.tick_ref, bf16[2048,256]{1,0:T(8,128)(2,1)} %q_hbm.1, ...), custom_call_target="tpu_custom_call" | custom-call | flops 3200000000 | bytes 4194304 | tf_op jit(solution)/shard_map/within_shard/pallas_call | solution.py:417
  23.0 0.7 %collective-permute-done.1.two_ref = f32[8,4224]{1,0:T(8,128)S(1)} collective-permute-done((f32[8,4224]{1,0:T(8,128)S(1)}, f32[8,4224]{1,0:T(8,128)S(1)}, u32[]{:S(2)}, u32[]{:S(2)}) %collective-permute-start.1) | collective-permute-done | bytes 135200 | tf_op jit(solution)/shard_map/ppermute | solution.py:519
  23.8 0.3 collective-permute-start.3
  24.0 4.8 %collective-permute-done.3.got_ref = f32[8,4224]{1,0:T(8,128)S(1)} collective-permute-done((f32[8,4224]{1,0:T(8,128)S(1)}, f32[8,4224]{1,0:T(8,128)S(1)}, u32[]{:S(2)}, u32[]{:S(2)}) %collective-permute-start.3) | collective-permute-done | bytes 135200 | tf_op jit(solution)/shard_map/ppermute | solution.py:524
  28.9 3.4 %collective-permute-start.4 = (f32[8,4224]{1,0:T(8,128)S(1)}, f32[8,4224]{1,0:T(8,128)S(1)}, u32[]{:S(2)}, u32[]{:S(2)}) collective-permute-start(f32[8,4224]{1,0:T(8,128)S(1)} %get-tuple-element.46.total_ref), channel_id=1, source_target_pairs={{0,64},{32,96},{64,0},{96,32},{128,192},{160,224},{192,128},{224,1... | collective-permute-start | bytes 405512 | tf_op jit(solution)/shard_map/ppermute | solution.py:524
  32.3 1.4 %within_shard.4 = (f32[1024,512]{1,0:T(8,128)S(1)}, f32[1024,128]{1,0:T(8,128)S(1)}) custom-call(f32[12,512]{1,0:T(8,128)S(1)} %get-tuple-element.48.table_ref, f32[8,4224]{1,0:T(8,128)S(1)} %get-tuple-element.47.tick_ref.prefix_ref, bf16[2048,256]{1,0:T(8,128)(2,1)S(1)} %get-tuple-element.39.q_ref, bf16[2048,256]{1,0:T(8,128)(2,1)S(1)} %get-tuple-element.49.k_ref, ...), custom_call_target="tpu_custom_call" | custom-call | flops 2400000000 | bytes 3145728 | tf_op jit(solution)/shard_map/within_shard/pallas_call | solution.py:417
  33.7 2.1 %collective-permute-done.4.got_ref = f32[8,4224]{1,0:T(8,128)S(1)} collective-permute-done((f32[8,4224]{1,0:T(8,128)S(1)}, f32[8,4224]{1,0:T(8,128)S(1)}, u32[]{:S(2)}, u32[]{:S(2)}) %collective-permute-start.4) | collective-permute-done | bytes 135200 | tf_op jit(solution)/shard_map/ppermute | solution.py:524
  35.9 6.1 %collective-permute-start.5 = (f32[8,4224]{1,0:T(8,128)S(1)}, f32[8,4224]{1,0:T(8,128)S(1)}, u32[]{:S(2)}, u32[]{:S(2)}) collective-permute-start(f32[8,4224]{1,0:T(8,128)S(1)} %get-tuple-element.51.total_ref), channel_id=1, source_target_pairs={{0,192},{32,224},{64,160},{96,128},{128,96},{160,64},{192,0},{224,... | collective-permute-start | bytes 405512 | tf_op jit(solution)/shard_map/ppermute | solution.py:524
  41.9 1.9 %within_shard.5 = (f32[512,512]{1,0:T(8,128)S(1)}, f32[512,128]{1,0:T(8,128)S(1)}) custom-call(f32[12,512]{1,0:T(8,128)S(1)} %get-tuple-element.48.table_ref, f32[8,4224]{1,0:T(8,128)S(1)} %get-tuple-element.52.tick_ref.prefix_ref, bf16[2048,256]{1,0:T(8,128)(2,1)S(1)} %get-tuple-element.39.q_ref, bf16[2048,256]{1,0:T(8,128)(2,1)S(1)} %get-tuple-element.49.k_ref, ...), custom_call_target="tpu_custom_call" | custom-call | flops 2400000000 | bytes 3145728 | tf_op jit(solution)/shard_map/within_shard/pallas_call | solution.py:417
  43.8 1.7 %collective-permute-done.5.got_ref = f32[8,4224]{1,0:T(8,128)S(1)} collective-permute-done((f32[8,4224]{1,0:T(8,128)S(1)}, f32[8,4224]{1,0:T(8,128)S(1)}, u32[]{:S(2)}, u32[]{:S(2)}) %collective-permute-start.5) | collective-permute-done | bytes 135200 | tf_op jit(solution)/shard_map/ppermute | solution.py:524
  45.6 2.3 %collective-permute-start.6 = (f32[8,4096]{1,0:T(8,128)S(1)}, f32[8,4096]{1,0:T(8,128)S(1)}, u32[]{:S(2)}, u32[]{:S(2)}) collective-permute-start(f32[8,4096]{1,0:T(8,128)S(1)} %get-tuple-element.56), channel_id=1, source_target_pairs={{0,8},{8,16},{16,24},{24,0},{1,9},{9,17},{17,25},{25,1},{2,10},{10... | collective-permute-start | bytes 393224 | tf_op jit(solution)/shard_map/ppermute | solution.py:519
  48.0 1.5 %collective-permute-start.7 = (f32[8,4096]{1,0:T(8,128)S(1)}, f32[8,4096]{1,0:T(8,128)S(1)}, u32[]{:S(2)}, u32[]{:S(2)}) collective-permute-start(f32[8,4096]{1,0:T(8,128)S(1)} %get-tuple-element.57), channel_id=1, source_target_pairs={{0,16},{8,24},{16,0},{24,8},{1,17},{9,25},{17,1},{25,9},{2,18},{10... | collective-permute-start | bytes 393224 | tf_op jit(solution)/shard_map/ppermute | solution.py:519
  49.4 1.6 %collective-permute-start.8 = (f32[8,4096]{1,0:T(8,128)S(1)}, f32[8,4096]{1,0:T(8,128)S(1)}, u32[]{:S(2)}, u32[]{:S(2)}) collective-permute-start(f32[8,4096]{1,0:T(8,128)S(1)} %get-tuple-element.58), channel_id=1, source_target_pairs={{0,24},{8,0},{16,8},{24,16},{1,25},{9,1},{17,9},{25,17},{2,26},{10... | collective-permute-start | bytes 393224 | tf_op jit(solution)/shard_map/ppermute | solution.py:519
  51.0 1.8 %row_scales.1 = (f32[2048,128]{1,0:T(8,128)S(1)}, f32[2048,128]{1,0:T(8,128)S(1)}, f32[1,8,512]{2,1,0:T(8,128)}, f32[1,256]{1,0:T(1,128)}, f32[1,128]{1,0:T(1,128)}) custom-call(f32[12,512]{1,0:T(8,128)S(1)} %get-tuple-element.48.table_ref, f32[8,128]{1,0:T(8,128)S(1)} %get-tuple-element.59.mine_ref, bf16[2048,256]{1,0:T(8,128)(2,1)S(1)} %get-tuple-element.39.q_ref, ...), custom_call_target="tpu_custom_call" | custom-call | flops 600000000 | bytes 4194304 | tf_op jit(solution)/shard_map/row_scales/pallas_call | solution.py:456
  52.8 1.6 %collective-permute-done.7.two_ref = f32[8,4096]{1,0:T(8,128)S(1)} collective-permute-done((f32[8,4096]{1,0:T(8,128)S(1)}, f32[8,4096]{1,0:T(8,128)S(1)}, u32[]{:S(2)}, u32[]{:S(2)}) %collective-permute-start.7) | collective-permute-done | bytes 131104 | tf_op jit(solution)/shard_map/ppermute | solution.py:519
  54.4 1.7 %join_memory.1 = bf16[2048,512]{1,0:T(8,128)(2,1)} custom-call(bf16[2048,256]{1,0:T(8,128)(2,1)S(1)} %get-tuple-element.39.q_ref, f32[8,4096]{1,0:T(8,128)S(1)} %get-tuple-element.55.own_ref, f32[8,4096]{1,0:T(8,128)S(1)} %collective-permute-done.6.one_ref, f32[8,4096]{1,0:T(8,128)S(1)} %collective-permute-done.7.two_ref, ...), custom_call_target="tpu_custom_call" | custom-call | flops 600000000 | bytes 9437184 | tf_op jit(solution)/shard_map/join_memory/pallas_call | solution.py:495
  (8 shorter events, 0.4 us)
Async XLA Ops:
  2.1 9.8 %all-to-all-start = ((f32[8,2,256]{2,1,0:T(2,128)}), f32[8,2,256]{2,1,0:T(2,128)S(1)}, u32[]{:S(2)}, u32[]{:S(2)}) async-start(f32[8,2,256]{2,1,0:T(2,128)} %gate_sums.1), calls=%async_computation | async-start | bytes 32768 | tf_op jit(solution)/shard_map/all_to_all | solution.py:513
  13.2 9.8 %collective-permute-start = (f32[8,4224]{1,0:T(8,128)S(1)}, f32[8,4224]{1,0:T(8,128)S(1)}, u32[]{:S(2)}, u32[]{:S(2)}) collective-permute-start(f32[8,4224]{1,0:T(8,128)S(1)} %get-tuple-element.41), channel_id=1, source_target_pairs={{0,8},{8,16},{16,24},{24,0},{1,9},{9,17},{17,25},{25,1},{2,10},{10... | collective-permute-start | bytes 405512 | tf_op jit(solution)/shard_map/ppermute | solution.py:519
  14.8 8.9 %collective-permute-start.1 = (f32[8,4224]{1,0:T(8,128)S(1)}, f32[8,4224]{1,0:T(8,128)S(1)}, u32[]{:S(2)}, u32[]{:S(2)}) collective-permute-start(f32[8,4224]{1,0:T(8,128)S(1)} %get-tuple-element.42), channel_id=1, source_target_pairs={{0,16},{8,24},{16,0},{24,8},{1,17},{9,25},{17,1},{25,9},{2,18},{10... | collective-permute-start | bytes 405512 | tf_op jit(solution)/shard_map/ppermute | solution.py:519
  17.5 6.2 %collective-permute-start.2 = (f32[8,4224]{1,0:T(8,128)S(1)}, f32[8,4224]{1,0:T(8,128)S(1)}, u32[]{:S(2)}, u32[]{:S(2)}) collective-permute-start(f32[8,4224]{1,0:T(8,128)S(1)} %get-tuple-element.43), channel_id=1, source_target_pairs={{0,24},{8,0},{16,8},{24,16},{1,25},{9,1},{17,9},{25,17},{2,26},{10... | collective-permute-start | bytes 405512 | tf_op jit(solution)/shard_map/ppermute | solution.py:519
  23.8 5.1 %collective-permute-start.3 = (f32[8,4224]{1,0:T(8,128)S(1)}, f32[8,4224]{1,0:T(8,128)S(1)}, u32[]{:S(2)}, u32[]{:S(2)}) collective-permute-start(f32[8,4224]{1,0:T(8,128)S(1)} %get-tuple-element.45.total_ref), channel_id=1, source_target_pairs={{0,32},{32,0},{64,96},{96,64},{128,160},{160,128},{192,224},{224,1... | collective-permute-start | bytes 405512 | tf_op jit(solution)/shard_map/ppermute | solution.py:524
  28.9 6.9 %collective-permute-start.4 = (f32[8,4224]{1,0:T(8,128)S(1)}, f32[8,4224]{1,0:T(8,128)S(1)}, u32[]{:S(2)}, u32[]{:S(2)}) collective-permute-start(f32[8,4224]{1,0:T(8,128)S(1)} %get-tuple-element.46.total_ref), channel_id=1, source_target_pairs={{0,64},{32,96},{64,0},{96,32},{128,192},{160,224},{192,128},{224,1... | collective-permute-start | bytes 405512 | tf_op jit(solution)/shard_map/ppermute | solution.py:524
  35.9 9.6 %collective-permute-start.5 = (f32[8,4224]{1,0:T(8,128)S(1)}, f32[8,4224]{1,0:T(8,128)S(1)}, u32[]{:S(2)}, u32[]{:S(2)}) collective-permute-start(f32[8,4224]{1,0:T(8,128)S(1)} %get-tuple-element.51.total_ref), channel_id=1, source_target_pairs={{0,192},{32,224},{64,160},{96,128},{128,96},{160,64},{192,0},{224,... | collective-permute-start | bytes 405512 | tf_op jit(solution)/shard_map/ppermute | solution.py:524
  45.6 7.2 %collective-permute-start.6 = (f32[8,4096]{1,0:T(8,128)S(1)}, f32[8,4096]{1,0:T(8,128)S(1)}, u32[]{:S(2)}, u32[]{:S(2)}) collective-permute-start(f32[8,4096]{1,0:T(8,128)S(1)} %get-tuple-element.56), channel_id=1, source_target_pairs={{0,8},{8,16},{16,24},{24,0},{1,9},{9,17},{17,25},{25,1},{2,10},{10... | collective-permute-start | bytes 393224 | tf_op jit(solution)/shard_map/ppermute | solution.py:519
  48.0 6.5 %collective-permute-start.7 = (f32[8,4096]{1,0:T(8,128)S(1)}, f32[8,4096]{1,0:T(8,128)S(1)}, u32[]{:S(2)}, u32[]{:S(2)}) collective-permute-start(f32[8,4096]{1,0:T(8,128)S(1)} %get-tuple-element.57), channel_id=1, source_target_pairs={{0,16},{8,24},{16,0},{24,8},{1,17},{9,25},{17,1},{25,9},{2,18},{10... | collective-permute-start | bytes 393224 | tf_op jit(solution)/shard_map/ppermute | solution.py:519
  49.4 5.0 %collective-permute-start.8 = (f32[8,4096]{1,0:T(8,128)S(1)}, f32[8,4096]{1,0:T(8,128)S(1)}, u32[]{:S(2)}, u32[]{:S(2)}) collective-permute-start(f32[8,4096]{1,0:T(8,128)S(1)} %get-tuple-element.58), channel_id=1, source_target_pairs={{0,24},{8,0},{16,8},{24,16},{1,25},{9,1},{17,9},{25,17},{2,26},{10... | collective-permute-start | bytes 393224 | tf_op jit(solution)/shard_map/ppermute | solution.py:519

commit v6 on v4

--- a/solution.py
+++ b/solution.py
@@ -533,7 +533,7 @@
     total, everything = grouped(moved, den_a)
     got = swapped(total, lambda i: i ^ 1)
     total, prefix = round_of(first_round_kernel, total, got, den_a)
-    got = swapped(total, lambda i: i ^ 2)
+    got = swapped(total, lambda i: i ^ 3)
     num_b, den_b = local(PARTS[1], None, prefix, *qkv, table)
     total, prefix = round_of(next_round_kernel, total, got, prefix, den_b)
     got = swapped(total, lambda i: (6, 7, 5, 4, 3, 2, 0, 1)[i])

time: 56.6 us -> 56.8 us (level)
  waiting for transfers between devices: 14.3 us -> 16.2 us
  starting transfers between devices: 25.3 us -> 23.7 us
    ppermute x3, starting transfers between devices: 9.67 us -> 8.14 us  [swapped(): return lax.ppermute(x, 'ctx_0', [(i, partner(i)) for i in range(ZS)])]
    ppermute x3, waiting for transfers between devices: 8.58 us -> 9.65 us  [swapped(): return lax.ppermute(x, 'ctx_0', [(i, partner(i)) for i in range(ZS)])]
    ppermute x6, waiting for transfers between devices: 2.29 us -> 3.17 us  [around(): lax.ppermute(parts[k], 'ctx_1', [(i, (i + k) % XS) for i in range(XS)])]
  transfers between devices with their start and end apart: 10 -> 10, of which waited for: 6 -> 7; matrix products, arithmetic and copies ran while one was open for 0% -> 0% of each run, Pallas kernels for 20% -> 20%
where the time goes in v6:
time: 56.8 us; the launch traced here: 56.5 us
  starting transfers between devices  23.7 us (42%)
  waiting for transfers between devices  16.2 us (29%)
  Pallas kernels  15.9 us (28%)
  between operations  0.72 us (1%)
    ppermute x6, starting transfers between devices, around(): lax.ppermute(parts[k], 'ctx_1', [(i, (i + k) % XS) for i in range(XS)])  11.1 us
    ppermute x3, waiting for transfers between devices, swapped(): return lax.ppermute(x, 'ctx_0', [(i, partner(i)) for i in range(ZS)])  9.65 us
    ppermute x3, starting transfers between devices, swapped(): return lax.ppermute(x, 'ctx_0', [(i, partner(i)) for i in range(ZS)])  8.14 us
    pallas_call x3, Pallas kernels, local(): pl.pallas_call(functools.partial(first_kernel if first else local_kernel,...  7.35 us
    all_to_all x1, starting transfers between devices, exchanged(): return lax.all_to_all(x, axis, split_axis=0, concat_axis=0, tiled=True)  4.48 us
    all_to_all x1, waiting for transfers between devices, exchanged(): return lax.all_to_all(x, axis, split_axis=0, concat_axis=0, tiled=True)  3.38 us
    ppermute x6, waiting for transfers between devices, around(): lax.ppermute(parts[k], 'ctx_1', [(i, (i + k) % XS) for i in range(XS)])  3.17 us
    pallas_call x1, Pallas kernels, turned(): pl.pallas_call(turned_kernel, in_specs=[HBM] * 2, out_specs=[VMEM] * 2, o...  1.97 us
  transfers between devices with their start and end apart: 10, of which 7 were waited for; matrix products, arithmetic and copies ran while one was open for 0% of the time, Pallas kernels for 20%

profile of v6, /device:TPU:32, one launch (start us, length us, event | category | flops | bytes accessed | tf_op | source)
XLA Modules:
  0.0 56.5 jit_solution(933383001175646662)
XLA Ops:
  0.6 1.5 %gate_sums.1 = f32[8,2,256]{2,1,0:T(2,128)} custom-call(f32[2,8,256]{2,1,0:T(8,128)} %g_hbm.1), custom_call_target="tpu_custom_call" | custom-call | tf_op jit(solution)/shard_map/gate_sums/pallas_call | solution.py:85
  2.1 4.5 %all-to-all-start = ((f32[8,2,256]{2,1,0:T(2,128)}), f32[8,2,256]{2,1,0:T(2,128)S(1)}, u32[]{:S(2)}, u32[]{:S(2)}) async-start(f32[8,2,256]{2,1,0:T(2,128)} %gate_sums.1), calls=%async_computation | async-start | bytes 32768 | tf_op jit(solution)/shard_map/all_to_all | solution.py:512
  6.6 2.0 %turn_keys.1 = (bf16[256,2048]{1,0:T(8,128)(2,1)S(1)}, bf16[2048,512]{1,0:T(8,128)(2,1)S(1)}) custom-call(bf16[2048,256]{1,0:T(8,128)(2,1)} %k_hbm.3, bf16[2048,512]{1,0:T(8,128)(2,1)} %v_hbm.1), custom_call_target="tpu_custom_call" | custom-call | bytes 4194304 | tf_op jit(solution)/shard_map/turn_keys/pallas_call | solution.py:112
  8.6 3.4 %all-to-all-done.g_ref = f32[8,2,256]{2,1,0:T(2,128)S(1)} async-done(((f32[8,2,256]{2,1,0:T(2,128)}), f32[8,2,256]{2,1,0:T(2,128)S(1)}, u32[]{:S(2)}, u32[]{:S(2)}) %all-to-all-start) | async-done | bytes 16416 | tf_op jit(solution)/shard_map/all_to_all | solution.py:512
  12.0 1.2 %shard_state.1 = (f32[8,4224]{1,0:T(8,128)S(1)}, f32[8,4224]{1,0:T(8,128)S(1)}, f32[8,4224]{1,0:T(8,128)S(1)}, f32[8,4224]{1,0:T(8,128)S(1)}, f32[8,128]{1,0:T(8,128)S(1)}) custom-call(f32[8,2,256]{2,1,0:T(2,128)S(1)} %all-to-all-done.g_ref, bf16[256,2048]{1,0:T(8,128)(2,1)S(1)} %get-tuple-element.36.kt_ref, bf16[2048,512]{1,0:T(8,128)(2,1)S(1)} %get-tuple-element.37.v_ref), custom_call_target="tpu_custom_call" | custom-call | flops 600000000 | bytes 5242880 | tf_op jit(solution)/shard_map/shard_state/pallas_call | solution.py:165
  13.2 1.6 %collective-permute-start = (f32[8,4224]{1,0:T(8,128)S(1)}, f32[8,4224]{1,0:T(8,128)S(1)}, u32[]{:S(2)}, u32[]{:S(2)}) collective-permute-start(f32[8,4224]{1,0:T(8,128)S(1)} %get-tuple-element.41), channel_id=1, source_target_pairs={{0,8},{8,16},{16,24},{24,0},{1,9},{9,17},{17,25},{25,1},{2,10},{10... | collective-permute-start | bytes 405512 | tf_op jit(solution)/shard_map/ppermute | solution.py:518
  14.8 2.7 %collective-permute-start.1 = (f32[8,4224]{1,0:T(8,128)S(1)}, f32[8,4224]{1,0:T(8,128)S(1)}, u32[]{:S(2)}, u32[]{:S(2)}) collective-permute-start(f32[8,4224]{1,0:T(8,128)S(1)} %get-tuple-element.42), channel_id=1, source_target_pairs={{0,16},{8,24},{16,0},{24,8},{1,17},{9,25},{17,1},{25,9},{2,18},{10... | collective-permute-start | bytes 405512 | tf_op jit(solution)/shard_map/ppermute | solution.py:518
  17.5 1.4 %collective-permute-start.2 = (f32[8,4224]{1,0:T(8,128)S(1)}, f32[8,4224]{1,0:T(8,128)S(1)}, u32[]{:S(2)}, u32[]{:S(2)}) collective-permute-start(f32[8,4224]{1,0:T(8,128)S(1)} %get-tuple-element.43), channel_id=1, source_target_pairs={{0,24},{8,0},{16,8},{24,16},{1,25},{9,1},{17,9},{25,17},{2,26},{10... | collective-permute-start | bytes 405512 | tf_op jit(solution)/shard_map/ppermute | solution.py:518
  18.9 4.0 %within_shard.3 = (f32[512,512]{1,0:T(8,128)S(1)}, f32[512,128]{1,0:T(8,128)S(1)}, f32[12,512]{1,0:T(8,128)S(1)}, bf16[2048,256]{1,0:T(8,128)(2,1)S(1)}, bf16[2048,256]{1,0:T(8,128)(2,1)S(1)}) custom-call(f32[8,2,256]{2,1,0:T(2,128)S(1)} %all-to-all-done.g_ref, f32[8,128]{1,0:T(8,128)S(1)} %get-tuple-element.38.tick_ref, bf16[2048,256]{1,0:T(8,128)(2,1)} %q_hbm.1, ...), custom_call_target="tpu_custom_call" | custom-call | flops 3200000000 | bytes 4194304 | tf_op jit(solution)/shard_map/within_shard/pallas_call | solution.py:417
  23.0 0.7 %collective-permute-done.1.two_ref = f32[8,4224]{1,0:T(8,128)S(1)} collective-permute-done((f32[8,4224]{1,0:T(8,128)S(1)}, f32[8,4224]{1,0:T(8,128)S(1)}, u32[]{:S(2)}, u32[]{:S(2)}) %collective-permute-start.1) | collective-permute-done | bytes 135200 | tf_op jit(solution)/shard_map/ppermute | solution.py:518
  24.0 4.8 %collective-permute-done.3.got_ref = f32[8,4224]{1,0:T(8,128)S(1)} collective-permute-done((f32[8,4224]{1,0:T(8,128)S(1)}, f32[8,4224]{1,0:T(8,128)S(1)}, u32[]{:S(2)}, u32[]{:S(2)}) %collective-permute-start.3) | collective-permute-done | bytes 135200 | tf_op jit(solution)/shard_map/ppermute | solution.py:523
  28.9 2.0 %collective-permute-start.4 = (f32[8,4224]{1,0:T(8,128)S(1)}, f32[8,4224]{1,0:T(8,128)S(1)}, u32[]{:S(2)}, u32[]{:S(2)}) collective-permute-start(f32[8,4224]{1,0:T(8,128)S(1)} %get-tuple-element.46.total_ref), channel_id=1, source_target_pairs={{0,96},{32,64},{64,32},{96,0},{128,224},{160,192},{192,160},{224,1... | collective-permute-start | bytes 405512 | tf_op jit(solution)/shard_map/ppermute | solution.py:523
  30.9 1.4 %within_shard.4 = (f32[1024,512]{1,0:T(8,128)S(1)}, f32[1024,128]{1,0:T(8,128)S(1)}) custom-call(f32[12,512]{1,0:T(8,128)S(1)} %get-tuple-element.48.table_ref, f32[8,4224]{1,0:T(8,128)S(1)} %get-tuple-element.47.tick_ref.prefix_ref, bf16[2048,256]{1,0:T(8,128)(2,1)S(1)} %get-tuple-element.39.q_ref, bf16[2048,256]{1,0:T(8,128)(2,1)S(1)} %get-tuple-element.49.k_ref, ...), custom_call_target="tpu_custom_call" | custom-call | flops 2400000000 | bytes 3145728 | tf_op jit(solution)/shard_map/within_shard/pallas_call | solution.py:417
  32.4 3.2 %collective-permute-done.4.got_ref = f32[8,4224]{1,0:T(8,128)S(1)} collective-permute-done((f32[8,4224]{1,0:T(8,128)S(1)}, f32[8,4224]{1,0:T(8,128)S(1)}, u32[]{:S(2)}, u32[]{:S(2)}) %collective-permute-start.4) | collective-permute-done | bytes 135200 | tf_op jit(solution)/shard_map/ppermute | solution.py:523
  35.6 5.9 %collective-permute-start.5 = (f32[8,4224]{1,0:T(8,128)S(1)}, f32[8,4224]{1,0:T(8,128)S(1)}, u32[]{:S(2)}, u32[]{:S(2)}) collective-permute-start(f32[8,4224]{1,0:T(8,128)S(1)} %get-tuple-element.51.total_ref), channel_id=1, source_target_pairs={{0,192},{32,224},{64,160},{96,128},{128,96},{160,64},{192,0},{224,... | collective-permute-start | bytes 405512 | tf_op jit(solution)/shard_map/ppermute | solution.py:523
  41.5 1.9 %within_shard.5 = (f32[512,512]{1,0:T(8,128)S(1)}, f32[512,128]{1,0:T(8,128)S(1)}) custom-call(f32[12,512]{1,0:T(8,128)S(1)} %get-tuple-element.48.table_ref, f32[8,4224]{1,0:T(8,128)S(1)} %get-tuple-element.52.tick_ref.prefix_ref, bf16[2048,256]{1,0:T(8,128)(2,1)S(1)} %get-tuple-element.39.q_ref, bf16[2048,256]{1,0:T(8,128)(2,1)S(1)} %get-tuple-element.49.k_ref, ...), custom_call_target="tpu_custom_call" | custom-call | flops 2400000000 | bytes 3145728 | tf_op jit(solution)/shard_map/within_shard/pallas_call | solution.py:417
  43.3 1.7 %collective-permute-done.5.got_ref = f32[8,4224]{1,0:T(8,128)S(1)} collective-permute-done((f32[8,4224]{1,0:T(8,128)S(1)}, f32[8,4224]{1,0:T(8,128)S(1)}, u32[]{:S(2)}, u32[]{:S(2)}) %collective-permute-start.5) | collective-permute-done | bytes 135200 | tf_op jit(solution)/shard_map/ppermute | solution.py:523
  45.2 2.3 %collective-permute-start.6 = (f32[8,8,512]{2,1,0:T(8,128)S(1)}, f32[8,8,512]{2,1,0:T(8,128)S(1)}, u32[]{:S(2)}, u32[]{:S(2)}) collective-permute-start(f32[8,8,512]{2,1,0:T(8,128)S(1)} %get-tuple-element.56), channel_id=1, source_target_pairs={{0,8},{8,16},{16,24},{24,0},{1,9},{9,17},{17,25},{25,1},{2,10},{10... | collective-permute-start | bytes 393224 | tf_op jit(solution)/shard_map/ppermute | solution.py:518
  47.5 2.4 %collective-permute-start.7 = (f32[8,8,512]{2,1,0:T(8,128)S(1)}, f32[8,8,512]{2,1,0:T(8,128)S(1)}, u32[]{:S(2)}, u32[]{:S(2)}) collective-permute-start(f32[8,8,512]{2,1,0:T(8,128)S(1)} %get-tuple-element.57), channel_id=1, source_target_pairs={{0,16},{8,24},{16,0},{24,8},{1,17},{9,25},{17,1},{25,9},{2,18},{10... | collective-permute-start | bytes 393224 | tf_op jit(solution)/shard_map/ppermute | solution.py:518
  49.9 0.7 %collective-permute-start.8 = (f32[8,8,512]{2,1,0:T(8,128)S(1)}, f32[8,8,512]{2,1,0:T(8,128)S(1)}, u32[]{:S(2)}, u32[]{:S(2)}) collective-permute-start(f32[8,8,512]{2,1,0:T(8,128)S(1)} %get-tuple-element.58), channel_id=1, source_target_pairs={{0,24},{8,0},{16,8},{24,16},{1,25},{9,1},{17,9},{25,17},{2,26},{10... | collective-permute-start | bytes 393224 | tf_op jit(solution)/shard_map/ppermute | solution.py:518
  50.5 1.8 %row_scales.1 = (f32[2048,128]{1,0:T(8,128)S(1)}, f32[2048,128]{1,0:T(8,128)S(1)}, f32[1,8,512]{2,1,0:T(8,128)}, f32[1,256]{1,0:T(1,128)}, f32[1,128]{1,0:T(1,128)}) custom-call(f32[12,512]{1,0:T(8,128)S(1)} %get-tuple-element.48.table_ref, f32[8,128]{1,0:T(8,128)S(1)} %get-tuple-element.59.mine_ref, bf16[2048,256]{1,0:T(8,128)(2,1)S(1)} %get-tuple-element.39.q_ref, ...), custom_call_target="tpu_custom_call" | custom-call | flops 600000000 | bytes 4194304 | tf_op jit(solution)/shard_map/row_scales/pallas_call | solution.py:456
  52.3 1.9 %collective-permute-done.7.two_ref = f32[8,8,512]{2,1,0:T(8,128)S(1)} collective-permute-done((f32[8,8,512]{2,1,0:T(8,128)S(1)}, f32[8,8,512]{2,1,0:T(8,128)S(1)}, u32[]{:S(2)}, u32[]{:S(2)}) %collective-permute-start.7) | collective-permute-done | bytes 131104 | tf_op jit(solution)/shard_map/ppermute | solution.py:518
  54.2 0.6 %collective-permute-done.8.three_ref = f32[8,8,512]{2,1,0:T(8,128)S(1)} collective-permute-done((f32[8,8,512]{2,1,0:T(8,128)S(1)}, f32[8,8,512]{2,1,0:T(8,128)S(1)}, u32[]{:S(2)}, u32[]{:S(2)}) %collective-permute-start.8) | collective-permute-done | bytes 131104 | tf_op jit(solution)/shard_map/ppermute | solution.py:518
  54.8 1.7 %join_memory.1 = bf16[2048,512]{1,0:T(8,128)(2,1)} custom-call(bf16[2048,256]{1,0:T(8,128)(2,1)S(1)} %get-tuple-element.39.q_ref, f32[8,8,512]{2,1,0:T(8,128)S(1)} %get-tuple-element.55.own_ref, f32[8,8,512]{2,1,0:T(8,128)S(1)} %collective-permute-done.6.one_ref, f32[8,8,512]{2,1,0:T(8,128)S(1)} %collective-permute-done.7.two_ref, ...), custom_call_target="tpu_custom_call" | custom-call | flops 600000000 | bytes 9437184 | tf_op jit(solution)/shard_map/join_memory/pallas_call | solution.py:494
  (8 shorter events, 0.6 us)
Async XLA Ops:
  2.1 9.8 %all-to-all-start = ((f32[8,2,256]{2,1,0:T(2,128)}), f32[8,2,256]{2,1,0:T(2,128)S(1)}, u32[]{:S(2)}, u32[]{:S(2)}) async-start(f32[8,2,256]{2,1,0:T(2,128)} %gate_sums.1), calls=%async_computation | async-start | bytes 32768 | tf_op jit(solution)/shard_map/all_to_all | solution.py:512
  13.2 9.8 %collective-permute-start = (f32[8,4224]{1,0:T(8,128)S(1)}, f32[8,4224]{1,0:T(8,128)S(1)}, u32[]{:S(2)}, u32[]{:S(2)}) collective-permute-start(f32[8,4224]{1,0:T(8,128)S(1)} %get-tuple-element.41), channel_id=1, source_target_pairs={{0,8},{8,16},{16,24},{24,0},{1,9},{9,17},{17,25},{25,1},{2,10},{10... | collective-permute-start | bytes 405512 | tf_op jit(solution)/shard_map/ppermute | solution.py:518
  14.8 8.9 %collective-permute-start.1 = (f32[8,4224]{1,0:T(8,128)S(1)}, f32[8,4224]{1,0:T(8,128)S(1)}, u32[]{:S(2)}, u32[]{:S(2)}) collective-permute-start(f32[8,4224]{1,0:T(8,128)S(1)} %get-tuple-element.42), channel_id=1, source_target_pairs={{0,16},{8,24},{16,0},{24,8},{1,17},{9,25},{17,1},{25,9},{2,18},{10... | collective-permute-start | bytes 405512 | tf_op jit(solution)/shard_map/ppermute | solution.py:518
  17.5 6.2 %collective-permute-start.2 = (f32[8,4224]{1,0:T(8,128)S(1)}, f32[8,4224]{1,0:T(8,128)S(1)}, u32[]{:S(2)}, u32[]{:S(2)}) collective-permute-start(f32[8,4224]{1,0:T(8,128)S(1)} %get-tuple-element.43), channel_id=1, source_target_pairs={{0,24},{8,0},{16,8},{24,16},{1,25},{9,1},{17,9},{25,17},{2,26},{10... | collective-permute-start | bytes 405512 | tf_op jit(solution)/shard_map/ppermute | solution.py:518
  23.8 5.1 %collective-permute-start.3 = (f32[8,4224]{1,0:T(8,128)S(1)}, f32[8,4224]{1,0:T(8,128)S(1)}, u32[]{:S(2)}, u32[]{:S(2)}) collective-permute-start(f32[8,4224]{1,0:T(8,128)S(1)} %get-tuple-element.45.total_ref), channel_id=1, source_target_pairs={{0,32},{32,0},{64,96},{96,64},{128,160},{160,128},{192,224},{224,1... | collective-permute-start | bytes 405512 | tf_op jit(solution)/shard_map/ppermute | solution.py:523
  28.9 6.6 %collective-permute-start.4 = (f32[8,4224]{1,0:T(8,128)S(1)}, f32[8,4224]{1,0:T(8,128)S(1)}, u32[]{:S(2)}, u32[]{:S(2)}) collective-permute-start(f32[8,4224]{1,0:T(8,128)S(1)} %get-tuple-element.46.total_ref), channel_id=1, source_target_pairs={{0,96},{32,64},{64,32},{96,0},{128,224},{160,192},{192,160},{224,1... | collective-permute-start | bytes 405512 | tf_op jit(solution)/shard_map/ppermute | solution.py:523
  35.6 9.4 %collective-permute-start.5 = (f32[8,4224]{1,0:T(8,128)S(1)}, f32[8,4224]{1,0:T(8,128)S(1)}, u32[]{:S(2)}, u32[]{:S(2)}) collective-permute-start(f32[8,4224]{1,0:T(8,128)S(1)} %get-tuple-element.51.total_ref), channel_id=1, source_target_pairs={{0,192},{32,224},{64,160},{96,128},{128,96},{160,64},{192,0},{224,... | collective-permute-start | bytes 405512 | tf_op jit(solution)/shard_map/ppermute | solution.py:523
  45.2 7.2 %collective-permute-start.6 = (f32[8,8,512]{2,1,0:T(8,128)S(1)}, f32[8,8,512]{2,1,0:T(8,128)S(1)}, u32[]{:S(2)}, u32[]{:S(2)}) collective-permute-start(f32[8,8,512]{2,1,0:T(8,128)S(1)} %get-tuple-element.56), channel_id=1, source_target_pairs={{0,8},{8,16},{16,24},{24,0},{1,9},{9,17},{17,25},{25,1},{2,10},{10... | collective-permute-start | bytes 393224 | tf_op jit(solution)/shard_map/ppermute | solution.py:518
  47.5 6.7 %collective-permute-start.7 = (f32[8,8,512]{2,1,0:T(8,128)S(1)}, f32[8,8,512]{2,1,0:T(8,128)S(1)}, u32[]{:S(2)}, u32[]{:S(2)}) collective-permute-start(f32[8,8,512]{2,1,0:T(8,128)S(1)} %get-tuple-element.57), channel_id=1, source_target_pairs={{0,16},{8,24},{16,0},{24,8},{1,17},{9,25},{17,1},{25,9},{2,18},{10... | collective-permute-start | bytes 393224 | tf_op jit(solution)/shard_map/ppermute | solution.py:518
  49.9 5.0 %collective-permute-start.8 = (f32[8,8,512]{2,1,0:T(8,128)S(1)}, f32[8,8,512]{2,1,0:T(8,128)S(1)}, u32[]{:S(2)}, u32[]{:S(2)}) collective-permute-start(f32[8,8,512]{2,1,0:T(8,128)S(1)} %get-tuple-element.58), channel_id=1, source_target_pairs={{0,24},{8,0},{16,8},{24,16},{1,25},{9,1},{17,9},{25,17},{2,26},{10... | collective-permute-start | bytes 393224 | tf_op jit(solution)/shard_map/ppermute | solution.py:518
